TPU v7x, 32 devices: a whole 2x2x4 slice. The times are simulated.
32 devices in a mesh: dp: 16 (over z, y, core), mp: 2 (over x).
Axes of the slice: x: 2, y: 2, z: 4, core: 2. Of those that a mesh axis runs over, the one named last changes fastest.
Arguments:
- tokens_in: bfloat16 [4096, 2048], P(('dp', 'mp')), may hold values from -6 to 6
- teacher: bfloat16 [4096, 2048], P(('dp', 'mp')), may hold values from -6 to 6
- valid_mask: int32 [16, 256], P('dp', 'mp'), may hold values from 0 to 1, as said below
- group_of: int32 [16], replicated, may hold values from 0 to 1, as said below
- prompt_len: int32 [2], replicated, may hold values from 128 to 256
- ln1_gain: bfloat16 [2048], P('dp'), may hold values from 0.5 to 1.5
- ln1_bias: bfloat16 [2048], P('dp'), may hold values from -2 to 2
- w_query: bfloat16 [2048, 2048], P('dp', 'mp'), may hold values from -0.125 to 0.125
- w_key: bfloat16 [2048, 2048], P('dp', 'mp'), may hold values from -0.125 to 0.125
- w_value: bfloat16 [2048, 4096], P('dp', 'mp'), may hold values from -0.125 to 0.125
- w_gate: bfloat16 [2048, 4096], P('dp', 'mp'), may hold values from -0.125 to 0.125
- w_out: bfloat16 [2048, 4096], P('dp', 'mp'), may hold values from -0.1875 to 0.1875
- ln2_gain: bfloat16 [2048], P('dp'), may hold values from 0.5 to 1.5
- ln2_bias: bfloat16 [2048], P('dp'), may hold values from -2 to 2
- w_up: bfloat16 [2048, 4096], P('dp', 'mp'), may hold values from -0.125 to 0.125
- w_down: bfloat16 [2048, 4096], P('dp', 'mp'), may hold values from -0.125 to 0.125
Outputs:
- block_out: float32 [4096, 2048], P(('dp', 'mp'))
- grad_tokens: float32 [4096, 2048], P(('dp', 'mp'))
- loss: float32 [], replicated
- grad_ln1_gain: float32 [2048], P('dp')
- grad_ln1_bias: float32 [2048], P('dp')
- grad_w_query: float32 [2048, 2048], P('dp', 'mp')
- grad_w_key: float32 [2048, 2048], P('dp', 'mp')
- grad_w_value: float32 [2048, 4096], P('dp', 'mp')
- grad_w_gate: float32 [2048, 4096], P('dp', 'mp')
- grad_w_out: float32 [2048, 4096], P('dp', 'mp')
- grad_ln2_gain: float32 [2048], P('dp')
- grad_ln2_bias: float32 [2048], P('dp')
- grad_w_up: float32 [2048, 4096], P('dp', 'mp')
- grad_w_down: float32 [2048, 4096], P('dp', 'mp')
Inputs may be any that keep to these rules, and one draw needn't show every extreme that they name: `valid_mask`: in each row the ones form a leading run of one or more positions, zeros follow. `group_of`: each group number is held by exactly 8 segments; a group's prompt is its lowest-numbered segment, the others are its continuations.
All inputs are finite; a program needn't handle non-finite values.
Results may differ from a plain program's by a relative error of at most 0.013.
Values may be sent and summed in bfloat16 or wider, within the bound.
A program may use at most 192 MiB of HBM per device.

v0:
```python
import math

import jax
import jax.numpy as jnp
from jax import lax
from jax.sharding import PartitionSpec as P

DK = 256
DV = 512


EPSILON = 1e-05
GROUP_EPSILON = 0.05


def norm_stats(values, floor_eps):
    center = jnp.mean(values, axis=-1, keepdims=True)
    shifted = values - center
    inv_std = lax.rsqrt(jnp.mean(shifted * shifted, axis=-1, keepdims=True) + floor_eps)
    return (shifted * inv_std, inv_std)


def norm_back(grad_in, normed, inv_std):
    mean_grad = jnp.mean(grad_in, axis=-1, keepdims=True)
    mean_proj = jnp.mean(grad_in * normed, axis=-1, keepdims=True)
    return (grad_in - mean_grad - normed * mean_proj) * inv_std


def xpos_tables(positions, direction):
    half_dim = DK // 2
    pair_index = jnp.arange(half_dim, dtype=jnp.float32)
    frequency = jnp.exp(-(2.0 * pair_index / DK) * math.log(10000.0))
    base_ratio = (2.0 * pair_index / DK + 0.4) / 1.4
    angles = positions[:, None] * frequency[None, :]
    factor = jnp.exp(direction * (positions[:, None] / 512.0) * jnp.log(base_ratio)[None, :])
    return (jnp.cos(angles), jnp.sin(angles), factor)


def rotate_pairs(values, cosine, sine_tab, factor):
    half_dim = values.shape[-1] // 2
    first_half = values[..., :half_dim]
    second = values[..., half_dim:]
    cosine = cosine[:, None, :]
    sine_tab = sine_tab[:, None, :]
    factor = factor[:, None, :]
    return jnp.concatenate(
        [
            (first_half * cosine - second * sine_tab) * factor,
            (second * cosine + first_half * sine_tab) * factor,
        ],
        axis=-1,
    )


def rotate_back(grad_rot, cosine, sine_tab, factor):
    half_dim = grad_rot.shape[-1] // 2
    first_half = grad_rot[..., :half_dim]
    second = grad_rot[..., half_dim:]
    cosine = cosine[:, None, :]
    sine_tab = sine_tab[:, None, :]
    factor = factor[:, None, :]
    return jnp.concatenate(
        [
            (first_half * cosine + second * sine_tab) * factor,
            (second * cosine - first_half * sine_tab) * factor,
        ],
        axis=-1,
    )


def plain_dot(first_op, second_op):
    return jnp.dot(first_op, second_op, preferred_element_type=jnp.float32)


def contract_last(first_op, second_op):
    return lax.dot_general(
        first_op, second_op, (((1,), (1,)), ((), ())), preferred_element_type=jnp.float32
    )


def contract_first(first_op, second_op):
    return lax.dot_general(
        first_op, second_op, (((0,), (0,)), ((), ())), preferred_element_type=jnp.float32
    )


def gather_rows(rows_low):
    return lax.all_gather(rows_low, "mp", axis=0, tiled=True)


def scatter_rows(terms):
    return lax.psum_scatter(terms, "mp", scatter_dimension=0, tiled=True)


def on_device(
    tokens_in,
    teacher,
    valid_mask,
    group_of,
    prompt_len,
    ln1_gain,
    ln1_bias,
    w_query,
    w_key,
    w_value,
    w_gate,
    w_out,
    ln2_gain,
    ln2_bias,
    w_up,
    w_down,
):
    half_rows = tokens_in.shape[0]
    model_dim = tokens_in.shape[1]
    seg_len = half_rows * lax.axis_size("mp")
    seg_count = group_of.shape[0]
    group_count = prompt_len.shape[0]
    heads_local = w_query.shape[1] // DK
    token_total = seg_len * seg_count
    dp_index = lax.axis_index("dp")
    mp_index = lax.axis_index("mp")
    attn_full = (
        lax.all_gather(ln1_gain, "dp", axis=0, tiled=True),
        lax.all_gather(ln1_bias, "dp", axis=0, tiled=True),
        lax.all_gather(w_query, "dp", axis=0, tiled=True),
        lax.all_gather(w_key, "dp", axis=0, tiled=True),
        lax.all_gather(w_value, "dp", axis=0, tiled=True),
        lax.all_gather(w_gate, "dp", axis=0, tiled=True),
        lax.all_gather(w_out, "dp", axis=0, tiled=True),
    )
    ffn_full = (
        lax.all_gather(ln2_gain, "dp", axis=0, tiled=True),
        lax.all_gather(ln2_bias, "dp", axis=0, tiled=True),
        lax.all_gather(w_up, "dp", axis=0, tiled=True),
        lax.all_gather(w_down, "dp", axis=0, tiled=True),
    )
    gain_one = attn_full[0].astype(jnp.float32)
    bias_one = attn_full[1].astype(jnp.float32)
    wq_full, wk_full, wv_full, wg_full, wo_full = (
        attn_full[2],
        attn_full[3],
        attn_full[4],
        attn_full[5],
        attn_full[6],
    )
    gain_two = ffn_full[0].astype(jnp.float32)
    bias_two = ffn_full[1].astype(jnp.float32)
    wu_full, wd_full = (ffn_full[2], ffn_full[3])
    segment_ids = jnp.arange(seg_count, dtype=jnp.int32)
    my_group = jnp.sum(jnp.where(segment_ids == dp_index, group_of, 0))
    first_member = jnp.min(jnp.where(group_of == my_group, segment_ids, seg_count))
    prompt_flag = (first_member == dp_index).astype(jnp.float32)
    group_match = jnp.arange(group_count, dtype=jnp.int32) == my_group
    group_onehot = group_match.astype(jnp.float32)
    prompt_size = jnp.sum(jnp.where(group_match, prompt_len, 0))
    token_ids = jnp.arange(seg_len, dtype=jnp.int32)
    offset = jnp.where(prompt_flag > 0, 0, prompt_size)
    positions = (token_ids + offset).astype(jnp.float32)
    head_ids = (mp_index * heads_local + jnp.arange(heads_local, dtype=jnp.int32)).astype(
        jnp.float32
    )
    log_decay = jnp.log(1.0 - 2.0 ** (-5.0 - head_ids))
    before_end = token_ids < prompt_size
    state_age = (prompt_size - 1 - token_ids).astype(jnp.float32)
    state_weighting = jnp.where(
        (before_end & (prompt_flag > 0))[:, None],
        jnp.exp(log_decay[None, :] * jnp.maximum(state_age, 0.0)[:, None]),
        0.0,
    )
    continuation_factor = (1.0 - prompt_flag) * jnp.exp(
        log_decay[None, :] * (token_ids.astype(jnp.float32) + 1.0)[:, None]
    )
    float_ids = token_ids.astype(jnp.float32)
    distance = float_ids[:, None] - float_ids[None, :]
    decay_mat = jnp.where(
        distance[None] >= 0.0,
        jnp.exp(log_decay[:, None, None] * jnp.maximum(distance, 0.0)[None]),
        0.0,
    )
    own_ids = mp_index * half_rows + jnp.arange(half_rows, dtype=jnp.int32)
    loss_mask = valid_mask[0].astype(jnp.float32) * jnp.where(
        prompt_flag > 0, own_ids < prompt_size, True
    ).astype(jnp.float32)
    token_rows = tokens_in.astype(jnp.float32)
    normed_one, inv_one = norm_stats(token_rows, EPSILON)
    a_all = gather_rows((normed_one * gain_one + bias_one).astype(jnp.bfloat16))
    queries = plain_dot(a_all, wq_full).reshape(seg_len, heads_local, DK)
    keys_raw = plain_dot(a_all, wk_full).reshape(seg_len, heads_local, DK)
    reduced_values = (
        plain_dot(a_all, wv_full).astype(jnp.bfloat16).reshape(seg_len, heads_local, DV)
    )
    gate_pre = plain_dot(a_all, wg_full)
    cosine, sine_tab, grow_fac = xpos_tables(positions, 1.0)
    _, _, shrink = xpos_tables(positions, -1.0)
    q_scale = DK ** (-0.5)
    rotated_queries = (rotate_pairs(queries, cosine, sine_tab, grow_fac) * q_scale).astype(
        jnp.bfloat16
    )
    rotated_keys = rotate_pairs(keys_raw, cosine, sine_tab, shrink).astype(jnp.bfloat16)
    local_state = jnp.einsum(
        "jld,jla->lda",
        rotated_keys.astype(jnp.float32) * state_weighting[:, :, None],
        reduced_values.astype(jnp.float32),
        precision=lax.Precision.HIGHEST,
    )
    slots = group_onehot[:, None, None, None] * (prompt_flag * local_state)[None]
    summed = lax.psum(slots, "dp")
    state_lookup = jnp.sum(summed * group_onehot[:, None, None, None], axis=0).astype(jnp.bfloat16)
    scores = jnp.einsum(
        "thk,nhk->htn", rotated_queries, rotated_keys, preferred_element_type=jnp.float32
    )
    weights_low = (scores * decay_mat).astype(jnp.bfloat16)
    retained_output = jnp.einsum(
        "htn,nhv->thv", weights_low, reduced_values, preferred_element_type=jnp.float32
    )
    carried_forward = jnp.einsum(
        "ozi,ziw->ozw", rotated_queries, state_lookup, preferred_element_type=jnp.float32
    )
    retained_output = retained_output + continuation_factor[:, :, None] * carried_forward
    grouped, inv_group = norm_stats(retained_output, GROUP_EPSILON)
    gate_act = jax.nn.silu(gate_pre).reshape(seg_len, heads_local, DV)
    gated_out = (gate_act * grouped).reshape(seg_len, heads_local * DV).astype(jnp.bfloat16)
    attn_own = scatter_rows(contract_last(gated_out, wo_full))
    hidden_res = token_rows + attn_own
    normed_two, inv_two = norm_stats(hidden_res, EPSILON)
    c_all = gather_rows((normed_two * gain_two + bias_two).astype(jnp.bfloat16))
    up_pre = plain_dot(c_all, wu_full)
    up_act = jax.nn.gelu(up_pre, approximate=False).astype(jnp.bfloat16)
    ffn_own = scatter_rows(contract_last(up_act, wd_full))
    block_out = hidden_res + ffn_own
    error_rows = block_out - teacher.astype(jnp.float32)
    weighted = loss_mask[:, None] * error_rows
    valid_count, squared = lax.psum(
        (jnp.sum(loss_mask), jnp.sum(weighted * error_rows)), ("dp", "mp")
    )
    grad_out = token_total / valid_count * weighted
    loss_value = squared / (valid_count * model_dim)
    grad_ffn_all = gather_rows(grad_out.astype(jnp.bfloat16))
    grad_up_act = plain_dot(grad_ffn_all, wd_full)
    _, gelu_pull = jax.vjp(lambda inner: jax.nn.gelu(inner, approximate=False), up_pre)
    grad_up = gelu_pull(grad_up_act)[0].astype(jnp.bfloat16)
    grad_wd = contract_first(grad_ffn_all, up_act)
    grad_wu = contract_first(c_all, grad_up)
    grad_c = scatter_rows(contract_last(grad_up, wu_full))
    grad_gain2_part = jnp.sum(grad_c * normed_two, axis=0)
    grad_bias2_part = jnp.sum(grad_c, axis=0)
    grad_hidden = grad_out + norm_back(grad_c * gain_two, normed_two, inv_two)
    ffn_reduced = (
        lax.psum_scatter(grad_gain2_part, "dp", scatter_dimension=0, tiled=True),
        lax.psum_scatter(grad_bias2_part, "dp", scatter_dimension=0, tiled=True),
        lax.psum_scatter(grad_wu, "dp", scatter_dimension=0, tiled=True),
        lax.psum_scatter(grad_wd, "dp", scatter_dimension=0, tiled=True),
    )
    grad_attn_all = gather_rows(grad_hidden.astype(jnp.bfloat16))
    grad_gated = plain_dot(grad_attn_all, wo_full).reshape(seg_len, heads_local, DV)
    grad_wo = contract_first(grad_attn_all, gated_out)
    _, silu_pull = jax.vjp(jax.nn.silu, gate_pre)
    grad_gate = silu_pull((grad_gated * grouped).reshape(seg_len, heads_local * DV))[0].astype(
        jnp.bfloat16
    )
    retained_gradient = norm_back(grad_gated * gate_act, grouped, inv_group).astype(jnp.bfloat16)
    grad_weights = jnp.einsum(
        "thv,nhv->htn", retained_gradient, reduced_values, preferred_element_type=jnp.float32
    )
    grad_values = jnp.einsum(
        "htn,thv->nhv", weights_low, retained_gradient, preferred_element_type=jnp.float32
    )
    grad_scores = (grad_weights * decay_mat).astype(jnp.bfloat16)
    grad_q_rot = jnp.einsum(
        "htn,nhk->thk", grad_scores, rotated_keys, preferred_element_type=jnp.float32
    )
    grad_q_rot = grad_q_rot + continuation_factor[:, :, None] * jnp.einsum(
        "mjr,jwr->mjw", retained_gradient, state_lookup, preferred_element_type=jnp.float32
    )
    grad_k_rot = jnp.einsum(
        "htn,thk->nhk", grad_scores, rotated_queries, preferred_element_type=jnp.float32
    )
    state_grad_own = jnp.einsum(
        "ybn,ybw->bnw",
        rotated_queries.astype(jnp.float32) * continuation_factor[:, :, None],
        retained_gradient.astype(jnp.float32),
        precision=lax.Precision.HIGHEST,
    )
    grad_slots = group_onehot[:, None, None, None] * state_grad_own[None]
    grad_summed = lax.psum(grad_slots, "dp")
    state_gradient = (
        prompt_flag * jnp.sum(grad_summed * group_onehot[:, None, None, None], axis=0)
    ).astype(jnp.bfloat16)
    grad_k_rot = grad_k_rot + state_weighting[:, :, None] * jnp.einsum(
        "ilm,lpm->ilp", reduced_values, state_gradient, preferred_element_type=jnp.float32
    )
    grad_values = grad_values + state_weighting[:, :, None] * jnp.einsum(
        "zdo,doi->zdi", rotated_keys, state_gradient, preferred_element_type=jnp.float32
    )
    grad_queries = (
        rotate_back(grad_q_rot * q_scale, cosine, sine_tab, grow_fac)
        .reshape(seg_len, heads_local * DK)
        .astype(jnp.bfloat16)
    )
    grad_keys = (
        rotate_back(grad_k_rot, cosine, sine_tab, shrink)
        .reshape(seg_len, heads_local * DK)
        .astype(jnp.bfloat16)
    )
    grad_vlow = grad_values.reshape(seg_len, heads_local * DV).astype(jnp.bfloat16)
    grad_wq = contract_first(a_all, grad_queries)
    grad_wk = contract_first(a_all, grad_keys)
    grad_wv = contract_first(a_all, grad_vlow)
    grad_wg = contract_first(a_all, grad_gate)
    grad_a_terms = (
        contract_last(grad_queries, wq_full)
        + contract_last(grad_keys, wk_full)
        + contract_last(grad_vlow, wv_full)
        + contract_last(grad_gate, wg_full)
    )
    grad_a = scatter_rows(grad_a_terms)
    grad_gain1_part = jnp.sum(grad_a * normed_one, axis=0)
    grad_bias1_part = jnp.sum(grad_a, axis=0)
    grad_tokens = grad_hidden + norm_back(grad_a * gain_one, normed_one, inv_one)
    attn_reduced = (
        lax.psum_scatter(grad_gain1_part, "dp", scatter_dimension=0, tiled=True),
        lax.psum_scatter(grad_bias1_part, "dp", scatter_dimension=0, tiled=True),
        lax.psum_scatter(grad_wq, "dp", scatter_dimension=0, tiled=True),
        lax.psum_scatter(grad_wk, "dp", scatter_dimension=0, tiled=True),
        lax.psum_scatter(grad_wv, "dp", scatter_dimension=0, tiled=True),
        lax.psum_scatter(grad_wg, "dp", scatter_dimension=0, tiled=True),
        lax.psum_scatter(grad_wo, "dp", scatter_dimension=0, tiled=True),
    )
    norm_sums = lax.psum((attn_reduced[0], attn_reduced[1], ffn_reduced[0], ffn_reduced[1]), "mp")
    return (
        block_out,
        grad_tokens,
        loss_value,
        norm_sums[0],
        norm_sums[1],
        attn_reduced[2],
        attn_reduced[3],
        attn_reduced[4],
        attn_reduced[5],
        attn_reduced[6],
        norm_sums[2],
        norm_sums[3],
        ffn_reduced[2],
        ffn_reduced[3],
    )


def solution(mesh):
    return jax.shard_map(
        on_device,
        mesh=mesh,
        in_specs=(
            P(("dp", "mp"), None),
            P(("dp", "mp"), None),
            P("dp", "mp"),
            P(),
            P(),
            P("dp"),
            P("dp"),
            P("dp", "mp"),
            P("dp", "mp"),
            P("dp", "mp"),
            P("dp", "mp"),
            P("dp", "mp"),
            P("dp"),
            P("dp"),
            P("dp", "mp"),
            P("dp", "mp"),
        ),
        out_specs=(
            P(("dp", "mp"), None),
            P(("dp", "mp"), None),
            P(),
            P("dp"),
            P("dp"),
            P("dp", "mp"),
            P("dp", "mp"),
            P("dp", "mp"),
            P("dp", "mp"),
            P("dp", "mp"),
            P("dp"),
            P("dp"),
            P("dp", "mp"),
            P("dp", "mp"),
        ),
        check_vma=False,
    )
```

profile of v0, /device:TPU:0, one launch (start us, length us, event | category | flops | bytes accessed | tf_op | source)
XLA Modules:
  0.0 2218.6 jit_solution(17705684298100000474)
XLA Ops:
  9.8 23.3 %all-gather = bf16[16,1,128]{2,1,0:T(2,128)(2,1)S(1)} all-gather(bf16[1,1,128]{2,1,0:T(2,128)(2,1)} %bitcast.140), channel_id=1, replica_groups=mesh['dp'=16,'mp'=2] {'dp'}, dimensions={0}, use_global_device_ids=true | all-gather | bytes 4352 | tf_op jit(solution)/shard_map/all_gather | solution.py:123
  33.1 17.6 all-gather.1
  64.5 8.4 all-gather.16.cloned.1.call-done
  72.8 52.6 %all-gather.24.cloned.1.call-done = bf16[2048,1024]{1,0:T(8,128)(2,1)} async-done(((bf16[128,1024]{1,0:T(8,128)(2,1)}), bf16[2048,1024]{1,0:T(8,128)(2,1)}) %all-gather.24.cloned.1.call-update) | async-done | bytes 4194320 | tf_op jit(solution)/shard_map/all_gather | solution.py:126
  129.7 46.8 %all-gather.22.cloned.1.call-done = bf16[2048,1024]{1,0:T(8,128)(2,1)} async-done(((bf16[128,1024]{1,0:T(8,128)(2,1)}), bf16[2048,1024]{1,0:T(8,128)(2,1)}) %all-gather.22.cloned.1.call-update) | async-done | bytes 4194320 | tf_op jit(solution)/shard_map/all_gather | solution.py:125
  185.0 66.4 %all-gather.20.cloned.1.call-done = bf16[2048,2048]{1,0:T(8,128)(2,1)} async-done(((bf16[128,2048]{1,0:T(8,128)(2,1)}), bf16[2048,2048]{1,0:T(8,128)(2,1)}) %all-gather.20.cloned.1.call-update) | async-done | bytes 8388624 | tf_op jit(solution)/shard_map/all_gather | solution.py:127
  265.3 61.0 %all-gather.18.cloned.1.call-done = bf16[2048,2048]{1,0:T(8,128)(2,1)} async-done(((bf16[128,2048]{1,0:T(8,128)(2,1)}), bf16[2048,2048]{1,0:T(8,128)(2,1)}) %all-gather.18.cloned.1.call-update) | async-done | bytes 8388624 | tf_op jit(solution)/shard_map/all_gather | solution.py:128
  339.0 100.6 %all-reduce.10.cloned.1.call-done = f32[2,4,256,512]{3,2,1,0:T(8,128)} async-done(((f32[2,4,256,512]{3,2,1,0:T(8,128)}), f32[2,4,256,512]{3,2,1,0:T(8,128)}) %all-reduce.10.cloned.1.call-update) | async-done | bytes 4194320 | tf_op jit(solution)/shard_map/psum | solution.py:207
  445.7 69.5 %all-gather.26.cloned.1.call-done = bf16[2048,2048]{1,0:T(8,128)(2,1)} async-done(((bf16[128,2048]{1,0:T(8,128)(2,1)}), bf16[2048,2048]{1,0:T(8,128)(2,1)}) %all-gather.26.cloned.1.call-update) | async-done | bytes 8388624 | tf_op jit(solution)/shard_map/all_gather | solution.py:129
  523.2 19.0 all-gather.2
  542.2 17.4 all-gather.3
  564.6 64.9 %all-gather.30.cloned.1.call-done = bf16[2048,2048]{1,0:T(8,128)(2,1)} async-done(((bf16[128,2048]{1,0:T(8,128)(2,1)}), bf16[2048,2048]{1,0:T(8,128)(2,1)}) %all-gather.30.cloned.1.call-update) | async-done | bytes 8388624 | tf_op jit(solution)/shard_map/all_gather | solution.py:134
  629.5 21.9 all-gather.28.cloned.1.call-done
  651.4 10.6 multiply_convert_fusion.2
  662.0 65.9 %all-gather.32.cloned.1.call-done = bf16[2048,2048]{1,0:T(8,128)(2,1)} async-done(((bf16[128,2048]{1,0:T(8,128)(2,1)}), bf16[2048,2048]{1,0:T(8,128)(2,1)}) %all-gather.32.cloned.1.call-update) | async-done | bytes 8388624 | tf_op jit(solution)/shard_map/all_gather | solution.py:135
  737.8 28.2 %reduce-scatter.14.cloned.1.call-done = f32[128,2048]{1,0:T(8,128)} async-done(((f32[256,2048]{1,0:T(8,128)}), f32[128,2048]{1,0:T(8,128)}) %reduce-scatter.14.cloned.1.call-update) | async-done | bytes 1048592 | tf_op jit(solution)/shard_map/reduce_scatter | solution.py:92
  769.2 39.5 %all-reduce.4 = (f32[]{:T(128)}, f32[]{:T(128)}) all-reduce(f32[]{:T(128)} %get-tuple-element.39, f32[]{:T(128)} %get-tuple-element.37), channel_id=1, replica_groups=mesh['dp'=16,'mp'=2] {'dp','mp'}, use_global_device_ids=true, to_apply=%region_14.15 | all-reduce | flops 2 | bytes 16 | tf_op jit(solution)/shard_map/psum | solution.py:233
  811.9 22.3 %all-gather.34.cloned.1.call-done = bf16[256,2048]{1,0:T(8,128)(2,1)} async-done(((bf16[128,2048]{1,0:T(8,128)(2,1)}), bf16[256,2048]{1,0:T(8,128)(2,1)}) %all-gather.34.cloned.1.call-update) | async-done | bytes 1048592 | tf_op jit(solution)/shard_map/all_gather | solution.py:88
  850.2 31.8 %reduce-scatter.16.cloned.1.call-done = f32[128,2048]{1,0:T(8,128)} async-done(((f32[256,2048]{1,0:T(8,128)}), f32[128,2048]{1,0:T(8,128)}) %reduce-scatter.16.cloned.1.call-update) | async-done | bytes 1048592 | tf_op jit(solution)/shard_map/reduce_scatter | solution.py:92
  887.6 21.4 all-gather.36.cloned.1.call-done
  936.7 98.4 %all-reduce.12.cloned.1.call-done = f32[2,4,256,512]{3,2,1,0:T(8,128)} async-done(((f32[2,4,256,512]{3,2,1,0:T(8,128)}), f32[2,4,256,512]{3,2,1,0:T(8,128)}) %all-reduce.12.cloned.1.call-update) | async-done | bytes 4194320 | tf_op jit(solution)/shard_map/psum | solution.py:285
  1068.8 9.4 fusion.82
  1079.4 9.4 fusion.83
  1090.0 9.8 fusion.81
  1100.2 9.8 fusion.80
  1124.5 62.8 %all-reduce.5 = (f32[2048]{0:T(1024)S(1)}, f32[2048]{0:T(1024)S(1)}, f32[2048]{0:T(1024)S(1)}, f32[2048]{0:T(1024)S(1)}) all-reduce(f32[2048]{0:T(1024)S(1)} %get-tuple-element.18, f32[2048]{0:T(1024)S(1)} %get-tuple-element.23, f32[2048]{0:T(1024)S(1)} %copy-done.51, ...), channel_id=6, replica_groups=mesh['dp'=16,'mp'=2] {'dp'}, use_global_device_ids=true, to_apply=%region_28.29.clone | all-reduce | flops 8192 | bytes 65536
  1196.8 107.8 %reduce-scatter.20.cloned.1.call-done = f32[128,1024]{1,0:T(8,128)} async-done(((f32[2048,1024]{1,0:T(8,128)}), f32[128,1024]{1,0:T(8,128)}) %reduce-scatter.20.cloned.1.call-update) | async-done | bytes 524304 | tf_op jit(solution)/shard_map/reduce_scatter | solution.py:323
  1304.6 181.5 %reduce-scatter.30.cloned.1.call-done = f32[128,2048]{1,0:T(8,128)} async-done(((f32[2048,2048]{1,0:T(8,128)}), f32[128,2048]{1,0:T(8,128)}) %reduce-scatter.30.cloned.1.call-update) | async-done | bytes 1048592 | tf_op jit(solution)/shard_map/reduce_scatter | solution.py:251
  1486.1 181.1 %reduce-scatter.32.cloned.1.call-done = f32[128,2048]{1,0:T(8,128)} async-done(((f32[2048,2048]{1,0:T(8,128)}), f32[128,2048]{1,0:T(8,128)}) %reduce-scatter.32.cloned.1.call-update) | async-done | bytes 1048592 | tf_op jit(solution)/shard_map/reduce_scatter | solution.py:252
  1667.2 181.1 %reduce-scatter.28.cloned.1.call-done = f32[128,2048]{1,0:T(8,128)} async-done(((f32[2048,2048]{1,0:T(8,128)}), f32[128,2048]{1,0:T(8,128)}) %reduce-scatter.28.cloned.1.call-update) | async-done | bytes 1048592 | tf_op jit(solution)/shard_map/reduce_scatter | solution.py:327
  1848.3 181.1 %reduce-scatter.26.cloned.1.call-done = f32[128,2048]{1,0:T(8,128)} async-done(((f32[2048,2048]{1,0:T(8,128)}), f32[128,2048]{1,0:T(8,128)}) %reduce-scatter.26.cloned.1.call-update) | async-done | bytes 1048592 | tf_op jit(solution)/shard_map/reduce_scatter | solution.py:326
  2029.5 181.0 %reduce-scatter.24.cloned.1.call-done = f32[128,2048]{1,0:T(8,128)} async-done(((f32[2048,2048]{1,0:T(8,128)}), f32[128,2048]{1,0:T(8,128)}) %reduce-scatter.24.cloned.1.call-update) | async-done | bytes 1048592 | tf_op jit(solution)/shard_map/reduce_scatter | solution.py:325
  (299 shorter events, 195.0 us)
Async XLA Ops:
  7.2 65.6 %all-gather.16.cloned.1.call-start = ((), (), s32[]{:S(2)}) async-start(), calls=%async_computation.11 | async-start | bytes 1572864 | tf_op jit(solution)/shard_map/all_gather | solution.py:88
  53.1 72.4 %all-gather.24.cloned.1.call-start = ((), (), s32[]{:S(2)}) async-start(), calls=%async_computation.15 | async-start | bytes 4456448 | tf_op jit(solution)/shard_map/all_gather | solution.py:126
  53.8 122.7 %all-gather.22.cloned.1.call-start = ((), (), s32[]{:S(2)}) async-start(), calls=%async_computation.14 | async-start | bytes 4456448 | tf_op jit(solution)/shard_map/all_gather | solution.py:125
  54.5 196.9 %all-gather.20.cloned.1.call-start = ((), (), s32[]{:S(2)}) async-start(), calls=%async_computation.13 | async-start | bytes 8912896 | tf_op jit(solution)/shard_map/all_gather | solution.py:127
  55.1 271.2 %all-gather.18.cloned.1.call-start = ((), (), s32[]{:S(2)}) async-start(), calls=%async_computation.12 | async-start | bytes 8912896 | tf_op jit(solution)/shard_map/all_gather | solution.py:128
  55.7 383.9 %all-reduce.10.cloned.1.call-start = ((), (), s32[]{:S(2)}) async-start(), calls=%async_computation.16 | async-start | bytes 8388608 | tf_op jit(solution)/shard_map/psum | solution.py:207
  61.6 378.1 %copy-start.57 = (f32[2]{0:T(128)}, f32[2]{0:T(128)S(1)}, u32[]{:S(2)}) copy-start(f32[2]{0:T(128)S(1)} %compare_convert_fusion) | copy-start | bytes 28
  62.3 201.8 %copy-start.66 = (f32[4]{0:T(128)}, f32[4]{0:T(128)S(1)}, u32[]{:S(2)}) copy-start(f32[4]{0:T(128)S(1)} %subtract_log_fusion) | copy-start | bytes 52
  62.4 194.7 %copy-start.46 = (f32[256,4]{0,1:T(4,128)}, f32[256,4]{0,1:T(4,128)S(1)}, u32[]{:S(2)}) copy-start(f32[256,4]{0,1:T(4,128)S(1)} %get-tuple-element.64) | copy-start | bytes 12292
  62.4 380.2 %copy-start.48 = (f32[256,4]{0,1:T(4,128)}, f32[256,4]{0,1:T(4,128)S(1)}, u32[]{:S(2)}) copy-start(f32[256,4]{0,1:T(4,128)S(1)} %get-tuple-element.65) | copy-start | bytes 12292
  257.1 80.0 %copy-start.5 = (bf16[256,2048]{1,0:T(8,128)(2,1)}, bf16[256,2048]{1,0:T(8,128)(2,1)S(1)}, u32[]{:S(2)}) copy-start(bf16[256,2048]{1,0:T(8,128)(2,1)S(1)} %convolution_convert_fusion) | copy-start | bytes 3145732
  261.1 254.1 %all-gather.26.cloned.1.call-start = ((), (), s32[]{:S(2)}) async-start(), calls=%async_computation.17 | async-start | bytes 8912896 | tf_op jit(solution)/shard_map/all_gather | solution.py:129
  261.9 298.4 %reduce-scatter.12.cloned.1.call-start = ((), (), s32[]{:S(2)}) async-start(), calls=%async_computation.18 | async-start | bytes 3145728 | tf_op jit(solution)/shard_map/reduce_scatter | solution.py:92
  264.1 178.6 %copy-start.13 = (bf16[256,4,256]{2,0,1:T(8,128)(2,1)}, bf16[256,4,256]{2,0,1:T(8,128)(2,1)S(1)}, u32[]{:S(2)}) copy-start(bf16[256,4,256]{2,0,1:T(8,128)(2,1)S(1)} %fusion.41) | copy-start | bytes 1572868
  522.4 107.2 %all-gather.30.cloned.1.call-start = ((), (), s32[]{:S(2)}) async-start(), calls=%async_computation.20 | async-start | bytes 8912896 | tf_op jit(solution)/shard_map/all_gather | solution.py:134
  523.1 128.3 %all-gather.28.cloned.1.call-start = ((), (), s32[]{:S(2)}) async-start(), calls=%async_computation.19 | async-start | bytes 1572864 | tf_op jit(solution)/shard_map/all_gather | solution.py:88
  563.7 164.2 %all-gather.32.cloned.1.call-start = ((), (), s32[]{:S(2)}) async-start(), calls=%async_computation.21 | async-start | bytes 8912896 | tf_op jit(solution)/shard_map/all_gather | solution.py:135
  564.4 201.6 %reduce-scatter.14.cloned.1.call-start = ((), (), s32[]{:S(2)}) async-start(), calls=%async_computation.22 | async-start | bytes 3145728 | tf_op jit(solution)/shard_map/reduce_scatter | solution.py:92
  735.4 98.8 %all-gather.34.cloned.1.call-start = ((), (), s32[]{:S(2)}) async-start(), calls=%async_computation.23 | async-start | bytes 1572864 | tf_op jit(solution)/shard_map/all_gather | solution.py:88
  811.8 70.2 %reduce-scatter.16.cloned.1.call-start = ((), (), s32[]{:S(2)}) async-start(), calls=%async_computation.24 | async-start | bytes 3145728 | tf_op jit(solution)/shard_map/reduce_scatter | solution.py:92
  850.0 59.0 %all-gather.36.cloned.1.call-start = ((), (), s32[]{:S(2)}) async-start(), calls=%async_computation.25 | async-start | bytes 1572864 | tf_op jit(solution)/shard_map/all_gather | solution.py:88
  887.5 147.5 %all-reduce.12.cloned.1.call-start = ((), (), s32[]{:S(2)}) async-start(), calls=%async_computation.26 | async-start | bytes 8388608 | tf_op jit(solution)/shard_map/psum | solution.py:285
  923.8 198.8 %reduce-scatter.18.cloned.1.call-start = ((), (), s32[]{:S(2)}) async-start(), calls=%async_computation.27 | async-start | bytes 3145728 | tf_op jit(solution)/shard_map/reduce_scatter | solution.py:92
  936.7 101.4 %copy-start.12 = (f32[4,512,256]{2,1,0:T(8,128)S(1)}, f32[4,512,256]{2,1,0:T(8,128)}, u32[]{:S(2)}) copy-start(f32[4,512,256]{2,1,0:T(8,128)} %fusion.76) | copy-start | bytes 6291460
  936.7 101.4 %copy-start.47 = (f32[256,4]{0,1:T(4,128)S(1)}, f32[256,4]{0,1:T(4,128)}, u32[]{:S(2)}) copy-start(f32[256,4]{0,1:T(4,128)} %copy-done.46) | copy-start | bytes 12292
  1056.9 139.8 %reduce-scatter.22.cloned.1.call-start = ((), (), s32[]{:S(2)}) async-start(), calls=%async_computation.29 | async-start | bytes 8912896 | tf_op jit(solution)/shard_map/reduce_scatter | solution.py:324
  1062.9 241.6 %reduce-scatter.20.cloned.1.call-start = ((), (), s32[]{:S(2)}) async-start(), calls=%async_computation.28 | async-start | bytes 8912896 | tf_op jit(solution)/shard_map/reduce_scatter | solution.py:323
  1067.6 418.4 %reduce-scatter.30.cloned.1.call-start = ((), (), s32[]{:S(2)}) async-start(), calls=%async_computation.33 | async-start | bytes 17825792 | tf_op jit(solution)/shard_map/reduce_scatter | solution.py:251
  1078.2 589.0 %reduce-scatter.32.cloned.1.call-start = ((), (), s32[]{:S(2)}) async-start(), calls=%async_computation.34 | async-start | bytes 17825792 | tf_op jit(solution)/shard_map/reduce_scatter | solution.py:252
  1088.8 759.5 %reduce-scatter.28.cloned.1.call-start = ((), (), s32[]{:S(2)}) async-start(), calls=%async_computation.32 | async-start | bytes 17825792 | tf_op jit(solution)/shard_map/reduce_scatter | solution.py:327
  1099.9 929.6 %reduce-scatter.26.cloned.1.call-start = ((), (), s32[]{:S(2)}) async-start(), calls=%async_computation.31 | async-start | bytes 17825792 | tf_op jit(solution)/shard_map/reduce_scatter | solution.py:326
  1109.9 1100.5 %reduce-scatter.24.cloned.1.call-start = ((), (), s32[]{:S(2)}) async-start(), calls=%async_computation.30 | async-start | bytes 17825792 | tf_op jit(solution)/shard_map/reduce_scatter | solution.py:325
  (65 other events, 695.0 us)
Sparse Core Ops, SparseCore 0:
  53.2 19.6 all-gather.15
  75.0 50.3 all-gather.23
  127.6 48.8 all-gather.21
  178.5 72.8 all-gather.19
  253.4 72.8 all-gather.17
  329.9 109.7 all-reduce.9
  441.8 73.4 all-gather.25
  522.5 30.4 reduce-scatter.11
  555.2 74.3 all-gather.29
  631.5 19.8 all-gather.27
  653.6 74.2 all-gather.31
  735.5 30.4 reduce-scatter.13
  811.9 22.1 all-gather.33
  850.1 31.8 reduce-scatter.15
  887.7 21.2 all-gather.35
  923.9 111.1 all-reduce.11
  1057.0 31.0 reduce-scatter.17
  1092.6 104.1 reduce-scatter.21
  1201.4 103.1 reduce-scatter.19
  1309.1 176.9 reduce-scatter.29
  1490.8 176.4 reduce-scatter.31
  1671.9 176.3 reduce-scatter.27
  1853.0 176.3 reduce-scatter.25
  2034.0 176.3 reduce-scatter.23
where the time goes:
time: 2230 us; the launch traced here: 2220 us
  waiting for transfers between devices  1780 us (80%)
  blocking collectives  185 us (8%)
  matrix products  155 us (7%)
  other arithmetic  51.2 us (2%)
  local copies, waits for them, and re-layouts  23 us (1%)
    reduce_scatter x1, waiting for transfers between devices, on_device(): lax.psum_scatter(grad_wu, 'dp', scatter_dimension=0, tiled=True)  182 us
    reduce_scatter x1, waiting for transfers between devices, on_device(): lax.psum_scatter(grad_wd, 'dp', scatter_dimension=0, tiled=True)  181 us
    reduce_scatter x1, waiting for transfers between devices, on_device(): lax.psum_scatter(grad_wg, 'dp', scatter_dimension=0, tiled=True)  181 us
    reduce_scatter x1, waiting for transfers between devices, on_device(): lax.psum_scatter(grad_wo, 'dp', scatter_dimension=0, tiled=True)  181 us
    reduce_scatter x1, waiting for transfers between devices, on_device(): lax.psum_scatter(grad_wv, 'dp', scatter_dimension=0, tiled=True)  181 us
    reduce_scatter x1, waiting for transfers between devices, on_device(): lax.psum_scatter(grad_wq, 'dp', scatter_dimension=0, tiled=True)  108 us
    psum x1, waiting for transfers between devices, on_device(): summed = lax.psum(slots, 'dp')  101 us
    psum x1, waiting for transfers between devices, on_device(): grad_summed = lax.psum(grad_slots, 'dp')  98.4 us
  transfers between devices with their start and end apart: 24, of which 22 were waited for; matrix products, arithmetic and copies ran while one was open for 6% of the time, Pallas kernels for 0%

commit v1 on v0

v1 whole, which is shorter than its diff:
```python
import math

import jax
import jax.numpy as jnp
from jax import lax
from jax.experimental import pallas as pl
from jax.experimental.pallas import tpu as pltpu
from jax.sharding import PartitionSpec as P

DK = 256
DV = 512


EPSILON = 1e-05
GROUP_EPSILON = 0.05


def norm_stats(values, floor_eps):
    center = jnp.mean(values, axis=-1, keepdims=True)
    shifted = values - center
    inv_std = lax.rsqrt(jnp.mean(shifted * shifted, axis=-1, keepdims=True) + floor_eps)
    return (shifted * inv_std, inv_std)


def norm_back(grad_in, normed, inv_std):
    mean_grad = jnp.mean(grad_in, axis=-1, keepdims=True)
    mean_proj = jnp.mean(grad_in * normed, axis=-1, keepdims=True)
    return (grad_in - mean_grad - normed * mean_proj) * inv_std


def xpos_tables(positions, direction):
    half_dim = DK // 2
    pair_index = jnp.arange(half_dim, dtype=jnp.float32)
    frequency = jnp.exp(-(2.0 * pair_index / DK) * math.log(10000.0))
    base_ratio = (2.0 * pair_index / DK + 0.4) / 1.4
    angles = positions[:, None] * frequency[None, :]
    factor = jnp.exp(direction * (positions[:, None] / 512.0) * jnp.log(base_ratio)[None, :])
    return (jnp.cos(angles), jnp.sin(angles), factor)


def rotate_pairs(values, cosine, sine_tab, factor):
    half_dim = values.shape[-1] // 2
    first_half = values[..., :half_dim]
    second = values[..., half_dim:]
    cosine = cosine[:, None, :]
    sine_tab = sine_tab[:, None, :]
    factor = factor[:, None, :]
    return jnp.concatenate(
        [
            (first_half * cosine - second * sine_tab) * factor,
            (second * cosine + first_half * sine_tab) * factor,
        ],
        axis=-1,
    )


def rotate_back(grad_rot, cosine, sine_tab, factor):
    half_dim = grad_rot.shape[-1] // 2
    first_half = grad_rot[..., :half_dim]
    second = grad_rot[..., half_dim:]
    cosine = cosine[:, None, :]
    sine_tab = sine_tab[:, None, :]
    factor = factor[:, None, :]
    return jnp.concatenate(
        [
            (first_half * cosine + second * sine_tab) * factor,
            (second * cosine - first_half * sine_tab) * factor,
        ],
        axis=-1,
    )


def plain_dot(first_op, second_op):
    return jnp.dot(first_op, second_op, preferred_element_type=jnp.float32)


def contract_last(first_op, second_op):
    return lax.dot_general(
        first_op, second_op, (((1,), (1,)), ((), ())), preferred_element_type=jnp.float32
    )


def contract_first(first_op, second_op):
    return lax.dot_general(
        first_op, second_op, (((0,), (0,)), ((), ())), preferred_element_type=jnp.float32
    )


class Ring:
    def __init__(self):
        self.devices = lax.axis_size("dp")
        self.chips = self.devices // 2
        half = self.chips // 2
        self.order = [2 * a for a in range(half)] + [2 * a + 1 for a in reversed(range(half))]
        self.index = lax.axis_index("dp")
        self.core = self.index % 2
        chip = self.index // 2
        self.place = jnp.where(chip % 2 == 0, chip // 2, self.chips - 1 - chip // 2)
        self.near = self.chips // 2
        self.far = self.chips - 1 - self.near

    def shift(self, rows, step):
        pairs = [
            (self.order[i] * 2 + c, self.order[(i + step) % self.chips] * 2 + c)
            for i in range(self.chips)
            for c in range(2)
        ]
        return lax.ppermute(rows, "dp", pairs)

    def swap(self, rows):
        return lax.ppermute(rows, "dp", [(i, i ^ 1) for i in range(self.devices)])

    def hops(self, flip):
        return (self.far, self.near) if flip else (self.near, self.far)

    def block_table(self):
        spot = (self.place + jnp.arange(self.chips, dtype=jnp.int32)) % self.chips
        chip = jnp.where(spot < self.chips // 2, 2 * spot, 2 * (self.chips - 1 - spot) + 1)
        return jnp.concatenate([chip * 2 + self.core, chip * 2 + 1 - self.core]).astype(jnp.int32)

    def gather(self, shard, flip):
        up, down = self.hops(flip)
        pieces = [None] * self.chips
        pieces[0] = shard
        moving_up, moving_down = shard, shard
        for step in range(1, max(up, down) + 1):
            if step <= up:
                moving_up = self.shift(moving_up, 1)
                pieces[self.chips - step] = moving_up
            if step <= down:
                moving_down = self.shift(moving_down, -1)
                pieces[step] = moving_down
        return pieces

    def reduce(self, term, flip):
        up, down = self.hops(flip)
        moving_up = term(up).astype(jnp.bfloat16)
        moving_down = term(self.chips - down).astype(jnp.bfloat16)
        for step in range(1, max(up, down) + 1):
            if step <= up:
                moving_up = self.shift(moving_up, 1)
                if step < up:
                    moving_up = (moving_up.astype(jnp.float32) + term(up - step)).astype(
                        jnp.bfloat16
                    )
            if step <= down:
                moving_down = self.shift(moving_down, -1)
                if step < down:
                    moving_down = (
                        moving_down.astype(jnp.float32) + term(self.chips - down + step)
                    ).astype(jnp.bfloat16)
        return term(0) + moving_up.astype(jnp.float32) + moving_down.astype(jnp.float32)

    def reduce_exact(self, parts, flip):
        up, down = self.hops(flip)
        moving_up, moving_down = parts(up), parts(self.chips - down)
        for step in range(1, max(up, down) + 1):
            if step <= up:
                moving_up = self.shift(moving_up, 1)
                if step < up:
                    moving_up = moving_up + parts(up - step)
            if step <= down:
                moving_down = self.shift(moving_down, -1)
                if step < down:
                    moving_down = moving_down + parts(self.chips - down + step)
        return parts(0) + moving_up + moving_down


def move_blocks(rows, table, outward):
    blocks = table.shape[0]
    width = rows.shape[1] // blocks

    def kernel(table_ref, in_ref, out_ref):
        for place in range(blocks):
            there = pl.ds(pl.multiple_of(table_ref[place] * width, width), width)
            here = pl.ds(place * width, width)
            if outward:
                out_ref[:, there] = in_ref[:, here]
            else:
                out_ref[:, here] = in_ref[:, there]

    if width % 128:
        order = table
        if outward:
            order = jnp.sum(
                jnp.where(table[None, :] == jnp.arange(blocks)[:, None], jnp.arange(blocks), 0),
                axis=1,
            )
        return jnp.take(rows.reshape(rows.shape[0], blocks, width), order, axis=1).reshape(
            rows.shape
        )
    return pl.pallas_call(
        kernel,
        out_shape=jax.ShapeDtypeStruct(rows.shape, rows.dtype),
        in_specs=[
            pl.BlockSpec(memory_space=pltpu.SMEM),
            pl.BlockSpec(memory_space=pltpu.VMEM),
        ],
        out_specs=pl.BlockSpec(memory_space=pltpu.VMEM),
    )(table, rows)


def swap_mp(rows):
    return lax.ppermute(rows, "mp", [(0, 1), (1, 0)])


def gather_rows(rows_low):
    return jnp.concatenate([rows_low, swap_mp(rows_low)], axis=0)


def scatter_rows(terms):
    half_rows = terms.shape[0] // 2
    arrived = swap_mp(terms[half_rows:].astype(jnp.bfloat16))
    return terms[:half_rows] + arrived.astype(jnp.float32)


def tie(value, other):
    return lax.optimization_barrier((value, other))[0]


def on_device(
    tokens_in,
    teacher,
    valid_mask,
    group_of,
    prompt_len,
    ln1_gain,
    ln1_bias,
    w_query,
    w_key,
    w_value,
    w_gate,
    w_out,
    ln2_gain,
    ln2_bias,
    w_up,
    w_down,
):
    half_rows = tokens_in.shape[0]
    model_dim = tokens_in.shape[1]
    seg_len = half_rows * lax.axis_size("mp")
    seg_count = group_of.shape[0]
    group_count = prompt_len.shape[0]
    heads_local = w_query.shape[1] // DK
    token_total = seg_len * seg_count
    dp_index = lax.axis_index("dp")
    mp_index = lax.axis_index("mp")
    ring = Ring()
    own_width = model_dim // 2
    table = ring.block_table()

    segment_ids = jnp.arange(seg_count, dtype=jnp.int32)
    my_group = jnp.sum(jnp.where(segment_ids == dp_index, group_of, 0))
    first_member = jnp.min(jnp.where(group_of == my_group, segment_ids, seg_count))
    prompt_flag = (first_member == dp_index).astype(jnp.float32)
    group_match = jnp.arange(group_count, dtype=jnp.int32) == my_group
    group_onehot = group_match.astype(jnp.float32)
    prompt_size = jnp.sum(jnp.where(group_match, prompt_len, 0))
    own_ids = mp_index * half_rows + jnp.arange(half_rows, dtype=jnp.int32)
    other_ids = (1 - mp_index) * half_rows + jnp.arange(half_rows, dtype=jnp.int32)
    token_ids = jnp.concatenate([own_ids, other_ids])
    loss_mask = valid_mask[0].astype(jnp.float32) * jnp.where(
        prompt_flag > 0, own_ids < prompt_size, True
    ).astype(jnp.float32)
    valid_count = lax.psum(jnp.sum(loss_mask.astype(jnp.int32)), ("dp", "mp")).astype(jnp.float32)

    vectors = jnp.stack([ln1_gain, ln1_bias, ln2_gain, ln2_bias])
    vector_own = jnp.concatenate(ring.gather(vectors, False), axis=1)
    vectors_full = jnp.concatenate([vector_own, ring.swap(vector_own)], axis=1).astype(jnp.float32)
    gain_one, bias_one, gain_two, bias_two = (vectors_full[i] for i in range(4))

    groups = [
        jnp.concatenate([w_key, w_value], axis=1),
        jnp.concatenate([w_query, w_gate], axis=1),
        w_out,
        w_up,
        w_down,
    ]
    gathered = []
    for i, shard in enumerate(groups):
        if i >= 2:
            shard = tie(shard, gathered[i - 2][0][ring.chips // 2])
        pieces = ring.gather(shard, i % 2 == 1)
        own = jnp.concatenate(pieces, axis=0)
        gathered.append((pieces, own, ring.swap(own)))
    full = [(own, other) for _, own, other in gathered]

    def times_full(rows, weight):
        return plain_dot(rows[:, :own_width], weight[0]) + plain_dot(rows[:, own_width:], weight[1])

    def times_full_t(rows, weight):
        return jnp.concatenate(
            [contract_last(rows, weight[0]), contract_last(rows, weight[1])], axis=1
        )

    key_width = w_key.shape[1]
    wkv, wqg, wo_full, wu_full, wd_full = full

    offset = jnp.where(prompt_flag > 0, 0, prompt_size)
    positions = (token_ids + offset).astype(jnp.float32)
    head_ids = (mp_index * heads_local + jnp.arange(heads_local, dtype=jnp.int32)).astype(
        jnp.float32
    )
    log_decay = jnp.log(1.0 - 2.0 ** (-5.0 - head_ids))
    before_end = token_ids < prompt_size
    state_age = (prompt_size - 1 - token_ids).astype(jnp.float32)
    state_weighting = jnp.where(
        (before_end & (prompt_flag > 0))[:, None],
        jnp.exp(log_decay[None, :] * jnp.maximum(state_age, 0.0)[:, None]),
        0.0,
    )
    float_ids = token_ids.astype(jnp.float32)
    continuation_factor = (1.0 - prompt_flag) * jnp.exp(
        log_decay[None, :] * (float_ids + 1.0)[:, None]
    )
    distance = float_ids[:, None] - float_ids[None, :]
    decay_mat = jnp.where(
        distance[None] >= 0.0,
        jnp.exp(log_decay[:, None, None] * jnp.maximum(distance, 0.0)[None]),
        0.0,
    )
    token_rows = move_blocks(tokens_in, table, False).astype(jnp.float32)
    teacher_rows = move_blocks(teacher, table, False).astype(jnp.float32)
    normed_one, inv_one = norm_stats(token_rows, EPSILON)
    a_all = gather_rows((normed_one * gain_one + bias_one).astype(jnp.bfloat16))
    key_value = times_full(a_all, wkv)
    keys_raw = key_value[:, :key_width].reshape(seg_len, heads_local, DK)
    reduced_values = (
        key_value[:, key_width:].astype(jnp.bfloat16).reshape(seg_len, heads_local, DV)
    )
    query_gate = times_full(a_all, wqg)
    queries = query_gate[:, :key_width].reshape(seg_len, heads_local, DK)
    gate_pre = query_gate[:, key_width:]
    cosine, sine_tab, grow_fac = xpos_tables(positions, 1.0)
    _, _, shrink = xpos_tables(positions, -1.0)
    q_scale = DK ** (-0.5)
    rotated_keys = rotate_pairs(keys_raw, cosine, sine_tab, shrink).astype(jnp.bfloat16)
    local_state = jnp.einsum(
        "jld,jla->lda",
        (rotated_keys.astype(jnp.float32) * state_weighting[:, :, None]).astype(jnp.bfloat16),
        reduced_values,
        preferred_element_type=jnp.float32,
    )
    slots = (group_onehot[:, None, None, None] * (prompt_flag * local_state)[None]).astype(
        jnp.bfloat16
    )
    summed = lax.psum(slots, "dp")
    state_lookup = jnp.sum(
        summed.astype(jnp.float32) * group_onehot[:, None, None, None], axis=0
    ).astype(jnp.bfloat16)
    rotated_queries = (rotate_pairs(queries, cosine, sine_tab, grow_fac) * q_scale).astype(
        jnp.bfloat16
    )
    scores = jnp.einsum(
        "thk,nhk->htn", rotated_queries, rotated_keys, preferred_element_type=jnp.float32
    )
    weights_low = (scores * decay_mat).astype(jnp.bfloat16)
    retained_output = jnp.einsum(
        "htn,nhv->thv", weights_low, reduced_values, preferred_element_type=jnp.float32
    )
    carried_forward = jnp.einsum(
        "ozi,ziw->ozw", rotated_queries, state_lookup, preferred_element_type=jnp.float32
    )
    retained_output = retained_output + continuation_factor[:, :, None] * carried_forward
    grouped, inv_group = norm_stats(retained_output, GROUP_EPSILON)
    gate_act = jax.nn.silu(gate_pre).reshape(seg_len, heads_local, DV)
    gated_out = (gate_act * grouped).reshape(seg_len, heads_local * DV).astype(jnp.bfloat16)
    attn_own = scatter_rows(times_full_t(gated_out, wo_full))
    hidden_res = token_rows + attn_own
    normed_two, inv_two = norm_stats(hidden_res, EPSILON)
    c_all = gather_rows((normed_two * gain_two + bias_two).astype(jnp.bfloat16))
    up_pre = times_full(c_all, wu_full)
    up_act = jax.nn.gelu(up_pre, approximate=False).astype(jnp.bfloat16)
    ffn_own = scatter_rows(times_full_t(up_act, wd_full))
    block_out = hidden_res + ffn_own
    error_rows = block_out - teacher_rows
    weighted = loss_mask[:, None] * error_rows
    squared = lax.psum(jnp.sum(weighted * error_rows), ("dp", "mp"))
    grad_out = token_total / valid_count * weighted
    loss_value = squared / (valid_count * model_dim)

    block = model_dim // ring.devices

    def weight_grad(feature_side, other_side, flip):
        mine = jnp.concatenate(
            [feature_side[:, :own_width], ring.swap(feature_side[:, own_width:])], axis=0
        )
        both = jnp.concatenate([other_side, ring.swap(other_side)], axis=0)

        def term(k):
            return contract_first(mine[:, k * block : (k + 1) * block], both)

        return ring.reduce(term, flip)

    grad_ffn_all = gather_rows(grad_out.astype(jnp.bfloat16))
    grad_wd = weight_grad(grad_ffn_all, up_act, False)
    grad_up_act = times_full(grad_ffn_all, wd_full)
    _, gelu_pull = jax.vjp(lambda inner: jax.nn.gelu(inner, approximate=False), up_pre)
    grad_up = gelu_pull(grad_up_act)[0].astype(jnp.bfloat16)
    grad_wu = weight_grad(c_all, grad_up, True)
    grad_c = scatter_rows(times_full_t(grad_up, wu_full))
    grad_gain2_part = jnp.sum(grad_c * normed_two, axis=0)
    grad_bias2_part = jnp.sum(grad_c, axis=0)
    grad_hidden = grad_out + norm_back(grad_c * gain_two, normed_two, inv_two)
    grad_attn_all = gather_rows(grad_hidden.astype(jnp.bfloat16))
    grad_wo = weight_grad(grad_attn_all, gated_out, False)
    grad_gated = times_full(grad_attn_all, wo_full).reshape(seg_len, heads_local, DV)
    _, silu_pull = jax.vjp(jax.nn.silu, gate_pre)
    grad_gate = silu_pull((grad_gated * grouped).reshape(seg_len, heads_local * DV))[0].astype(
        jnp.bfloat16
    )
    grad_wg = weight_grad(a_all, grad_gate, True)
    retained_gradient = norm_back(grad_gated * gate_act, grouped, inv_group).astype(jnp.bfloat16)
    state_grad_own = jnp.einsum(
        "ybn,ybw->bnw",
        (rotated_queries.astype(jnp.float32) * continuation_factor[:, :, None]).astype(
            jnp.bfloat16
        ),
        retained_gradient,
        preferred_element_type=jnp.float32,
    )
    grad_slots = (group_onehot[:, None, None, None] * state_grad_own[None]).astype(jnp.bfloat16)
    grad_summed = lax.psum(grad_slots, "dp")
    grad_weights = jnp.einsum(
        "thv,nhv->htn", retained_gradient, reduced_values, preferred_element_type=jnp.float32
    )
    grad_values = jnp.einsum(
        "htn,thv->nhv", weights_low, retained_gradient, preferred_element_type=jnp.float32
    )
    grad_scores = (grad_weights * decay_mat).astype(jnp.bfloat16)
    grad_q_rot = jnp.einsum(
        "htn,nhk->thk", grad_scores, rotated_keys, preferred_element_type=jnp.float32
    )
    grad_q_rot = grad_q_rot + continuation_factor[:, :, None] * jnp.einsum(
        "mjr,jwr->mjw", retained_gradient, state_lookup, preferred_element_type=jnp.float32
    )
    grad_k_rot = jnp.einsum(
        "htn,thk->nhk", grad_scores, rotated_queries, preferred_element_type=jnp.float32
    )
    grad_queries = (
        rotate_back(grad_q_rot * q_scale, cosine, sine_tab, grow_fac)
        .reshape(seg_len, heads_local * DK)
        .astype(jnp.bfloat16)
    )
    grad_wq = weight_grad(a_all, grad_queries, False)
    state_gradient = (
        prompt_flag
        * jnp.sum(grad_summed.astype(jnp.float32) * group_onehot[:, None, None, None], axis=0)
    ).astype(jnp.bfloat16)
    grad_k_rot = grad_k_rot + state_weighting[:, :, None] * jnp.einsum(
        "ilm,lpm->ilp", reduced_values, state_gradient, preferred_element_type=jnp.float32
    )
    grad_values = grad_values + state_weighting[:, :, None] * jnp.einsum(
        "zdo,doi->zdi", rotated_keys, state_gradient, preferred_element_type=jnp.float32
    )
    grad_keys = (
        rotate_back(grad_k_rot, cosine, sine_tab, shrink)
        .reshape(seg_len, heads_local * DK)
        .astype(jnp.bfloat16)
    )
    grad_vlow = grad_values.reshape(seg_len, heads_local * DV).astype(jnp.bfloat16)
    grad_key_value = jnp.concatenate([grad_keys, grad_vlow], axis=1)
    grad_wkv = weight_grad(a_all, grad_key_value, True)
    grad_query_gate = jnp.concatenate([grad_queries, grad_gate], axis=1)
    grad_a = scatter_rows(
        times_full_t(grad_query_gate, wqg) + times_full_t(grad_key_value, wkv)
    )
    grad_gain1_part = jnp.sum(grad_a * normed_one, axis=0)
    grad_bias1_part = jnp.sum(grad_a, axis=0)
    grad_tokens = grad_hidden + norm_back(grad_a * gain_one, normed_one, inv_one)

    sums = jnp.stack([grad_gain1_part, grad_bias1_part, grad_gain2_part, grad_bias2_part])
    sums = sums + swap_mp(sums)
    sums = sums[:, :own_width] + ring.swap(sums[:, own_width:])
    sums = ring.reduce_exact(lambda k: sums[:, k * block : (k + 1) * block], False)

    return (
        move_blocks(block_out, table, True),
        move_blocks(grad_tokens, table, True),
        loss_value,
        sums[0],
        sums[1],
        grad_wq,
        grad_wkv[:, :key_width],
        grad_wkv[:, key_width:],
        grad_wg,
        grad_wo,
        sums[2],
        sums[3],
        grad_wu,
        grad_wd,
    )


def solution(mesh):
    return jax.shard_map(
        on_device,
        mesh=mesh,
        in_specs=(
            P(("dp", "mp"), None),
            P(("dp", "mp"), None),
            P("dp", "mp"),
            P(),
            P(),
            P("dp"),
            P("dp"),
            P("dp", "mp"),
            P("dp", "mp"),
            P("dp", "mp"),
            P("dp", "mp"),
            P("dp", "mp"),
            P("dp"),
            P("dp"),
            P("dp", "mp"),
            P("dp", "mp"),
        ),
        out_specs=(
            P(("dp", "mp"), None),
            P(("dp", "mp"), None),
            P(),
            P("dp"),
            P("dp"),
            P("dp", "mp"),
            P("dp", "mp"),
            P("dp", "mp"),
            P("dp", "mp"),
            P("dp", "mp"),
            P("dp"),
            P("dp"),
            P("dp", "mp"),
            P("dp", "mp"),
        ),
        check_vma=False,
    )
```

time: 2230 us -> 1050 us (0.47)
  waiting for transfers between devices: 1780 us -> 482 us
  starting transfers between devices: 2.09 us -> 118 us
  blocking collectives: 185 us -> 82.4 us
  matrix products: 155 us -> 203 us
  local copies, waits for them, and re-layouts: 23 us -> 66.7 us
    reduce_scatter x11 -> x0, waiting for transfers between devices: 1080 us -> none  [the longest x1 182 us: on_device(): lax.psum_scatter(grad_wu, 'dp', scatter_dimension=0, tiled=True)]
    all_gather x11 -> x0, waiting for transfers between devices: 501 us -> none  [the longest x4 73.9 us: gather_rows(): return lax.all_gather(rows_low, 'mp', axis=0, tiled=True)]
    ppermute x0 -> x117, waiting for transfers between devices: none -> 341 us  [the longest x91 295 us: shift(): return lax.ppermute(rows, 'dp', pairs)]
    ppermute x0 -> x117, starting transfers between devices: none -> 118 us  [the longest x91 101 us: shift(): return lax.ppermute(rows, 'dp', pairs)]
    all_gather x4 -> x0, blocking collectives: 77.4 us -> none  [the longest x1 23.3 us: on_device(): lax.all_gather(ln1_gain, 'dp', axis=0, tiled=True)]
    unnamed x1 -> x0, blocking collectives: 62.8 us -> none
    dot_general x7 -> x48, matrix products: 55.9 us -> 102 us  [contract_first(): lax.dot_general(first_op, second_op, (((0,), (0,)), ((), ())), preferred_...]
    psum x1, waiting for transfers between devices: 98.4 us -> 52.8 us  [on_device(): grad_summed = lax.psum(grad_slots, 'dp')]
  transfers between devices with their start and end apart: 24 -> 119, of which waited for: 22 -> 53; matrix products, arithmetic and copies ran while one was open for 6% -> 28% of each run, Pallas kernels for 0% -> 1%
where the time goes in v1:
time: 1050 us; the launch traced here: 1040 us
  waiting for transfers between devices  482 us (46%)
  matrix products  203 us (19%)
  starting transfers between devices  118 us (11%)
  blocking collectives  82.4 us (8%)
  local copies, waits for them, and re-layouts  66.7 us (6%)
  other arithmetic  55.7 us (5%)
  between operations  20.9 us (2%)
    ppermute x91, waiting for transfers between devices, shift(): return lax.ppermute(rows, 'dp', pairs)  295 us
    dot_general x48, matrix products, contract_first(): lax.dot_general(first_op, second_op, (((0,), (0,)), ((), ())), preferred_...  102 us
    ppermute x91, starting transfers between devices, shift(): return lax.ppermute(rows, 'dp', pairs)  101 us
    psum x1, waiting for transfers between devices, on_device(): summed = lax.psum(slots, 'dp')  88.1 us
    psum x1, waiting for transfers between devices, on_device(): grad_summed = lax.psum(grad_slots, 'dp')  52.8 us
    ppermute x9, waiting for transfers between devices, swap_mp(): return lax.ppermute(rows, 'mp', [(0, 1), (1, 0)])  46.3 us
    dot_general x10, matrix products, plain_dot(): return jnp.dot(first_op, second_op, preferred_element_type=jnp.float32)  44.3 us
    psum x1, blocking collectives, on_device(): squared = lax.psum(jnp.sum(weighted * error_rows), ('dp', 'mp'))  41.9 us
  transfers between devices with their start and end apart: 119, of which 53 were waited for; matrix products, arithmetic and copies ran while one was open for 28% of the time, Pallas kernels for 1%

profile of v1, /device:TPU:0, one launch (start us, length us, event | category | flops | bytes accessed | tf_op | source)
XLA Modules:
  0.0 1036.9 jit_solution(15823194296306291889)
XLA Ops:
  40.3 12.9 %collective-permute-done.4 = bf16[4,128]{1,0:T(4,128)(2,1)S(1)} collective-permute-done((bf16[4,128]{1,0:T(4,128)(2,1)}, bf16[4,128]{1,0:T(4,128)(2,1)S(1)}, u32[]{:S(2)}, u32[]{:S(2)}) %collective-permute-start.4) | collective-permute-done | bytes 1056 | tf_op jit(solution)/shard_map/ppermute | solution.py:108
  65.0 9.2 collective-permute-done.17
  84.0 7.0 collective-permute-done.10
  93.7 14.2 %collective-permute-done.18 = bf16[128,3072]{1,0:T(8,128)(2,1)S(1)} collective-permute-done((bf16[128,3072]{1,0:T(8,128)(2,1)S(1)}, bf16[128,3072]{1,0:T(8,128)(2,1)S(1)}, u32[]{:S(2)}, u32[]{:S(2)}) %collective-permute-start.18) | collective-permute-done | bytes 786464 | tf_op jit(solution)/shard_map/ppermute | solution.py:108
  117.7 7.0 collective-permute-done.11
  127.4 14.3 %collective-permute-done.19 = bf16[128,3072]{1,0:T(8,128)(2,1)S(1)} collective-permute-done((bf16[128,3072]{1,0:T(8,128)(2,1)S(1)}, bf16[128,3072]{1,0:T(8,128)(2,1)S(1)}, u32[]{:S(2)}, u32[]{:S(2)}) %collective-permute-start.19) | collective-permute-done | bytes 786464 | tf_op jit(solution)/shard_map/ppermute | solution.py:108
  142.6 7.0 collective-permute-done.23
  172.3 5.9 collective-permute-done.35
  195.6 8.7 collective-permute-done.26
  207.9 7.6 collective-permute-done.37
  218.1 6.0 collective-permute-done.27
  253.6 8.5 collective-permute-done.47
  266.7 7.1 collective-permute-done.48
  276.0 7.4 collective-permute-done.49
  298.3 6.4 convolution_add_fusion.1
  327.6 88.1 %all-reduce.3.cloned.1.call-done = bf16[2,4,256,512]{3,2,1,0:T(8,128)(2,1)} async-done(((bf16[2,4,256,512]{3,2,1,0:T(8,128)(2,1)}), bf16[2,4,256,512]{3,2,1,0:T(8,128)(2,1)}) %all-reduce.3.cloned.1.call-update) | async-done | bytes 2097168 | tf_op jit(solution)/shard_map/psum | solution.py:347
  431.2 11.3 %collective-permute-done.33 = bf16[128,2048]{1,0:T(8,128)(2,1)S(1)} collective-permute-done((bf16[128,2048]{1,0:T(8,128)(2,1)S(1)}, bf16[128,2048]{1,0:T(8,128)(2,1)S(1)}, u32[]{:S(2)}, u32[]{:S(2)}) %collective-permute-start.33) | collective-permute-done | bytes 524320 | tf_op jit(solution)/shard_map/ppermute | solution.py:204
  445.5 10.7 %collective-permute-done.34 = bf16[128,2048]{1,0:T(8,128)(2,1)S(1)} collective-permute-done((bf16[128,2048]{1,0:T(8,128)(2,1)S(1)}, bf16[128,2048]{1,0:T(8,128)(2,1)S(1)}, u32[]{:S(2)}, u32[]{:S(2)}) %collective-permute-start.34) | collective-permute-done | bytes 524320 | tf_op jit(solution)/shard_map/ppermute | solution.py:204
  460.2 9.7 multiply_convert_fusion.4
  480.0 40.5 %psum.29 = s32[]{:T(128)} all-reduce(s32[]{:T(128)} %get-tuple-element.36), channel_id=1, replica_groups=mesh['dp'=16,'mp'=2] {'dp','mp'}, use_global_device_ids=true, to_apply=%region_12.13 | all-reduce | flops 1 | bytes 8 | tf_op jit(solution)/shard_map/psum | solution.py:265
  528.8 10.8 %collective-permute-done.52 = bf16[128,2048]{1,0:T(8,128)(2,1)S(1)} collective-permute-done((bf16[128,2048]{1,0:T(8,128)(2,1)S(1)}, bf16[128,2048]{1,0:T(8,128)(2,1)S(1)}, u32[]{:S(2)}, u32[]{:S(2)}) %collective-permute-start.52) | collective-permute-done | bytes 524320 | tf_op jit(solution)/shard_map/ppermute | solution.py:204
  555.4 9.9 collective-permute-done.53
  570.5 41.9 %psum.31 = f32[]{:T(128)} all-reduce(f32[]{:T(128)} %get-tuple-element.30), channel_id=1, replica_groups=mesh['dp'=16,'mp'=2] {'dp','mp'}, use_global_device_ids=true, to_apply=%region_22.23 | all-reduce | flops 1 | bytes 8 | tf_op jit(solution)/shard_map/psum | solution.py:378
  678.0 10.3 collective-permute-done.104
  710.8 52.8 %all-reduce.5.cloned.1.call-done = bf16[2,4,256,512]{3,2,1,0:T(8,128)(2,1)} async-done(((bf16[2,4,256,512]{3,2,1,0:T(8,128)(2,1)}), bf16[2,4,256,512]{3,2,1,0:T(8,128)(2,1)}) %all-reduce.5.cloned.1.call-update) | async-done | bytes 2097168 | tf_op jit(solution)/shard_map/psum | solution.py:423
  768.1 5.8 fusion.59
  821.8 20.1 %collective-permute-done.113 = bf16[128,2048]{1,0:T(8,128)(2,1)S(1)} collective-permute-done((bf16[128,2048]{1,0:T(8,128)(2,1)S(1)}, bf16[128,2048]{1,0:T(8,128)(2,1)S(1)}, u32[]{:S(2)}, u32[]{:S(2)}) %collective-permute-start.113) | collective-permute-done | bytes 524320 | tf_op jit(solution)/shard_map/ppermute | solution.py:108
  895.0 7.1 collective-permute-done.87
  916.6 15.5 %collective-permute-done.72 = bf16[128,1024]{1,0:T(8,128)(2,1)S(1)} collective-permute-done((bf16[128,1024]{1,0:T(8,128)(2,1)S(1)}, bf16[128,1024]{1,0:T(8,128)(2,1)S(1)}, u32[]{:S(2)}, u32[]{:S(2)}) %collective-permute-start.72) | collective-permute-done | bytes 262176 | tf_op jit(solution)/shard_map/ppermute | solution.py:108
  954.4 9.4 collective-permute-done.79
  968.8 11.8 %collective-permute-done.88 = bf16[128,2048]{1,0:T(8,128)(2,1)S(1)} collective-permute-done((bf16[128,2048]{1,0:T(8,128)(2,1)S(1)}, bf16[128,2048]{1,0:T(8,128)(2,1)S(1)}, u32[]{:S(2)}, u32[]{:S(2)}) %collective-permute-start.88) | collective-permute-done | bytes 524320 | tf_op jit(solution)/shard_map/ppermute | solution.py:108
  997.9 14.4 %collective-permute-done.70 = bf16[128,1024]{1,0:T(8,128)(2,1)S(1)} collective-permute-done((bf16[128,1024]{1,0:T(8,128)(2,1)S(1)}, bf16[128,1024]{1,0:T(8,128)(2,1)S(1)}, u32[]{:S(2)}, u32[]{:S(2)}) %collective-permute-start.70) | collective-permute-done | bytes 262176 | tf_op jit(solution)/shard_map/ppermute | solution.py:108
  (712 shorter events, 516.8 us)
Async XLA Ops:
  7.2 408.4 %all-reduce.3.cloned.1.call-start = ((), (), s32[]{:S(2)}) async-start(), calls=%async_computation | async-start | bytes 4194304 | tf_op jit(solution)/shard_map/psum | solution.py:347
  15.7 47.6 %collective-permute-start.9 = (bf16[128,3072]{1,0:T(8,128)(2,1)}, bf16[128,3072]{1,0:T(8,128)(2,1)S(1)}, u32[]{:S(2)}, u32[]{:S(2)}) collective-permute-start(bf16[128,3072]{1,0:T(8,128)(2,1)} %get-tuple-element.69), channel_id=1, source_target_pairs={{0,4},{2,6},{8,0},{10,2},{16,8},{18,10},{24,16},{26,18},{28,24},{3... | collective-permute-start | bytes 2359304 | tf_op jit(solution)/shard_map/ppermute | solution.py:108
  17.6 60.2 %collective-permute-start.13 = (bf16[128,3072]{1,0:T(8,128)(2,1)}, bf16[128,3072]{1,0:T(8,128)(2,1)S(1)}, u32[]{:S(2)}, u32[]{:S(2)}) collective-permute-start(bf16[128,3072]{1,0:T(8,128)(2,1)} %get-tuple-element.69), channel_id=1, source_target_pairs={{0,8},{2,10},{8,16},{10,18},{16,24},{18,26},{24,28},{26,30},{28,20... | collective-permute-start | bytes 2359304 | tf_op jit(solution)/shard_map/ppermute | solution.py:108
  19.7 42.6 %collective-permute-start.20 = (bf16[128,3072]{1,0:T(8,128)(2,1)}, bf16[128,3072]{1,0:T(8,128)(2,1)S(1)}, u32[]{:S(2)}, u32[]{:S(2)}) collective-permute-start(bf16[128,3072]{1,0:T(8,128)(2,1)} %get-tuple-element.67), channel_id=1, source_target_pairs={{0,8},{2,10},{8,16},{10,18},{16,24},{18,26},{24,28},{26,30},{28,20... | collective-permute-start | bytes 2359304 | tf_op jit(solution)/shard_map/ppermute | solution.py:108
  76.3 86.7 %collective-permute-start.8 = (bf16[128,2048]{1,0:T(8,128)(2,1)S(1)}, bf16[128,2048]{1,0:T(8,128)(2,1)S(1)}, u32[]{:S(2)}, u32[]{:S(2)}) collective-permute-start(bf16[128,2048]{1,0:T(8,128)(2,1)S(1)} %fusion.34), channel_id=1, source_target_pairs={{0,1},{1,0},{2,3},{3,2},{4,5},{5,4},{6,7},{7,6},{8,9},{9,8},{10,11... | collective-permute-start | bytes 1572872 | tf_op jit(solution)/shard_map/ppermute | solution.py:204
  110.5 48.9 %collective-permute-start.15 = (bf16[128,3072]{1,0:T(8,128)(2,1)S(1)}, bf16[128,3072]{1,0:T(8,128)(2,1)S(1)}, u32[]{:S(2)}, u32[]{:S(2)}) collective-permute-start(bf16[128,3072]{1,0:T(8,128)(2,1)S(1)} %collective-permute-done.14), channel_id=1, source_target_pairs={{0,8},{2,10},{8,16},{10,18},{16,24},{18,26},{24,28},{26,30},{28,20... | collective-permute-start | bytes 2359304 | tf_op jit(solution)/shard_map/ppermute | solution.py:108
  158.5 125.0 %collective-permute-start.24 = (bf16[1024,3072]{1,0:T(8,128)(2,1)}, bf16[1024,3072]{1,0:T(8,128)(2,1)S(1)}, u32[]{:S(2)}, u32[]{:S(2)}) collective-permute-start(bf16[1024,3072]{1,0:T(8,128)(2,1)} %constant_dynamic-update-slice_fusion.30), channel_id=1, source_target_pairs={{0,2},{2,0},{4,6},{6,4},{8,10},{10,8},{12,14},{14,12},{16,18},{18,... | collective-permute-start | bytes 18874376 | tf_op jit(solution)/shard_map/ppermute | solution.py:111
  169.7 125.3 %collective-permute-start.16 = (bf16[1024,3072]{1,0:T(8,128)(2,1)}, bf16[1024,3072]{1,0:T(8,128)(2,1)S(1)}, u32[]{:S(2)}, u32[]{:S(2)}) collective-permute-start(bf16[1024,3072]{1,0:T(8,128)(2,1)} %constant_dynamic-update-slice_fusion.19), channel_id=1, source_target_pairs={{0,2},{2,0},{4,6},{6,4},{8,10},{10,8},{12,14},{14,12},{16,18},{18,... | collective-permute-start | bytes 18874376 | tf_op jit(solution)/shard_map/ppermute | solution.py:111
  253.6 172.0 %collective-permute-start.32 = (bf16[1024,2048]{1,0:T(8,128)(2,1)}, bf16[1024,2048]{1,0:T(8,128)(2,1)}, u32[]{:S(2)}, u32[]{:S(2)}) collective-permute-start(bf16[1024,2048]{1,0:T(8,128)(2,1)} %constant_dynamic-update-slice_fusion.39), channel_id=1, source_target_pairs={{0,2},{2,0},{4,6},{6,4},{8,10},{10,8},{12,14},{14,12},{16,18},{18,... | collective-permute-start | bytes 12582920 | tf_op jit(solution)/shard_map/ppermute | solution.py:111
  275.9 180.4 %collective-permute-start.42 = (bf16[1024,2048]{1,0:T(8,128)(2,1)}, bf16[1024,2048]{1,0:T(8,128)(2,1)}, u32[]{:S(2)}, u32[]{:S(2)}) collective-permute-start(bf16[1024,2048]{1,0:T(8,128)(2,1)} %constant_dynamic-update-slice_fusion.47), channel_id=1, source_target_pairs={{0,2},{2,0},{4,6},{6,4},{8,10},{10,8},{12,14},{14,12},{16,18},{18,... | collective-permute-start | bytes 12582920 | tf_op jit(solution)/shard_map/ppermute | solution.py:111
  315.3 448.2 %all-reduce.5.cloned.1.call-start = ((), (), s32[]{:S(2)}) async-start(), calls=%async_computation.1 | async-start | bytes 4194304 | tf_op jit(solution)/shard_map/psum | solution.py:423
  431.1 41.3 %collective-permute-start.50 = (bf16[1024,2048]{1,0:T(8,128)(2,1)S(1)}, bf16[1024,2048]{1,0:T(8,128)(2,1)S(1)}, u32[]{:S(2)}, u32[]{:S(2)}) collective-permute-start(bf16[1024,2048]{1,0:T(8,128)(2,1)S(1)} %constant_dynamic-update-slice_fusion.55), channel_id=1, source_target_pairs={{0,2},{2,0},{4,6},{6,4},{8,10},{10,8},{12,14},{14,12},{16,18},{18,... | collective-permute-start | bytes 12582920 | tf_op jit(solution)/shard_map/ppermute | solution.py:111
  476.7 46.4 %collective-permute-start.51 = (bf16[128,2048]{1,0:T(8,128)(2,1)S(1)}, bf16[128,2048]{1,0:T(8,128)(2,1)}, u32[]{:S(2)}, u32[]{:S(2)}) collective-permute-start(bf16[128,2048]{1,0:T(8,128)(2,1)S(1)} %fusion.55), channel_id=1, source_target_pairs={{0,1},{1,0},{2,3},{3,2},{4,5},{5,4},{6,7},{7,6},{8,9},{9,8},{10,11... | collective-permute-start | bytes 1572872 | tf_op jit(solution)/shard_map/ppermute | solution.py:204
  554.9 60.5 %collective-permute-start.109 = (bf16[256,2048]{1,0:T(8,128)(2,1)}, bf16[256,2048]{1,0:T(8,128)(2,1)}, u32[]{:S(2)}, u32[]{:S(2)}) collective-permute-start(bf16[256,2048]{1,0:T(8,128)(2,1)} %get-tuple-element.38), channel_id=1, source_target_pairs={{0,2},{2,0},{4,6},{6,4},{8,10},{10,8},{12,14},{14,12},{16,18},{18,... | collective-permute-start | bytes 3145736 | tf_op jit(solution)/shard_map/ppermute | solution.py:111
  555.4 60.1 %collective-permute-start.108 = (bf16[256,1024]{1,0:T(8,128)(2,1)}, bf16[256,1024]{1,0:T(8,128)(2,1)}, u32[]{:S(2)}, u32[]{:S(2)}) collective-permute-start(bf16[256,1024]{1,0:T(8,128)(2,1)} %get-tuple-element.58), channel_id=1, source_target_pairs={{0,2},{2,0},{4,6},{6,4},{8,10},{10,8},{12,14},{14,12},{16,18},{18,... | collective-permute-start | bytes 1572872 | tf_op jit(solution)/shard_map/ppermute | solution.py:111
  568.3 55.5 %collective-permute-start.54 = (bf16[128,2048]{1,0:T(8,128)(2,1)}, bf16[128,2048]{1,0:T(8,128)(2,1)}, u32[]{:S(2)}, u32[]{:S(2)}) collective-permute-start(bf16[128,2048]{1,0:T(8,128)(2,1)} %get-tuple-element.33), channel_id=1, source_target_pairs={{0,1},{1,0},{2,3},{3,2},{4,5},{5,4},{6,7},{7,6},{8,9},{9,8},{10,11... | collective-permute-start | bytes 1572872 | tf_op jit(solution)/shard_map/ppermute | solution.py:204
  569.9 102.9 %collective-permute-start.91 = (bf16[256,2048]{0,1:T(8,128)(2,1)}, bf16[256,2048]{0,1:T(8,128)(2,1)}, u32[]{:S(2)}, u32[]{:S(2)}) collective-permute-start(bf16[256,2048]{0,1:T(8,128)(2,1)} %bitcast.144), channel_id=1, source_target_pairs={{0,2},{2,0},{4,6},{6,4},{8,10},{10,8},{12,14},{14,12},{16,18},{18,... | collective-permute-start | bytes 3145736 | tf_op jit(solution)/shard_map/ppermute | solution.py:111
  570.0 91.9 %collective-permute-start.99 = (bf16[256,1024]{1,0:T(8,128)(2,1)}, bf16[256,1024]{1,0:T(8,128)(2,1)}, u32[]{:S(2)}, u32[]{:S(2)}) collective-permute-start(bf16[256,1024]{1,0:T(8,128)(2,1)} %copy-done.78), channel_id=1, source_target_pairs={{0,2},{2,0},{4,6},{6,4},{8,10},{10,8},{12,14},{14,12},{16,18},{18,... | collective-permute-start | bytes 1572872 | tf_op jit(solution)/shard_map/ppermute | solution.py:111
  615.4 46.7 %collective-permute-start.100 = (bf16[256,2048]{1,0:T(8,128)(2,1)}, bf16[256,2048]{1,0:T(8,128)(2,1)}, u32[]{:S(2)}, u32[]{:S(2)}) collective-permute-start(bf16[256,2048]{1,0:T(8,128)(2,1)} %copy-done.2), channel_id=1, source_target_pairs={{0,2},{2,0},{4,6},{6,4},{8,10},{10,8},{12,14},{14,12},{16,18},{18,... | collective-permute-start | bytes 3145736 | tf_op jit(solution)/shard_map/ppermute | solution.py:111
  618.5 45.8 %collective-permute-start.114 = (bf16[128,2048]{1,0:T(8,128)(2,1)}, bf16[128,2048]{1,0:T(8,128)(2,1)}, u32[]{:S(2)}, u32[]{:S(2)}) collective-permute-start(bf16[128,2048]{1,0:T(8,128)(2,1)} %convolution_convert_fusion.2), channel_id=1, source_target_pairs={{0,4},{2,6},{8,0},{10,2},{16,8},{18,10},{24,16},{26,18},{28,24},{3... | collective-permute-start | bytes 1572872 | tf_op jit(solution)/shard_map/ppermute | solution.py:108
  623.8 46.7 %collective-permute-start.110 = (bf16[128,2048]{1,0:T(8,128)(2,1)}, bf16[128,2048]{1,0:T(8,128)(2,1)}, u32[]{:S(2)}, u32[]{:S(2)}) collective-permute-start(bf16[128,2048]{1,0:T(8,128)(2,1)} %convolution_convert_fusion.3), channel_id=1, source_target_pairs={{0,8},{2,10},{8,16},{10,18},{16,24},{18,26},{24,28},{26,30},{28,20... | collective-permute-start | bytes 1572872 | tf_op jit(solution)/shard_map/ppermute | solution.py:108
  662.1 140.7 %collective-permute-start.82 = (bf16[256,2048]{1,0:T(8,128)(2,1)S(1)}, bf16[256,2048]{1,0:T(8,128)(2,1)}, u32[]{:S(2)}, u32[]{:S(2)}) collective-permute-start(bf16[256,2048]{1,0:T(8,128)(2,1)S(1)} %fusion.8), channel_id=1, source_target_pairs={{0,2},{2,0},{4,6},{6,4},{8,10},{10,8},{12,14},{14,12},{16,18},{18,... | collective-permute-start | bytes 3145736 | tf_op jit(solution)/shard_map/ppermute | solution.py:111
  688.3 102.3 %collective-permute-start.96 = (bf16[128,2048]{1,0:T(8,128)(2,1)}, bf16[128,2048]{1,0:T(8,128)(2,1)}, u32[]{:S(2)}, u32[]{:S(2)}) collective-permute-start(bf16[128,2048]{1,0:T(8,128)(2,1)} %convolution_convert_fusion.6), channel_id=1, source_target_pairs={{0,4},{2,6},{8,0},{10,2},{16,8},{18,10},{24,16},{26,18},{28,24},{3... | collective-permute-start | bytes 1572872 | tf_op jit(solution)/shard_map/ppermute | solution.py:108
  694.3 100.4 %collective-permute-start.92 = (bf16[128,2048]{1,0:T(8,128)(2,1)}, bf16[128,2048]{1,0:T(8,128)(2,1)}, u32[]{:S(2)}, u32[]{:S(2)}) collective-permute-start(bf16[128,2048]{1,0:T(8,128)(2,1)} %convolution_convert_fusion.7), channel_id=1, source_target_pairs={{0,8},{2,10},{8,16},{10,18},{16,24},{18,26},{24,28},{26,30},{28,20... | collective-permute-start | bytes 1572872 | tf_op jit(solution)/shard_map/ppermute | solution.py:108
  703.0 97.0 %collective-permute-start.105 = (bf16[128,2048]{1,0:T(8,128)(2,1)}, bf16[128,2048]{1,0:T(8,128)(2,1)}, u32[]{:S(2)}, u32[]{:S(2)}) collective-permute-start(bf16[128,2048]{1,0:T(8,128)(2,1)} %add_convert_fusion.13), channel_id=1, source_target_pairs={{0,4},{2,6},{8,0},{10,2},{16,8},{18,10},{24,16},{26,18},{28,24},{3... | collective-permute-start | bytes 1572872 | tf_op jit(solution)/shard_map/ppermute | solution.py:108
  705.9 102.0 %collective-permute-start.102 = (bf16[128,2048]{1,0:T(8,128)(2,1)}, bf16[128,2048]{1,0:T(8,128)(2,1)}, u32[]{:S(2)}, u32[]{:S(2)}) collective-permute-start(bf16[128,2048]{1,0:T(8,128)(2,1)} %add_convert_fusion.15), channel_id=1, source_target_pairs={{0,8},{2,10},{8,16},{10,18},{16,24},{18,26},{24,28},{26,30},{28,20... | collective-permute-start | bytes 1572872 | tf_op jit(solution)/shard_map/ppermute | solution.py:108
  807.9 96.0 %collective-permute-start.74 = (bf16[256,3072]{0,1:T(8,128)(2,1)}, bf16[256,3072]{0,1:T(8,128)(2,1)}, u32[]{:S(2)}, u32[]{:S(2)}) collective-permute-start(bf16[256,3072]{0,1:T(8,128)(2,1)} %pad_maximum_fusion.6), channel_id=1, source_target_pairs={{0,2},{2,0},{4,6},{6,4},{8,10},{10,8},{12,14},{14,12},{16,18},{18,... | collective-permute-start | bytes 4718600 | tf_op jit(solution)/shard_map/ppermute | solution.py:111
  810.9 39.6 %collective-permute-start.86 = (bf16[128,2048]{1,0:T(8,128)(2,1)S(1)}, bf16[128,2048]{1,0:T(8,128)(2,1)S(1)}, u32[]{:S(2)}, u32[]{:S(2)}) collective-permute-start(bf16[128,2048]{1,0:T(8,128)(2,1)S(1)} %convolution_convert_fusion.8), channel_id=1, source_target_pairs={{0,4},{2,6},{8,0},{10,2},{16,8},{18,10},{24,16},{26,18},{28,24},{3... | collective-permute-start | bytes 1572872 | tf_op jit(solution)/shard_map/ppermute | solution.py:108
  820.4 42.4 %collective-permute-start.97 = (bf16[128,2048]{1,0:T(8,128)(2,1)S(1)}, bf16[128,2048]{1,0:T(8,128)(2,1)S(1)}, u32[]{:S(2)}, u32[]{:S(2)}) collective-permute-start(bf16[128,2048]{1,0:T(8,128)(2,1)S(1)} %add_convert_fusion.17), channel_id=1, source_target_pairs={{0,4},{2,6},{8,0},{10,2},{16,8},{18,10},{24,16},{26,18},{28,24},{3... | collective-permute-start | bytes 1572872 | tf_op jit(solution)/shard_map/ppermute | solution.py:108
  866.3 76.6 %collective-permute-start.103 = (bf16[128,2048]{1,0:T(8,128)(2,1)}, bf16[128,2048]{1,0:T(8,128)(2,1)}, u32[]{:S(2)}, u32[]{:S(2)}) collective-permute-start(bf16[128,2048]{1,0:T(8,128)(2,1)} %add_convert_fusion.14), channel_id=1, source_target_pairs={{0,8},{2,10},{8,16},{10,18},{16,24},{18,26},{24,28},{26,30},{28,20... | collective-permute-start | bytes 1572872 | tf_op jit(solution)/shard_map/ppermute | solution.py:108
  894.0 101.9 %collective-permute-start.98 = (bf16[128,2048]{1,0:T(8,128)(2,1)S(1)}, bf16[128,2048]{1,0:T(8,128)(2,1)S(1)}, u32[]{:S(2)}, u32[]{:S(2)}) collective-permute-start(bf16[128,2048]{1,0:T(8,128)(2,1)S(1)} %copy-done.125), channel_id=1, source_target_pairs={{0,4},{2,6},{8,0},{10,2},{16,8},{18,10},{24,16},{26,18},{28,24},{3... | collective-permute-start | bytes 1572872 | tf_op jit(solution)/shard_map/ppermute | solution.py:108
  942.9 53.0 %collective-permute-start.73 = (bf16[128,1024]{1,0:T(8,128)(2,1)S(1)}, bf16[128,1024]{1,0:T(8,128)(2,1)S(1)}, u32[]{:S(2)}, u32[]{:S(2)}) collective-permute-start(bf16[128,1024]{1,0:T(8,128)(2,1)S(1)} %add_convert_fusion.27), channel_id=1, source_target_pairs={{0,4},{2,6},{8,0},{10,2},{16,8},{18,10},{24,16},{26,18},{28,24},{3... | collective-permute-start | bytes 786440 | tf_op jit(solution)/shard_map/ppermute | solution.py:108
  (222 other events, 3481.3 us)
Sparse Core Ops, SparseCore 0:
  315.5 100.1 all-reduce.2
  659.1 104.4 all-reduce.4

commit v2 on v1

--- a/solution.py
+++ b/solution.py
@@ -118,52 +118,264 @@
         chip = jnp.where(spot < self.chips // 2, 2 * spot, 2 * (self.chips - 1 - spot) + 1)
         return jnp.concatenate([chip * 2 + self.core, chip * 2 + 1 - self.core]).astype(jnp.int32)
 
-    def gather(self, shard, flip):
-        up, down = self.hops(flip)
-        pieces = [None] * self.chips
-        pieces[0] = shard
-        moving_up, moving_down = shard, shard
-        for step in range(1, max(up, down) + 1):
-            if step <= up:
-                moving_up = self.shift(moving_up, 1)
-                pieces[self.chips - step] = moving_up
-            if step <= down:
-                moving_down = self.shift(moving_down, -1)
-                pieces[step] = moving_down
-        return pieces
-
-    def reduce(self, term, flip):
-        up, down = self.hops(flip)
-        moving_up = term(up).astype(jnp.bfloat16)
-        moving_down = term(self.chips - down).astype(jnp.bfloat16)
-        for step in range(1, max(up, down) + 1):
-            if step <= up:
-                moving_up = self.shift(moving_up, 1)
-                if step < up:
-                    moving_up = (moving_up.astype(jnp.float32) + term(up - step)).astype(
-                        jnp.bfloat16
-                    )
-            if step <= down:
-                moving_down = self.shift(moving_down, -1)
-                if step < down:
-                    moving_down = (
-                        moving_down.astype(jnp.float32) + term(self.chips - down + step)
-                    ).astype(jnp.bfloat16)
-        return term(0) + moving_up.astype(jnp.float32) + moving_down.astype(jnp.float32)
-
-    def reduce_exact(self, parts, flip):
-        up, down = self.hops(flip)
-        moving_up, moving_down = parts(up), parts(self.chips - down)
-        for step in range(1, max(up, down) + 1):
-            if step <= up:
-                moving_up = self.shift(moving_up, 1)
-                if step < up:
-                    moving_up = moving_up + parts(up - step)
-            if step <= down:
-                moving_down = self.shift(moving_down, -1)
-                if step < down:
-                    moving_down = moving_down + parts(self.chips - down + step)
-        return parts(0) + moving_up + moving_down
+
+class RingSum:
+    def __init__(self, ring, full, flip):
+        self.ring = ring
+        self.full = full
+        self.block = full.shape[0] // ring.chips
+        self.up, self.down = ring.hops(flip)
+        self.moving = [self.term(self.up), self.term(ring.chips - self.down)]
+        self.count = 0
+
+    def term(self, k):
+        return self.full[k * self.block : (k + 1) * self.block]
+
+    def step(self):
+        ring = self.ring
+        self.count += 1
+        for way, hops, k in (
+            (0, self.up, self.up - self.count),
+            (1, self.down, ring.chips - self.down + self.count),
+        ):
+            if self.count <= hops:
+                moved = ring.shift(self.moving[way], 1 - 2 * way)
+                if self.count < hops:
+                    moved = moved.astype(jnp.float32) + self.term(k).astype(jnp.float32)
+                    moved = moved.astype(jnp.bfloat16)
+                self.moving[way] = moved
+
+    def run(self, steps):
+        for _ in range(min(steps, max(self.up, self.down) - self.count)):
+            self.step()
+
+    def result(self):
+        self.run(self.ring.chips)
+        return (
+            self.term(0).astype(jnp.float32)
+            + self.moving[0].astype(jnp.float32)
+            + self.moving[1].astype(jnp.float32)
+        )
+
+
+def gather_ring(shards, call_id=1):
+    devices = lax.axis_size("dp")
+    chips = devices // 2
+    half = chips // 2
+    rows = shards[0].shape[0]
+    count = len(shards)
+    parts = 2
+    piece = rows // parts
+    hops = ((half, half - 1), (half - 1, half))
+
+    def kernel(*refs):
+        ins, outs = refs[:count], refs[count : 2 * count]
+        own_sem, side_send, side_recv, ring_send, ring_recv = refs[2 * count :]
+        index = lax.axis_index("dp")
+        core, chip = index % 2, index // 2
+        odd = chip % 2
+        place = (1 - odd) * (chip // 2) + odd * (chips - 1 - chip // 2)
+
+        def device_at(spot, which):
+            spot = (spot + 2 * chips) % chips
+            upper = spot // half
+            there = (1 - upper) * (2 * spot) + upper * (2 * (chips - 1 - spot) + 1)
+            return there * 2 + which
+
+        def window(spot, which, part):
+            first = device_at(spot, which) * rows + part * piece
+            return pl.ds(pl.multiple_of(first, piece), piece)
+
+        partner = chip * 2 + 1 - core
+        neighbours = (device_at(place + 1, core), device_at(place - 1, core))
+
+        barrier = pltpu.get_barrier_semaphore()
+        for target in (*neighbours, partner):
+            pl.semaphore_signal(
+                barrier, inc=1, device_id={"dp": target}, device_id_type=pl.DeviceIdType.MESH
+            )
+        pl.semaphore_wait(barrier, 3)
+
+        sends = []
+
+        def source(j, spot, part, own):
+            if own:
+                return ins[j].at[pl.ds(part * piece, piece)]
+            return outs[j].at[window(spot, core, part)]
+
+        def ring_copy(j, way, part, hop):
+            spot = place - (hop - 1) * (1 - 2 * way)
+            return pltpu.make_async_remote_copy(
+                src_ref=source(j, spot, part, hop == 1),
+                dst_ref=outs[j].at[window(spot, core, part)],
+                send_sem=ring_send.at[j, way, part, hop - 1],
+                recv_sem=ring_recv.at[j, way, part, hop - 1],
+                device_id={"dp": neighbours[way]},
+                device_id_type=pl.DeviceIdType.MESH,
+            )
+
+        def ring_arrival(j, way, part, hop):
+            spot = place - hop * (1 - 2 * way)
+            here = outs[j].at[window(spot, core, part)]
+            return pltpu.make_async_remote_copy(
+                src_ref=here,
+                dst_ref=here,
+                send_sem=ring_send.at[j, way, part, hop - 1],
+                recv_sem=ring_recv.at[j, way, part, hop - 1],
+                device_id={"dp": neighbours[way]},
+                device_id_type=pl.DeviceIdType.MESH,
+            )
+
+        def side_copy(j, part, slot, spot, own):
+            return pltpu.make_async_remote_copy(
+                src_ref=source(j, spot, part, own),
+                dst_ref=outs[j].at[window(spot, core, part)],
+                send_sem=side_send.at[j, part, slot],
+                recv_sem=side_recv.at[j, part, slot],
+                device_id={"dp": partner},
+                device_id_type=pl.DeviceIdType.MESH,
+            )
+
+        def side_arrival(j, part, slot, spot):
+            here = outs[j].at[window(spot, 1 - core, part)]
+            return pltpu.make_async_remote_copy(
+                src_ref=here,
+                dst_ref=here,
+                send_sem=side_send.at[j, part, slot],
+                recv_sem=side_recv.at[j, part, slot],
+                device_id={"dp": partner},
+                device_id_type=pl.DeviceIdType.MESH,
+            )
+
+        def launch(copy):
+            copy.start()
+            sends.append(copy)
+
+        for part in range(parts):
+            for j in range(count):
+                for way in range(2):
+                    launch(ring_copy(j, way, part, 1))
+        owns = []
+        for part in range(parts):
+            for j in range(count):
+                launch(side_copy(j, part, 0, place, True))
+                own = pltpu.make_async_copy(
+                    source(j, place, part, True),
+                    outs[j].at[window(place, core, part)],
+                    own_sem.at[j, part],
+                )
+                own.start()
+                owns.append(own)
+        for hop in range(1, half + 1):
+            for part in range(parts):
+                for j in range(count):
+                    for way in range(2):
+                        if hop <= hops[way][part]:
+                            ring_arrival(j, way, part, hop).wait_recv()
+                            if hop < hops[way][part]:
+                                launch(ring_copy(j, way, part, hop + 1))
+                            turn = 1 - 2 * way
+                            slot = (chips - hop * turn) % chips
+                            launch(side_copy(j, part, slot, place - hop * turn, False))
+        for own in owns:
+            own.wait()
+        for copy in sends:
+            copy.wait_send()
+        for slot in range(chips):
+            for part in range(parts):
+                for j in range(count):
+                    side_arrival(j, part, slot, place + slot).wait_recv()
+
+    total = sum(shard.shape[1] for shard in shards) * rows * 2
+    return pl.pallas_call(
+        kernel,
+        out_shape=[
+            jax.ShapeDtypeStruct((devices * rows, shard.shape[1]), shard.dtype) for shard in shards
+        ],
+        in_specs=[pl.BlockSpec(memory_space=pl.ANY)] * count,
+        out_specs=[pl.BlockSpec(memory_space=pl.ANY)] * count,
+        scratch_shapes=[
+            pltpu.SemaphoreType.DMA((count, parts)),
+            pltpu.SemaphoreType.DMA((count, parts, chips)),
+            pltpu.SemaphoreType.DMA((count, parts, chips)),
+            pltpu.SemaphoreType.DMA((count, 2, parts, half)),
+            pltpu.SemaphoreType.DMA((count, 2, parts, half)),
+        ],
+        compiler_params=pltpu.CompilerParams(collective_id=call_id, has_side_effects=True),
+        cost_estimate=pl.CostEstimate(
+            flops=0, bytes_accessed=total * devices * 4, transcendentals=0
+        ),
+    )(*shards)
+
+
+def exchange_blocks(blocks):
+    dp_size, mp_size = lax.axis_size("dp"), lax.axis_size("mp")
+    total = dp_size * mp_size
+
+    def kernel(in_ref, out_ref, send_sem, recv_sem):
+        dp_index = lax.axis_index("dp")
+        me = dp_index * mp_size + lax.axis_index("mp")
+
+        def place(offset):
+            target = (me + offset) % total
+            return target // mp_size, target % mp_size
+
+        barrier = pltpu.get_barrier_semaphore()
+
+        def greet(offset, carry):
+            row, col = place(offset)
+            pl.semaphore_signal(
+                barrier, inc=1, device_id=(row, col), device_id_type=pl.DeviceIdType.MESH
+            )
+            return carry
+
+        lax.fori_loop(1, total, greet, 0)
+        pl.semaphore_wait(barrier, total - 1)
+
+        def send(offset):
+            row, col = place(offset)
+            return pltpu.make_async_remote_copy(
+                src_ref=in_ref.at[row],
+                dst_ref=out_ref.at[me],
+                send_sem=send_sem.at[offset],
+                recv_sem=recv_sem.at[offset],
+                device_id=(row, col),
+                device_id_type=pl.DeviceIdType.MESH,
+            )
+
+        def begin(offset, carry):
+            send(offset).start()
+            return carry
+
+        lax.fori_loop(1, total, begin, 0)
+        out_ref[me] = in_ref[dp_index]
+
+        def finish(offset, carry):
+            sender = (me + total - offset) % total
+            send(offset).wait_send()
+            pltpu.make_async_remote_copy(
+                src_ref=out_ref.at[sender],
+                dst_ref=out_ref.at[sender],
+                send_sem=send_sem.at[offset],
+                recv_sem=recv_sem.at[offset],
+                device_id=place(offset),
+                device_id_type=pl.DeviceIdType.MESH,
+            ).wait_recv()
+            return carry
+
+        lax.fori_loop(1, total, finish, 0)
+
+    return pl.pallas_call(
+        kernel,
+        out_shape=jax.ShapeDtypeStruct((total, *blocks.shape[1:]), blocks.dtype),
+        in_specs=[pl.BlockSpec(memory_space=pltpu.VMEM)],
+        out_specs=pl.BlockSpec(memory_space=pltpu.VMEM),
+        scratch_shapes=[
+            pltpu.SemaphoreType.DMA((total,)),
+            pltpu.SemaphoreType.DMA((total,)),
+        ],
+        compiler_params=pltpu.CompilerParams(collective_id=2, has_side_effects=True),
+    )(blocks)
 
 
 def move_blocks(rows, table, outward):
@@ -262,39 +474,26 @@
     loss_mask = valid_mask[0].astype(jnp.float32) * jnp.where(
         prompt_flag > 0, own_ids < prompt_size, True
     ).astype(jnp.float32)
-    valid_count = lax.psum(jnp.sum(loss_mask.astype(jnp.int32)), ("dp", "mp")).astype(jnp.float32)
-
-    vectors = jnp.stack([ln1_gain, ln1_bias, ln2_gain, ln2_bias])
-    vector_own = jnp.concatenate(ring.gather(vectors, False), axis=1)
-    vectors_full = jnp.concatenate([vector_own, ring.swap(vector_own)], axis=1).astype(jnp.float32)
-    gain_one, bias_one, gain_two, bias_two = (vectors_full[i] for i in range(4))
-
-    groups = [
-        jnp.concatenate([w_key, w_value], axis=1),
-        jnp.concatenate([w_query, w_gate], axis=1),
-        w_out,
-        w_up,
-        w_down,
-    ]
-    gathered = []
-    for i, shard in enumerate(groups):
-        if i >= 2:
-            shard = tie(shard, gathered[i - 2][0][ring.chips // 2])
-        pieces = ring.gather(shard, i % 2 == 1)
-        own = jnp.concatenate(pieces, axis=0)
-        gathered.append((pieces, own, ring.swap(own)))
-    full = [(own, other) for _, own, other in gathered]
-
-    def times_full(rows, weight):
-        return plain_dot(rows[:, :own_width], weight[0]) + plain_dot(rows[:, own_width:], weight[1])
-
-    def times_full_t(rows, weight):
-        return jnp.concatenate(
-            [contract_last(rows, weight[0]), contract_last(rows, weight[1])], axis=1
-        )
-
-    key_width = w_key.shape[1]
-    wkv, wqg, wo_full, wu_full, wd_full = full
+    block = model_dim // ring.devices
+
+    def packed(rows, scalar):
+        split = rows.reshape(rows.shape[0], -1, block).transpose(1, 0, 2)
+        split = jnp.pad(split, ((0, 0), (0, 0), (0, 128 - block)))
+        extra = jnp.broadcast_to(scalar, (split.shape[0], 8 - rows.shape[0], 128))
+        return jnp.concatenate([split, extra], axis=1)
+
+    vectors = jnp.stack([ln1_gain, ln1_bias, ln2_gain, ln2_bias]).astype(jnp.float32)
+    from_all = exchange_blocks(
+        packed(jnp.tile(vectors, (1, ring.devices)), jnp.sum(loss_mask))
+    )
+    valid_count = jnp.sum(from_all[:, 4, 0])
+    by_row = from_all.reshape(ring.devices, -1, 8, 128)[:, 0, :4, :block]
+    gain_one, bias_one, gain_two, bias_two = (
+        by_row[:, i].reshape(1, model_dim) for i in range(4)
+    )
+
+    def gather_all(shard):
+        return lax.all_gather(shard, "dp", axis=0, tiled=True)
 
     offset = jnp.where(prompt_flag > 0, 0, prompt_size)
     positions = (token_ids + offset).astype(jnp.float32)
@@ -319,18 +518,16 @@
         jnp.exp(log_decay[:, None, None] * jnp.maximum(distance, 0.0)[None]),
         0.0,
     )
-    token_rows = move_blocks(tokens_in, table, False).astype(jnp.float32)
-    teacher_rows = move_blocks(teacher, table, False).astype(jnp.float32)
+    token_rows = tokens_in.astype(jnp.float32)
+    teacher_rows = teacher.astype(jnp.float32)
     normed_one, inv_one = norm_stats(token_rows, EPSILON)
-    a_all = gather_rows((normed_one * gain_one + bias_one).astype(jnp.bfloat16))
-    key_value = times_full(a_all, wkv)
-    keys_raw = key_value[:, :key_width].reshape(seg_len, heads_local, DK)
+    a_own = (normed_one * gain_one + bias_one).astype(jnp.bfloat16)
+    a_all = gather_rows(a_own)
+    wk_full, wv_full = gather_ring([tie(w_key, a_own), w_value])
+    keys_raw = plain_dot(a_all, wk_full).reshape(seg_len, heads_local, DK)
     reduced_values = (
-        key_value[:, key_width:].astype(jnp.bfloat16).reshape(seg_len, heads_local, DV)
-    )
-    query_gate = times_full(a_all, wqg)
-    queries = query_gate[:, :key_width].reshape(seg_len, heads_local, DK)
-    gate_pre = query_gate[:, key_width:]
+        plain_dot(a_all, wv_full).astype(jnp.bfloat16).reshape(seg_len, heads_local, DV)
+    )
     cosine, sine_tab, grow_fac = xpos_tables(positions, 1.0)
     _, _, shrink = xpos_tables(positions, -1.0)
     q_scale = DK ** (-0.5)
@@ -345,9 +542,15 @@
         jnp.bfloat16
     )
     summed = lax.psum(slots, "dp")
+    wq_full, wg_full = gather_ring([tie(w_query, slots), w_gate])
+    both_ffn = gather_all(jnp.concatenate([w_up, tie(w_down, wq_full[:8])], axis=1))
+    wu_full, wd_full = both_ffn[:, : w_up.shape[1]], both_ffn[:, w_up.shape[1] :]
+    (wo_full,) = gather_ring([tie(w_out, wq_full[:8])], 3)
     state_lookup = jnp.sum(
         summed.astype(jnp.float32) * group_onehot[:, None, None, None], axis=0
     ).astype(jnp.bfloat16)
+    queries = plain_dot(a_all, wq_full).reshape(seg_len, heads_local, DK)
+    gate_pre = plain_dot(a_all, wg_full)
     rotated_queries = (rotate_pairs(queries, cosine, sine_tab, grow_fac) * q_scale).astype(
         jnp.bfloat16
     )
@@ -365,51 +568,58 @@
     grouped, inv_group = norm_stats(retained_output, GROUP_EPSILON)
     gate_act = jax.nn.silu(gate_pre).reshape(seg_len, heads_local, DV)
     gated_out = (gate_act * grouped).reshape(seg_len, heads_local * DV).astype(jnp.bfloat16)
-    attn_own = scatter_rows(times_full_t(gated_out, wo_full))
+    attn_own = scatter_rows(contract_last(gated_out, wo_full))
     hidden_res = token_rows + attn_own
     normed_two, inv_two = norm_stats(hidden_res, EPSILON)
     c_all = gather_rows((normed_two * gain_two + bias_two).astype(jnp.bfloat16))
-    up_pre = times_full(c_all, wu_full)
+    up_pre = plain_dot(c_all, wu_full)
     up_act = jax.nn.gelu(up_pre, approximate=False).astype(jnp.bfloat16)
-    ffn_own = scatter_rows(times_full_t(up_act, wd_full))
+    ffn_own = scatter_rows(contract_last(up_act, wd_full))
     block_out = hidden_res + ffn_own
     error_rows = block_out - teacher_rows
     weighted = loss_mask[:, None] * error_rows
-    squared = lax.psum(jnp.sum(weighted * error_rows), ("dp", "mp"))
+    squared_own = jnp.sum(weighted * error_rows)
     grad_out = token_total / valid_count * weighted
-    loss_value = squared / (valid_count * model_dim)
-
-    block = model_dim // ring.devices
 
     def weight_grad(feature_side, other_side, flip):
         mine = jnp.concatenate(
             [feature_side[:, :own_width], ring.swap(feature_side[:, own_width:])], axis=0
         )
         both = jnp.concatenate([other_side, ring.swap(other_side)], axis=0)
-
-        def term(k):
-            return contract_first(mine[:, k * block : (k + 1) * block], both)
-
-        return ring.reduce(term, flip)
+        return RingSum(ring, contract_first(mine, both).astype(jnp.bfloat16), flip)
+
+    def in_order(rows):
+        return move_blocks(rows, table, False)
+
+    def then(value, *ring_sums):
+        return tie(value, tuple(r.moving[way] for r in ring_sums for way in range(2)))
 
     grad_ffn_all = gather_rows(grad_out.astype(jnp.bfloat16))
-    grad_wd = weight_grad(grad_ffn_all, up_act, False)
-    grad_up_act = times_full(grad_ffn_all, wd_full)
+    sum_wd = weight_grad(in_order(grad_ffn_all), up_act, False)
+    grad_up_act = plain_dot(tie(grad_ffn_all, sum_wd.full[:16, :128]), wd_full)
     _, gelu_pull = jax.vjp(lambda inner: jax.nn.gelu(inner, approximate=False), up_pre)
     grad_up = gelu_pull(grad_up_act)[0].astype(jnp.bfloat16)
-    grad_wu = weight_grad(c_all, grad_up, True)
-    grad_c = scatter_rows(times_full_t(grad_up, wu_full))
+    sum_wu = weight_grad(in_order(c_all), grad_up, True)
+    sum_wd.run(1)
+    grad_up = tie(then(grad_up, sum_wd), sum_wu.full[:16, :128])
+    grad_c_parts = contract_last(grad_up, wu_full)
+    grad_c = scatter_rows(grad_c_parts)
+    sum_wd.run(1)
+    grad_c = then(grad_c, sum_wd)
     grad_gain2_part = jnp.sum(grad_c * normed_two, axis=0)
     grad_bias2_part = jnp.sum(grad_c, axis=0)
     grad_hidden = grad_out + norm_back(grad_c * gain_two, normed_two, inv_two)
     grad_attn_all = gather_rows(grad_hidden.astype(jnp.bfloat16))
-    grad_wo = weight_grad(grad_attn_all, gated_out, False)
-    grad_gated = times_full(grad_attn_all, wo_full).reshape(seg_len, heads_local, DV)
+    sum_wd.run(2)
+    sum_wu.run(1)
+    grad_attn_all = then(grad_attn_all, sum_wd, sum_wu)
+    sum_wo = weight_grad(in_order(grad_attn_all), gated_out, False)
+    grad_attn_all = tie(grad_attn_all, sum_wo.full[:16, :128])
+    grad_gated = plain_dot(grad_attn_all, wo_full).reshape(seg_len, heads_local, DV)
     _, silu_pull = jax.vjp(jax.nn.silu, gate_pre)
     grad_gate = silu_pull((grad_gated * grouped).reshape(seg_len, heads_local * DV))[0].astype(
         jnp.bfloat16
     )
-    grad_wg = weight_grad(a_all, grad_gate, True)
     retained_gradient = norm_back(grad_gated * gate_act, grouped, inv_group).astype(jnp.bfloat16)
     state_grad_own = jnp.einsum(
         "ybn,ybw->bnw",
@@ -421,13 +631,21 @@
     )
     grad_slots = (group_onehot[:, None, None, None] * state_grad_own[None]).astype(jnp.bfloat16)
     grad_summed = lax.psum(grad_slots, "dp")
+    sum_wu.run(2)
+    a_order = in_order(a_all)
+    grad_gate = tie(then(grad_gate, sum_wu), grad_slots[:, :, :8, :128])
+    sum_wg = weight_grad(a_order, grad_gate, True)
+    retained_gradient = tie(retained_gradient, sum_wg.full[:16, :128])
+    sum_wu.run(1)
+    sum_wo.run(1)
     grad_weights = jnp.einsum(
         "thv,nhv->htn", retained_gradient, reduced_values, preferred_element_type=jnp.float32
     )
     grad_values = jnp.einsum(
         "htn,thv->nhv", weights_low, retained_gradient, preferred_element_type=jnp.float32
     )
-    grad_scores = (grad_weights * decay_mat).astype(jnp.bfloat16)
+    grad_scores = then((grad_weights * decay_mat).astype(jnp.bfloat16), sum_wu, sum_wo)
+    sum_wo.run(1)
     grad_q_rot = jnp.einsum(
         "htn,nhk->thk", grad_scores, rotated_keys, preferred_element_type=jnp.float32
     )
@@ -442,7 +660,11 @@
         .reshape(seg_len, heads_local * DK)
         .astype(jnp.bfloat16)
     )
-    grad_wq = weight_grad(a_all, grad_queries, False)
+    grad_queries = then(grad_queries, sum_wo)
+    sum_wq = weight_grad(a_order, grad_queries, False)
+    sum_wo.run(2)
+    sum_wg.run(2)
+    grad_summed = tie(then(grad_summed, sum_wo, sum_wg), sum_wq.full[:16, :128])
     state_gradient = (
         prompt_flag
         * jnp.sum(grad_summed.astype(jnp.float32) * group_onehot[:, None, None, None], axis=0)
@@ -460,35 +682,45 @@
     )
     grad_vlow = grad_values.reshape(seg_len, heads_local * DV).astype(jnp.bfloat16)
     grad_key_value = jnp.concatenate([grad_keys, grad_vlow], axis=1)
-    grad_wkv = weight_grad(a_all, grad_key_value, True)
-    grad_query_gate = jnp.concatenate([grad_queries, grad_gate], axis=1)
+    sum_wg.run(1)
+    grad_key_value = then(grad_key_value, sum_wg)
+    sum_wkv = weight_grad(a_order, grad_key_value, True)
+    grad_queries, grad_keys = (tie(x, sum_wkv.full[:16, :128]) for x in (grad_queries, grad_keys))
     grad_a = scatter_rows(
-        times_full_t(grad_query_gate, wqg) + times_full_t(grad_key_value, wkv)
-    )
+        contract_last(grad_queries, wq_full)
+        + contract_last(grad_gate, wg_full)
+        + contract_last(grad_keys, wk_full)
+        + contract_last(grad_vlow, wv_full)
+    )
+    sum_wg.run(1)
+    sum_wq.run(2)
+    sum_wkv.run(1)
+    grad_a = then(grad_a, sum_wg, sum_wq, sum_wkv)
     grad_gain1_part = jnp.sum(grad_a * normed_one, axis=0)
     grad_bias1_part = jnp.sum(grad_a, axis=0)
     grad_tokens = grad_hidden + norm_back(grad_a * gain_one, normed_one, inv_one)
 
     sums = jnp.stack([grad_gain1_part, grad_bias1_part, grad_gain2_part, grad_bias2_part])
-    sums = sums + swap_mp(sums)
-    sums = sums[:, :own_width] + ring.swap(sums[:, own_width:])
-    sums = ring.reduce_exact(lambda k: sums[:, k * block : (k + 1) * block], False)
+    totals = jnp.sum(exchange_blocks(packed(sums, squared_own)), axis=0)
+    loss_value = totals[4, 0] / (valid_count * model_dim)
+    key_width = w_key.shape[1]
+    grad_wkv = sum_wkv.result()
 
     return (
-        move_blocks(block_out, table, True),
-        move_blocks(grad_tokens, table, True),
+        block_out,
+        grad_tokens,
         loss_value,
-        sums[0],
-        sums[1],
-        grad_wq,
+        totals[0, :block],
+        totals[1, :block],
+        sum_wq.result(),
         grad_wkv[:, :key_width],
         grad_wkv[:, key_width:],
-        grad_wg,
-        grad_wo,
-        sums[2],
-        sums[3],
-        grad_wu,
-        grad_wd,
+        sum_wg.result(),
+        sum_wo.result(),
+        totals[2, :block],
+        totals[3, :block],
+        sum_wu.result(),
+        sum_wd.result(),
     )
 
 

time: 1050 us -> 884 us (0.84)
  Pallas kernels: 8.69 us -> 270 us
  waiting for transfers between devices: 482 us -> 276 us
  matrix products: 203 us -> 112 us
  blocking collectives: 82.4 us -> 0 us
  starting transfers between devices: 118 us -> 57.7 us
  other arithmetic: 55.7 us -> 93.2 us
  local copies, waits for them, and re-layouts: 66.7 us -> 45 us
    pallas_call x0 -> x5, Pallas kernels: none -> 260 us  [the longest x3 232 us: gather_ring(): pl.pallas_call(kernel, out_shape=[jax.ShapeDtypeStruct((devices * rows, s...]
    ppermute x91 -> x42, waiting for transfers between devices: 295 us -> 137 us  [shift(): return lax.ppermute(rows, 'dp', pairs)]
    psum x1, waiting for transfers between devices: 88.1 us -> 0.01 us  [on_device(): summed = lax.psum(slots, 'dp')]
    psum x2 -> x0, blocking collectives: 82.4 us -> none  [the longest x1 41.9 us: on_device(): squared = lax.psum(jnp.sum(weighted * error_rows), ('dp', 'mp'))]
    dot_general x48 -> x6, matrix products: 102 us -> 23.3 us  [contract_first(): lax.dot_general(first_op, second_op, (((0,), (0,)), ((), ())), preferred_...]
    ppermute x91 -> x42, starting transfers between devices: 101 us -> 46.7 us  [shift(): return lax.ppermute(rows, 'dp', pairs)]
    all_gather x0 -> x1, waiting for transfers between devices: none -> 29.3 us  [gather_all(): return lax.all_gather(shard, 'dp', axis=0, tiled=True)]
    convert_element_type x1 -> x20, other arithmetic: 0.4 us -> 27.1 us  [the longest x18 25 us: step(): moved = moved.astype(jnp.bfloat16)]
  transfers between devices with their start and end apart: 119 -> 63, of which waited for: 53 -> 32; matrix products, arithmetic and copies ran while one was open for 28% -> 20% of each run, Pallas kernels for 1% -> 29%
where the time goes in v2:
time: 884 us; the launch traced here: 875 us
  waiting for transfers between devices  276 us (31%)
  Pallas kernels  270 us (31%)
  matrix products  112 us (13%)
  other arithmetic  93.2 us (11%)
  starting transfers between devices  57.7 us (7%)
  local copies, waits for them, and re-layouts  45 us (5%)
  between operations  20.8 us (2%)
    pallas_call x3, Pallas kernels, gather_ring(): pl.pallas_call(kernel, out_shape=[jax.ShapeDtypeStruct((devices * rows, s...  232 us
    ppermute x42, waiting for transfers between devices, shift(): return lax.ppermute(rows, 'dp', pairs)  137 us
    ppermute x8, waiting for transfers between devices, swap_mp(): return lax.ppermute(rows, 'mp', [(0, 1), (1, 0)])  54.9 us
    psum x1, waiting for transfers between devices, on_device(): grad_summed = lax.psum(grad_slots, 'dp')  54.4 us
    dot_general x7, matrix products, plain_dot(): return jnp.dot(first_op, second_op, preferred_element_type=jnp.float32)  49.5 us
    ppermute x42, starting transfers between devices, shift(): return lax.ppermute(rows, 'dp', pairs)  46.7 us
    all_gather x1, waiting for transfers between devices, gather_all(): return lax.all_gather(shard, 'dp', axis=0, tiled=True)  29.3 us
    dot_general x7, matrix products, contract_last(): lax.dot_general(first_op, second_op, (((1,), (1,)), ((), ())), preferred_...  29.2 us
  transfers between devices with their start and end apart: 63, of which 32 were waited for; matrix products, arithmetic and copies ran while one was open for 20% of the time, Pallas kernels for 29%

profile of v2, /device:TPU:0, one launch (start us, length us, event | category | flops | bytes accessed | tf_op | source)
XLA Modules:
  0.0 874.6 jit_solution(2422554850884110680)
XLA Ops:
  17.5 12.2 %shard_map.263 = f32[32,8,128]{2,1,0:T(8,128)} custom-call(f32[16,8,128]{2,1,0:T(8,128)} %concatenate.111.in_ref), custom_call_target="tpu_custom_call" | custom-call | tf_op jit(solution)/shard_map/pallas_call | solution.py:368
  40.0 66.1 %shard_map.264 = (bf16[2048,1024]{1,0:T(8,128)(2,1)}, bf16[2048,2048]{1,0:T(8,128)(2,1)}) custom-call(bf16[128,1024]{1,0:T(8,128)(2,1)} %refs_0_, bf16[128,2048]{1,0:T(8,128)(2,1)} %refs_1_.2), custom_call_target="tpu_custom_call" | custom-call | bytes 50331648 | tf_op jit(solution)/shard_map/pallas_call | solution.py:290
  113.4 5.8 convolution_convert_fusion.5
  121.8 85.1 %shard_map.265 = (bf16[2048,1024]{1,0:T(8,128)(2,1)}, bf16[2048,2048]{1,0:T(8,128)(2,1)}) custom-call(bf16[128,1024]{1,0:T(8,128)(2,1)} %refs_0_.1, bf16[128,2048]{1,0:T(8,128)(2,1)} %refs_1_.3), custom_call_target="tpu_custom_call" | custom-call | bytes 50331648 | tf_op jit(solution)/shard_map/pallas_call | solution.py:290
  210.2 8.0 fusion.37
  227.8 80.7 %shard_map.266 = bf16[2048,2048]{1,0:T(8,128)(2,1)} custom-call(bf16[128,2048]{1,0:T(8,128)(2,1)} %refs_0_.2), custom_call_target="tpu_custom_call" | custom-call | bytes 33554432 | tf_op jit(solution)/shard_map/pallas_call | solution.py:290
  318.9 6.2 fusion.124
  326.0 13.4 %collective-permute-done.1 = bf16[128,2048]{1,0:T(8,128)(2,1)S(1)} collective-permute-done((bf16[128,2048]{1,0:T(8,128)(2,1)S(1)}, bf16[128,2048]{1,0:T(8,128)(2,1)S(1)}, u32[]{:S(2)}, u32[]{:S(2)}) %collective-permute-start.1) | collective-permute-done | bytes 524320 | tf_op jit(solution)/shard_map/ppermute | solution.py:416
  341.8 12.8 %collective-permute-done.2 = bf16[128,2048]{1,0:T(8,128)(2,1)} collective-permute-done((bf16[128,2048]{1,0:T(8,128)(2,1)S(1)}, bf16[128,2048]{1,0:T(8,128)(2,1)}, u32[]{:S(2)}, u32[]{:S(2)}) %collective-permute-start.2) | collective-permute-done | bytes 524320 | tf_op jit(solution)/shard_map/ppermute | solution.py:416
  354.6 29.3 %all-gather.2.cloned.1.call-done = bf16[2048,4096]{1,0:T(8,128)(2,1)} async-done(((bf16[128,4096]{1,0:T(8,128)(2,1)}), bf16[2048,4096]{1,0:T(8,128)(2,1)}) %all-gather.2.cloned.1.call-update) | async-done | bytes 16777232 | tf_op jit(solution)/shard_map/all_gather | solution.py:496
  383.9 10.6 %multiply_convert_fusion.4 = (bf16[256,2048]{1,0:T(8,128)(2,1)S(1)}, f32[256,2048]{1,0:T(8,128)}) fusion(bf16[2048,4096]{1,0:T(8,128)(2,1)} %all-gather.2.cloned.1.call-done, bf16[128,2048]{1,0:T(8,128)(2,1)} %collective-permute-done.2, bf16[128,2048]{1,0:T(8,128)(2,1)} %copy-done.39), kind=kOutput, calls=%fused_computation.51 | convolution fusion | flops 2183659520 | bytes 12582912 | tf_op jit(solution)/shard_map/dot_general | solution.py:74
  402.8 10.7 %collective-permute-done.3 = bf16[128,2048]{1,0:T(8,128)(2,1)} collective-permute-done((bf16[128,2048]{1,0:T(8,128)(2,1)}, bf16[128,2048]{1,0:T(8,128)(2,1)}, u32[]{:S(2)}, u32[]{:S(2)}) %collective-permute-start.3) | collective-permute-done | bytes 524320 | tf_op jit(solution)/shard_map/ppermute | solution.py:416
  420.1 11.4 %collective-permute-done.4 = bf16[128,2048]{1,0:T(8,128)(2,1)} collective-permute-done((bf16[128,2048]{1,0:T(8,128)(2,1)}, bf16[128,2048]{1,0:T(8,128)(2,1)}, u32[]{:S(2)}, u32[]{:S(2)}) %collective-permute-start.4) | collective-permute-done | bytes 524320 | tf_op jit(solution)/shard_map/ppermute | solution.py:416
  437.9 10.3 %add_convert_fusion = bf16[256,2048]{1,0:T(8,128)(2,1)} fusion(bf16[256,2048]{1,0:T(8,128)(2,1)S(1)} %copy-done.28, bf16[2048,4096]{1,0:T(8,128)(2,1)} %all-gather.2.cloned.1.call-done, f32[256,2048]{1,0:T(8,128)} %get-tuple-element.155), kind=kOutput, calls=%fused_computation.50 | convolution fusion | flops 2185232384 | bytes 12582912 | tf_op jit(solution)/shard_map/dot_general | solution.py:74
  478.6 5.6 collective-permute-done.10
  486.8 6.1 fusion.4
  509.3 14.4 %collective-permute-done.13 = bf16[128,2048]{1,0:T(8,128)(2,1)S(1)} collective-permute-done((bf16[128,2048]{1,0:T(8,128)(2,1)}, bf16[128,2048]{1,0:T(8,128)(2,1)S(1)}, u32[]{:S(2)}, u32[]{:S(2)}) %collective-permute-start.13) | collective-permute-done | bytes 524320 | tf_op jit(solution)/shard_map/ppermute | solution.py:108
  548.6 6.9 fusion.125
  574.1 5.7 collective-permute-done.21
  593.0 7.2 collective-permute-done.27
  603.2 9.0 %collective-permute-done.38 = bf16[128,2048]{1,0:T(8,128)(2,1)S(1)} collective-permute-done((bf16[128,2048]{1,0:T(8,128)(2,1)S(1)}, bf16[128,2048]{1,0:T(8,128)(2,1)S(1)}, u32[]{:S(2)}, u32[]{:S(2)}) %collective-permute-start.38) | collective-permute-done | bytes 524320 | tf_op jit(solution)/shard_map/ppermute | solution.py:108
  619.3 8.6 collective-permute-done.36
  634.9 12.9 %collective-permute-done.32 = bf16[128,2048]{1,0:T(8,128)(2,1)} collective-permute-done((bf16[128,2048]{1,0:T(8,128)(2,1)}, bf16[128,2048]{1,0:T(8,128)(2,1)}, u32[]{:S(2)}, u32[]{:S(2)}) %collective-permute-start.32) | collective-permute-done | bytes 524320 | tf_op jit(solution)/shard_map/ppermute | solution.py:108
  659.0 6.4 collective-permute-done.41
  667.9 54.4 %all-reduce.7.cloned.1.call-done = bf16[2,4,256,512]{3,2,1,0:T(8,128)(2,1)} async-done(((bf16[2,4,256,512]{3,2,1,0:T(8,128)(2,1)}), bf16[2,4,256,512]{3,2,1,0:T(8,128)(2,1)}) %all-reduce.7.cloned.1.call-update) | async-done | bytes 2097168 | tf_op jit(solution)/shard_map/psum | solution.py:633
  743.7 10.2 %collective-permute-done.46 = bf16[128,1024]{1,0:T(8,128)(2,1)S(1)} collective-permute-done((bf16[128,1024]{1,0:T(8,128)(2,1)S(1)}, bf16[128,1024]{1,0:T(8,128)(2,1)S(1)}, u32[]{:S(2)}, u32[]{:S(2)}) %collective-permute-start.46) | collective-permute-done | bytes 262176 | tf_op jit(solution)/shard_map/ppermute | solution.py:108
  787.5 6.0 convolution_add_fusion.2
  796.4 7.6 collective-permute-done.51
  805.2 5.9 convolution_add_fusion.1
  812.7 6.9 collective-permute-done.57
  824.3 10.1 %collective-permute-done.55 = bf16[128,3072]{1,0:T(8,128)(2,1)S(1)} collective-permute-done((bf16[128,3072]{1,0:T(8,128)(2,1)S(1)}, bf16[128,3072]{1,0:T(8,128)(2,1)S(1)}, u32[]{:S(2)}, u32[]{:S(2)}) %collective-permute-start.55) | collective-permute-done | bytes 786464 | tf_op jit(solution)/shard_map/ppermute | solution.py:108
  842.8 15.8 %shard_map.271 = f32[32,8,128]{2,1,0:T(8,128)} custom-call(f32[16,8,128]{2,1,0:T(8,128)} %concatenate.134.in_ref), custom_call_target="tpu_custom_call" | custom-call | tf_op jit(solution)/shard_map/pallas_call | solution.py:368
  (474 shorter events, 291.5 us)
Async XLA Ops:
  7.2 304.8 %all-reduce.5.cloned.1.call-start = ((), (), s32[]{:S(2)}) async-start(), calls=%async_computation | async-start | bytes 4194304 | tf_op jit(solution)/shard_map/psum | solution.py:544
  35.1 72.3 %collective-permute-start = (bf16[128,2048]{1,0:T(8,128)(2,1)S(1)}, bf16[128,2048]{1,0:T(8,128)(2,1)S(1)}, u32[]{:S(2)}, u32[]{:S(2)}) collective-permute-start(bf16[128,2048]{1,0:T(8,128)(2,1)S(1)} %fusion.53), channel_id=1, source_target_pairs={{0,1},{1,0},{2,3},{3,2},{4,5},{5,4},{6,7},{7,6},{8,9},{9,8},{10,11... | collective-permute-start | bytes 1572872 | tf_op jit(solution)/shard_map/ppermute | solution.py:416
  121.7 262.1 %all-gather.2.cloned.1.call-start = ((), (), s32[]{:S(2)}) async-start(), calls=%async_computation.1 | async-start | bytes 17825792 | tf_op jit(solution)/shard_map/all_gather | solution.py:496
  208.0 514.4 %all-reduce.7.cloned.1.call-start = ((), (), s32[]{:S(2)}) async-start(), calls=%async_computation.2 | async-start | bytes 4194304 | tf_op jit(solution)/shard_map/psum | solution.py:633
  420.1 28.5 %collective-permute-start.6 = (bf16[256,2048]{1,0:T(8,128)(2,1)}, bf16[256,2048]{1,0:T(8,128)(2,1)}, u32[]{:S(2)}, u32[]{:S(2)}) collective-permute-start(bf16[256,2048]{1,0:T(8,128)(2,1)} %copy-done.103), channel_id=1, source_target_pairs={{0,2},{2,0},{4,6},{6,4},{8,10},{10,8},{12,14},{14,12},{16,18},{18,... | collective-permute-start | bytes 3145736 | tf_op jit(solution)/shard_map/ppermute | solution.py:111
  448.2 23.2 %collective-permute-start.17 = (bf16[256,2048]{1,0:T(8,128)(2,1)}, bf16[256,2048]{1,0:T(8,128)(2,1)}, u32[]{:S(2)}, u32[]{:S(2)}) collective-permute-start(bf16[256,2048]{1,0:T(8,128)(2,1)} %add_convert_fusion), channel_id=1, source_target_pairs={{0,2},{2,0},{4,6},{6,4},{8,10},{10,8},{12,14},{14,12},{16,18},{18,... | collective-permute-start | bytes 3145736 | tf_op jit(solution)/shard_map/ppermute | solution.py:111
  476.8 25.9 %collective-permute-start.19 = (bf16[128,2048]{1,0:T(8,128)(2,1)}, bf16[128,2048]{1,0:T(8,128)(2,1)}, u32[]{:S(2)}, u32[]{:S(2)}) collective-permute-start(bf16[128,2048]{1,0:T(8,128)(2,1)} %get-tuple-element.96), channel_id=1, source_target_pairs={{0,4},{2,6},{8,0},{10,2},{16,8},{18,10},{24,16},{26,18},{28,24},{3... | collective-permute-start | bytes 1572872 | tf_op jit(solution)/shard_map/ppermute | solution.py:108
  500.2 29.9 %collective-permute-start.18 = (bf16[128,2048]{1,0:T(8,128)(2,1)}, bf16[128,2048]{1,0:T(8,128)(2,1)S(1)}, u32[]{:S(2)}, u32[]{:S(2)}) collective-permute-start(bf16[128,2048]{1,0:T(8,128)(2,1)} %get-tuple-element.97), channel_id=1, source_target_pairs={{0,8},{2,10},{8,16},{10,18},{16,24},{18,26},{24,28},{26,30},{28,20... | collective-permute-start | bytes 1572872 | tf_op jit(solution)/shard_map/ppermute | solution.py:108
  500.7 22.9 %collective-permute-start.11 = (bf16[128,2048]{1,0:T(8,128)(2,1)}, bf16[128,2048]{1,0:T(8,128)(2,1)S(1)}, u32[]{:S(2)}, u32[]{:S(2)}) collective-permute-start(bf16[128,2048]{1,0:T(8,128)(2,1)} %get-tuple-element.101), channel_id=1, source_target_pairs={{0,4},{2,6},{8,0},{10,2},{16,8},{18,10},{24,16},{26,18},{28,24},{3... | collective-permute-start | bytes 1572872 | tf_op jit(solution)/shard_map/ppermute | solution.py:108
  502.2 21.4 %collective-permute-start.13 = (bf16[128,2048]{1,0:T(8,128)(2,1)}, bf16[128,2048]{1,0:T(8,128)(2,1)S(1)}, u32[]{:S(2)}, u32[]{:S(2)}) collective-permute-start(bf16[128,2048]{1,0:T(8,128)(2,1)} %get-tuple-element.100), channel_id=1, source_target_pairs={{0,8},{2,10},{8,16},{10,18},{16,24},{18,26},{24,28},{26,30},{28,20... | collective-permute-start | bytes 1572872 | tf_op jit(solution)/shard_map/ppermute | solution.py:108
  504.1 26.6 %collective-permute-start.22 = (bf16[128,2048]{1,0:T(8,128)(2,1)S(1)}, bf16[128,2048]{1,0:T(8,128)(2,1)S(1)}, u32[]{:S(2)}, u32[]{:S(2)}) collective-permute-start(bf16[128,2048]{1,0:T(8,128)(2,1)S(1)} %add_convert_fusion.19), channel_id=1, source_target_pairs={{0,4},{2,6},{8,0},{10,2},{16,8},{18,10},{24,16},{26,18},{28,24},{3... | collective-permute-start | bytes 1572872 | tf_op jit(solution)/shard_map/ppermute | solution.py:108
  529.5 58.5 %collective-permute-start.31 = (bf16[256,1024]{1,0:T(8,128)(2,1)}, bf16[256,1024]{1,0:T(8,128)(2,1)}, u32[]{:S(2)}, u32[]{:S(2)}) collective-permute-start(bf16[256,1024]{1,0:T(8,128)(2,1)} %get-tuple-element.119), channel_id=1, source_target_pairs={{0,2},{2,0},{4,6},{6,4},{8,10},{10,8},{12,14},{14,12},{16,18},{18,... | collective-permute-start | bytes 1572872 | tf_op jit(solution)/shard_map/ppermute | solution.py:111
  529.5 52.1 %collective-permute-start.26 = (bf16[256,2048]{0,1:T(8,128)(2,1)}, bf16[256,2048]{0,1:T(8,128)(2,1)}, u32[]{:S(2)}, u32[]{:S(2)}) collective-permute-start(bf16[256,2048]{0,1:T(8,128)(2,1)} %bitcast.11), channel_id=1, source_target_pairs={{0,2},{2,0},{4,6},{6,4},{8,10},{10,8},{12,14},{14,12},{16,18},{18,... | collective-permute-start | bytes 3145736 | tf_op jit(solution)/shard_map/ppermute | solution.py:111
  539.1 23.0 %collective-permute-start.23 = (bf16[128,2048]{1,0:T(8,128)(2,1)}, bf16[128,2048]{1,0:T(8,128)(2,1)}, u32[]{:S(2)}, u32[]{:S(2)}) collective-permute-start(bf16[128,2048]{1,0:T(8,128)(2,1)} %get-tuple-element.94), channel_id=1, source_target_pairs={{0,4},{2,6},{8,0},{10,2},{16,8},{18,10},{24,16},{26,18},{28,24},{3... | collective-permute-start | bytes 1572872 | tf_op jit(solution)/shard_map/ppermute | solution.py:108
  559.1 22.5 %collective-permute-start.25 = (bf16[256,1024]{1,0:T(8,128)(2,1)}, bf16[256,1024]{1,0:T(8,128)(2,1)}, u32[]{:S(2)}, u32[]{:S(2)}) collective-permute-start(bf16[256,1024]{1,0:T(8,128)(2,1)} %get-tuple-element.121), channel_id=1, source_target_pairs={{0,2},{2,0},{4,6},{6,4},{8,10},{10,8},{12,14},{14,12},{16,18},{18,... | collective-permute-start | bytes 1572872 | tf_op jit(solution)/shard_map/ppermute | solution.py:111
  566.5 52.8 %collective-permute-start.24 = (bf16[128,2048]{1,0:T(8,128)(2,1)}, bf16[128,2048]{1,0:T(8,128)(2,1)S(1)}, u32[]{:S(2)}, u32[]{:S(2)}) collective-permute-start(bf16[128,2048]{1,0:T(8,128)(2,1)} %get-tuple-element.92), channel_id=1, source_target_pairs={{0,4},{2,6},{8,0},{10,2},{16,8},{18,10},{24,16},{26,18},{28,24},{3... | collective-permute-start | bytes 1572872 | tf_op jit(solution)/shard_map/ppermute | solution.py:108
  586.7 27.6 %collective-permute-start.28 = (bf16[128,2048]{1,0:T(8,128)(2,1)S(1)}, bf16[128,2048]{1,0:T(8,128)(2,1)S(1)}, u32[]{:S(2)}, u32[]{:S(2)}) collective-permute-start(bf16[128,2048]{1,0:T(8,128)(2,1)S(1)} %get-tuple-element.90), channel_id=1, source_target_pairs={{0,4},{2,6},{8,0},{10,2},{16,8},{18,10},{24,16},{26,18},{28,24},{3... | collective-permute-start | bytes 1572872 | tf_op jit(solution)/shard_map/ppermute | solution.py:108
  592.4 19.7 %collective-permute-start.38 = (bf16[128,2048]{1,0:T(8,128)(2,1)S(1)}, bf16[128,2048]{1,0:T(8,128)(2,1)S(1)}, u32[]{:S(2)}, u32[]{:S(2)}) collective-permute-start(bf16[128,2048]{1,0:T(8,128)(2,1)S(1)} %get-tuple-element.84), channel_id=1, source_target_pairs={{0,4},{2,6},{8,0},{10,2},{16,8},{18,10},{24,16},{26,18},{28,24},{3... | collective-permute-start | bytes 1572872 | tf_op jit(solution)/shard_map/ppermute | solution.py:108
  601.9 26.1 %collective-permute-start.36 = (bf16[128,2048]{1,0:T(8,128)(2,1)}, bf16[128,2048]{1,0:T(8,128)(2,1)}, u32[]{:S(2)}, u32[]{:S(2)}) collective-permute-start(bf16[128,2048]{1,0:T(8,128)(2,1)} %get-tuple-element.85), channel_id=1, source_target_pairs={{0,8},{2,10},{8,16},{10,18},{16,24},{18,26},{24,28},{26,30},{28,20... | collective-permute-start | bytes 1572872 | tf_op jit(solution)/shard_map/ppermute | solution.py:108
  613.1 17.8 %collective-permute-start.39 = (bf16[128,2048]{1,0:T(8,128)(2,1)}, bf16[128,2048]{1,0:T(8,128)(2,1)}, u32[]{:S(2)}, u32[]{:S(2)}) collective-permute-start(bf16[128,2048]{1,0:T(8,128)(2,1)} %add_convert_fusion.8), channel_id=1, source_target_pairs={{0,4},{2,6},{8,0},{10,2},{16,8},{18,10},{24,16},{26,18},{28,24},{3... | collective-permute-start | bytes 1572872 | tf_op jit(solution)/shard_map/ppermute | solution.py:108
  616.6 31.2 %collective-permute-start.32 = (bf16[128,2048]{1,0:T(8,128)(2,1)}, bf16[128,2048]{1,0:T(8,128)(2,1)}, u32[]{:S(2)}, u32[]{:S(2)}) collective-permute-start(bf16[128,2048]{1,0:T(8,128)(2,1)} %get-tuple-element.88), channel_id=1, source_target_pairs={{0,8},{2,10},{8,16},{10,18},{16,24},{18,26},{24,28},{26,30},{28,20... | collective-permute-start | bytes 1572872 | tf_op jit(solution)/shard_map/ppermute | solution.py:108
  617.4 35.3 %collective-permute-start.30 = (bf16[128,2048]{1,0:T(8,128)(2,1)}, bf16[128,2048]{1,0:T(8,128)(2,1)}, u32[]{:S(2)}, u32[]{:S(2)}) collective-permute-start(bf16[128,2048]{1,0:T(8,128)(2,1)} %get-tuple-element.89), channel_id=1, source_target_pairs={{0,4},{2,6},{8,0},{10,2},{16,8},{18,10},{24,16},{26,18},{28,24},{3... | collective-permute-start | bytes 1572872 | tf_op jit(solution)/shard_map/ppermute | solution.py:108
  632.9 32.5 %collective-permute-start.41 = (bf16[128,2048]{1,0:T(8,128)(2,1)S(1)}, bf16[128,2048]{1,0:T(8,128)(2,1)S(1)}, u32[]{:S(2)}, u32[]{:S(2)}) collective-permute-start(bf16[128,2048]{1,0:T(8,128)(2,1)S(1)} %get-tuple-element.82), channel_id=1, source_target_pairs={{0,4},{2,6},{8,0},{10,2},{16,8},{18,10},{24,16},{26,18},{28,24},{3... | collective-permute-start | bytes 1572872 | tf_op jit(solution)/shard_map/ppermute | solution.py:108
  634.7 30.7 %collective-permute-start.37 = (bf16[128,2048]{1,0:T(8,128)(2,1)S(1)}, bf16[128,2048]{1,0:T(8,128)(2,1)S(1)}, u32[]{:S(2)}, u32[]{:S(2)}) collective-permute-start(bf16[128,2048]{1,0:T(8,128)(2,1)S(1)} %get-tuple-element.83), channel_id=1, source_target_pairs={{0,8},{2,10},{8,16},{10,18},{16,24},{18,26},{24,28},{26,30},{28,20... | collective-permute-start | bytes 1572872 | tf_op jit(solution)/shard_map/ppermute | solution.py:108
  655.6 66.7 %collective-permute-start.33 = (bf16[128,2048]{1,0:T(8,128)(2,1)}, bf16[128,2048]{1,0:T(8,128)(2,1)S(1)}, u32[]{:S(2)}, u32[]{:S(2)}) collective-permute-start(bf16[128,2048]{1,0:T(8,128)(2,1)} %get-tuple-element.86), channel_id=1, source_target_pairs={{0,8},{2,10},{8,16},{10,18},{16,24},{18,26},{24,28},{26,30},{28,20... | collective-permute-start | bytes 1572872 | tf_op jit(solution)/shard_map/ppermute | solution.py:108
  656.9 65.5 %collective-permute-start.34 = (bf16[128,2048]{1,0:T(8,128)(2,1)}, bf16[128,2048]{1,0:T(8,128)(2,1)S(1)}, u32[]{:S(2)}, u32[]{:S(2)}) collective-permute-start(bf16[128,2048]{1,0:T(8,128)(2,1)} %get-tuple-element.87), channel_id=1, source_target_pairs={{0,4},{2,6},{8,0},{10,2},{16,8},{18,10},{24,16},{26,18},{28,24},{3... | collective-permute-start | bytes 1572872 | tf_op jit(solution)/shard_map/ppermute | solution.py:108
  733.8 22.5 %collective-permute-start.40 = (bf16[128,2048]{1,0:T(8,128)(2,1)}, bf16[128,2048]{1,0:T(8,128)(2,1)}, u32[]{:S(2)}, u32[]{:S(2)}) collective-permute-start(bf16[128,2048]{1,0:T(8,128)(2,1)} %get-tuple-element.81), channel_id=1, source_target_pairs={{0,8},{2,10},{8,16},{10,18},{16,24},{18,26},{24,28},{26,30},{28,20... | collective-permute-start | bytes 1572872 | tf_op jit(solution)/shard_map/ppermute | solution.py:108
  737.8 35.4 %collective-permute-start.44 = (bf16[128,2048]{1,0:T(8,128)(2,1)}, bf16[128,2048]{1,0:T(8,128)(2,1)S(1)}, u32[]{:S(2)}, u32[]{:S(2)}) collective-permute-start(bf16[128,2048]{1,0:T(8,128)(2,1)} %get-tuple-element.80), channel_id=1, source_target_pairs={{0,4},{2,6},{8,0},{10,2},{16,8},{18,10},{24,16},{26,18},{28,24},{3... | collective-permute-start | bytes 1572872 | tf_op jit(solution)/shard_map/ppermute | solution.py:108
  756.3 22.4 %collective-permute-start.42 = (bf16[256,3072]{0,1:T(8,128)(2,1)S(1)}, bf16[256,3072]{0,1:T(8,128)(2,1)S(1)}, u32[]{:S(2)}, u32[]{:S(2)}) collective-permute-start(bf16[256,3072]{0,1:T(8,128)(2,1)S(1)} %pad_maximum_fusion), channel_id=1, source_target_pairs={{0,2},{2,0},{4,6},{6,4},{8,10},{10,8},{12,14},{14,12},{16,18},{18,... | collective-permute-start | bytes 4718600 | tf_op jit(solution)/shard_map/ppermute | solution.py:111
  793.5 19.2 %collective-permute-start.50 = (bf16[128,3072]{1,0:T(8,128)(2,1)S(1)}, bf16[128,3072]{1,0:T(8,128)(2,1)S(1)}, u32[]{:S(2)}, u32[]{:S(2)}) collective-permute-start(bf16[128,3072]{1,0:T(8,128)(2,1)S(1)} %get-tuple-element.78), channel_id=1, source_target_pairs={{0,8},{2,10},{8,16},{10,18},{16,24},{18,26},{24,28},{26,30},{28,20... | collective-permute-start | bytes 2359304 | tf_op jit(solution)/shard_map/ppermute | solution.py:108
  839.4 23.2 %collective-permute-start.59 = (bf16[128,3072]{1,0:T(8,128)(2,1)}, bf16[128,3072]{1,0:T(8,128)(2,1)}, u32[]{:S(2)}, u32[]{:S(2)}) collective-permute-start(bf16[128,3072]{1,0:T(8,128)(2,1)} %get-tuple-element.74), channel_id=1, source_target_pairs={{0,4},{2,6},{8,0},{10,2},{16,8},{18,10},{24,16},{26,18},{28,24},{3... | collective-permute-start | bytes 2359304 | tf_op jit(solution)/shard_map/ppermute | solution.py:108
  841.1 21.6 %collective-permute-start.56 = (bf16[128,3072]{1,0:T(8,128)(2,1)S(1)}, bf16[128,3072]{1,0:T(8,128)(2,1)}, u32[]{:S(2)}, u32[]{:S(2)}) collective-permute-start(bf16[128,3072]{1,0:T(8,128)(2,1)S(1)} %get-tuple-element.73), channel_id=1, source_target_pairs={{0,8},{2,10},{8,16},{10,18},{16,24},{18,26},{24,28},{26,30},{28,20... | collective-permute-start | bytes 2359304 | tf_op jit(solution)/shard_map/ppermute | solution.py:108
  (136 other events, 2774.2 us)
Sparse Core Ops, SparseCore 0:
  121.9 105.4 all-reduce.4
  230.1 153.7 all-gather.1
  619.4 102.8 all-reduce.6

commit v3 on v2

--- a/solution.py
+++ b/solution.py
@@ -1,3 +1,4 @@
+import functools
 import math
 
 import jax
@@ -120,16 +121,20 @@
 
 
 class RingSum:
-    def __init__(self, ring, full, flip):
+    def __init__(self, ring, full, arrived, flip):
         self.ring = ring
         self.full = full
+        self.arrived = arrived
         self.block = full.shape[0] // ring.chips
         self.up, self.down = ring.hops(flip)
-        self.moving = [self.term(self.up), self.term(ring.chips - self.down)]
+        self.moving = [
+            self.term(k).astype(jnp.bfloat16) for k in (self.up, ring.chips - self.down)
+        ]
         self.count = 0
 
     def term(self, k):
-        return self.full[k * self.block : (k + 1) * self.block]
+        rows = slice(k * self.block, (k + 1) * self.block)
+        return self.full[rows].astype(jnp.float32) + self.arrived[rows].astype(jnp.float32)
 
     def step(self):
         ring = self.ring
@@ -141,8 +146,7 @@
             if self.count <= hops:
                 moved = ring.shift(self.moving[way], 1 - 2 * way)
                 if self.count < hops:
-                    moved = moved.astype(jnp.float32) + self.term(k).astype(jnp.float32)
-                    moved = moved.astype(jnp.bfloat16)
+                    moved = (moved.astype(jnp.float32) + self.term(k)).astype(jnp.bfloat16)
                 self.moving[way] = moved
 
     def run(self, steps):
@@ -152,13 +156,13 @@
     def result(self):
         self.run(self.ring.chips)
         return (
-            self.term(0).astype(jnp.float32)
+            self.term(0)
             + self.moving[0].astype(jnp.float32)
             + self.moving[1].astype(jnp.float32)
         )
 
 
-def gather_ring(shards, call_id=1):
+def gather_ring(shards, call_id=1, first=None):
     devices = lax.axis_size("dp")
     chips = devices // 2
     half = chips // 2
@@ -169,8 +173,13 @@
     hops = ((half, half - 1), (half - 1, half))
 
     def kernel(*refs):
-        ins, outs = refs[:count], refs[count : 2 * count]
-        own_sem, side_send, side_recv, ring_send, ring_recv = refs[2 * count :]
+        ins, refs = refs[:count], refs[count:]
+        if first is not None:
+            (blocks_ref, rows_ref), refs = refs[:2], refs[2:]
+        outs, refs = refs[:count], refs[count:]
+        if first is not None:
+            (from_ref, norm_ref), refs = refs[:2], refs[2:]
+        own_sem, side_send, side_recv, ring_send, ring_recv = refs[:5]
         index = lax.axis_index("dp")
         core, chip = index % 2, index // 2
         odd = chip % 2
@@ -189,12 +198,16 @@
         partner = chip * 2 + 1 - core
         neighbours = (device_at(place + 1, core), device_at(place - 1, core))
 
-        barrier = pltpu.get_barrier_semaphore()
-        for target in (*neighbours, partner):
-            pl.semaphore_signal(
-                barrier, inc=1, device_id={"dp": target}, device_id_type=pl.DeviceIdType.MESH
-            )
-        pl.semaphore_wait(barrier, 3)
+        if first is None:
+            barrier = pltpu.get_barrier_semaphore()
+            for target in (*neighbours, partner):
+                pl.semaphore_signal(
+                    barrier, inc=1, device_id={"dp": target}, device_id_type=pl.DeviceIdType.MESH
+                )
+            pl.semaphore_wait(barrier, 3)
+        else:
+            small = (blocks_ref, from_ref, refs[5], refs[6])
+            exchange_start(*small)
 
         sends = []
 
@@ -266,7 +279,28 @@
                 )
                 own.start()
                 owns.append(own)
+        if first is not None:
+            exchange_finish(*small)
+            values = rows_ref[...].astype(jnp.float32)
+            normed, _ = norm_stats(values, EPSILON)
+            mp_size = lax.axis_size("mp")
+            for d in range(devices):
+                cols = slice(d * rows, (d + 1) * rows)
+                sent = from_ref[d * mp_size]
+                norm_ref[0, :, cols] = (normed[:, cols] * sent[0:1] + sent[1:2]).astype(
+                    norm_ref.dtype
+                )
         for hop in range(1, half + 1):
+            if first is not None and hop == 2:
+                across = pltpu.make_async_remote_copy(
+                    src_ref=norm_ref.at[0],
+                    dst_ref=norm_ref.at[1],
+                    send_sem=refs[7].at[0],
+                    recv_sem=refs[7].at[1],
+                    device_id={"mp": 1 - lax.axis_index("mp")},
+                    device_id_type=pl.DeviceIdType.MESH,
+                )
+                across.start()
             for part in range(parts):
                 for j in range(count):
                     for way in range(2):
@@ -285,27 +319,260 @@
             for part in range(parts):
                 for j in range(count):
                     side_arrival(j, part, slot, place + slot).wait_recv()
+        if first is not None:
+            across.wait()
 
     total = sum(shard.shape[1] for shard in shards) * rows * 2
+    out_shape = [
+        jax.ShapeDtypeStruct((devices * rows, shard.shape[1]), shard.dtype) for shard in shards
+    ]
+    in_specs = [pl.BlockSpec(memory_space=pl.ANY)] * count
+    out_specs = [pl.BlockSpec(memory_space=pl.ANY)] * count
+    scratch = [
+        pltpu.SemaphoreType.DMA((count, parts)),
+        pltpu.SemaphoreType.DMA((count, parts, chips)),
+        pltpu.SemaphoreType.DMA((count, parts, chips)),
+        pltpu.SemaphoreType.DMA((count, 2, parts, half)),
+        pltpu.SemaphoreType.DMA((count, 2, parts, half)),
+    ]
+    extra = ()
+    if first is not None:
+        extra = first
+        peers = devices * lax.axis_size("mp")
+        in_specs = in_specs + [pl.BlockSpec(memory_space=pltpu.VMEM)] * 2
+        out_specs = out_specs + [pl.BlockSpec(memory_space=pltpu.VMEM)] * 2
+        out_shape = out_shape + [
+            jax.ShapeDtypeStruct((peers, *first[0].shape[1:]), first[0].dtype),
+            jax.ShapeDtypeStruct((2, *first[1].shape), jnp.bfloat16),
+        ]
+        scratch = scratch + [
+            pltpu.SemaphoreType.DMA((peers,)),
+            pltpu.SemaphoreType.DMA((peers,)),
+            pltpu.SemaphoreType.DMA((2,)),
+        ]
     return pl.pallas_call(
         kernel,
-        out_shape=[
-            jax.ShapeDtypeStruct((devices * rows, shard.shape[1]), shard.dtype) for shard in shards
-        ],
-        in_specs=[pl.BlockSpec(memory_space=pl.ANY)] * count,
-        out_specs=[pl.BlockSpec(memory_space=pl.ANY)] * count,
-        scratch_shapes=[
-            pltpu.SemaphoreType.DMA((count, parts)),
-            pltpu.SemaphoreType.DMA((count, parts, chips)),
-            pltpu.SemaphoreType.DMA((count, parts, chips)),
-            pltpu.SemaphoreType.DMA((count, 2, parts, half)),
-            pltpu.SemaphoreType.DMA((count, 2, parts, half)),
-        ],
+        out_shape=out_shape,
+        in_specs=in_specs,
+        out_specs=out_specs,
+        scratch_shapes=scratch,
         compiler_params=pltpu.CompilerParams(collective_id=call_id, has_side_effects=True),
         cost_estimate=pl.CostEstimate(
             flops=0, bytes_accessed=total * devices * 4, transcendentals=0
         ),
-    )(*shards)
+    )(*shards, *extra)
+
+
+def ring_total(rows):
+    devices = lax.axis_size("dp")
+    chips = devices // 2
+    half = chips // 2
+    hops = (half, chips - 1 - half)
+    width = rows.shape[1]
+    piece = rows.shape[0] // (2 * chips)
+    low = rows.dtype
+
+    def kernel(
+        in_ref,
+        out_ref,
+        mate,
+        mine,
+        landed,
+        packed,
+        pair_sem,
+        sum_send,
+        sum_recv,
+        ring_send,
+        ring_recv,
+        side_send,
+        side_recv,
+    ):
+        index = lax.axis_index("dp")
+        core, chip = index % 2, index // 2
+        odd = chip % 2
+        place = (1 - odd) * (chip // 2) + odd * (chips - 1 - chip // 2)
+
+        def device_at(spot):
+            spot = (spot + 2 * chips) % chips
+            upper = spot // half
+            there = (1 - upper) * (2 * spot) + upper * (2 * (chips - 1 - spot) + 1)
+            return there * 2 + core
+
+        def spot(k):
+            return (place + k + 2 * chips) % chips
+
+        partner = chip * 2 + 1 - core
+        neighbours = (device_at(place + 1), device_at(place - 1))
+
+        def copy_to(target, source, dest, send, recv):
+            return pltpu.make_async_remote_copy(
+                src_ref=source,
+                dst_ref=dest,
+                send_sem=send,
+                recv_sem=recv,
+                device_id={"dp": target},
+                device_id_type=pl.DeviceIdType.MESH,
+            )
+
+        barrier = pltpu.get_barrier_semaphore()
+        for target in (*neighbours, partner):
+            pl.semaphore_signal(
+                barrier, inc=1, device_id={"dp": target}, device_id_type=pl.DeviceIdType.MESH
+            )
+        pl.semaphore_wait(barrier, 3)
+
+        pair = copy_to(partner, in_ref.at[1 - core], mate, pair_sem.at[0], pair_sem.at[1])
+        pair.start()
+        pair.wait()
+
+        def add_mate(k, carry):
+            mine[k] = (in_ref[core, k].astype(jnp.float32) + mate[k].astype(jnp.float32)).astype(
+                low
+            )
+            return carry
+
+        lax.fori_loop(0, chips, add_mate, 0)
+
+        sends = []
+
+        def launch(copy):
+            copy.start()
+            sends.append(copy)
+
+        def sum_copy(way, step, source):
+            return copy_to(
+                neighbours[way],
+                source,
+                landed.at[way, step],
+                sum_send.at[way, step],
+                sum_recv.at[way, step],
+            )
+
+        for way in range(2):
+            launch(sum_copy(way, 0, mine.at[spot(hops[way] * (1 - 2 * way))]))
+        for step in range(1, half + 1):
+            for way in range(2):
+                if step <= hops[way]:
+                    sum_copy(way, step - 1, landed.at[way, step - 1]).wait_recv()
+                    if step < hops[way]:
+                        ahead = spot((hops[way] - step) * (1 - 2 * way))
+                        packed[way, step] = (
+                            landed[way, step - 1].astype(jnp.float32)
+                            + mine[ahead].astype(jnp.float32)
+                        ).astype(low)
+                        launch(sum_copy(way, step, packed.at[way, step]))
+        out_ref[core, place] = (
+            mine[place].astype(jnp.float32)
+            + landed[0, hops[0] - 1].astype(jnp.float32)
+            + landed[1, hops[1] - 1].astype(jnp.float32)
+        ).astype(low)
+
+        def ring_copy(way, hop):
+            there = out_ref.at[core, spot(-(hop - 1) * (1 - 2 * way))]
+            return copy_to(
+                neighbours[way], there, there, ring_send.at[way, hop - 1], ring_recv.at[way, hop - 1]
+            )
+
+        def ring_arrival(way, hop):
+            here = out_ref.at[core, spot(-hop * (1 - 2 * way))]
+            return copy_to(
+                neighbours[way], here, here, ring_send.at[way, hop - 1], ring_recv.at[way, hop - 1]
+            )
+
+        def side_copy(slot, which):
+            there = out_ref.at[which, spot(slot)]
+            return copy_to(partner, there, there, side_send.at[slot], side_recv.at[slot])
+
+        for way in range(2):
+            launch(ring_copy(way, 1))
+        launch(side_copy(0, core))
+        for hop in range(1, half + 1):
+            for way in range(2):
+                if hop <= hops[way]:
+                    ring_arrival(way, hop).wait_recv()
+                    if hop < hops[way]:
+                        launch(ring_copy(way, hop + 1))
+                    launch(side_copy((chips - hop * (1 - 2 * way)) % chips, core))
+        for copy in sends:
+            copy.wait_send()
+        for slot in range(chips):
+            side_copy(slot, 1 - core).wait_recv()
+
+    shape = (2, chips, piece, width)
+    total = pl.pallas_call(
+        kernel,
+        out_shape=jax.ShapeDtypeStruct(shape, low),
+        in_specs=[pl.BlockSpec(memory_space=pltpu.VMEM)],
+        out_specs=pl.BlockSpec(memory_space=pltpu.VMEM),
+        scratch_shapes=[
+            pltpu.VMEM(shape[1:], low),
+            pltpu.VMEM(shape[1:], low),
+            pltpu.VMEM((2, half, piece, width), low),
+            pltpu.VMEM((2, half, piece, width), low),
+            pltpu.SemaphoreType.DMA((2,)),
+            pltpu.SemaphoreType.DMA((2, half)),
+            pltpu.SemaphoreType.DMA((2, half)),
+            pltpu.SemaphoreType.DMA((2, half)),
+            pltpu.SemaphoreType.DMA((2, half)),
+            pltpu.SemaphoreType.DMA((chips,)),
+            pltpu.SemaphoreType.DMA((chips,)),
+        ],
+        compiler_params=pltpu.CompilerParams(collective_id=5, has_side_effects=True),
+    )(rows.reshape(shape))
+    return total.reshape(rows.shape)
+
+
+def each_peer(action):
+    dp_size, mp_size = lax.axis_size("dp"), lax.axis_size("mp")
+    me = lax.axis_index("dp") * mp_size + lax.axis_index("mp")
+    for place in range(dp_size * mp_size):
+        pl.when(me != place)(
+            functools.partial(action, place, place // mp_size, place % mp_size)
+        )
+
+
+def exchange_start(in_ref, out_ref, send_sem, recv_sem):
+    dp_size, mp_size = lax.axis_size("dp"), lax.axis_size("mp")
+    dp_index = lax.axis_index("dp")
+    me = dp_index * mp_size + lax.axis_index("mp")
+    barrier = pltpu.get_barrier_semaphore()
+
+    def greet(place, row, col):
+        pl.semaphore_signal(
+            barrier, inc=1, device_id=(row, col), device_id_type=pl.DeviceIdType.MESH
+        )
+
+    each_peer(greet)
+    pl.semaphore_wait(barrier, dp_size * mp_size - 1)
+
+    def send(place, row, col):
+        pltpu.make_async_remote_copy(
+            src_ref=in_ref.at[row],
+            dst_ref=out_ref.at[me],
+            send_sem=send_sem.at[place],
+            recv_sem=recv_sem.at[me],
+            device_id=(row, col),
+            device_id_type=pl.DeviceIdType.MESH,
+        ).start()
+
+    each_peer(send)
+    out_ref[me] = in_ref[dp_index]
+
+
+def exchange_finish(in_ref, out_ref, send_sem, recv_sem):
+    def finish(place, row, col):
+        copy = pltpu.make_async_remote_copy(
+            src_ref=in_ref.at[row],
+            dst_ref=out_ref.at[place],
+            send_sem=send_sem.at[place],
+            recv_sem=recv_sem.at[place],
+            device_id=(row, col),
+            device_id_type=pl.DeviceIdType.MESH,
+        )
+        copy.wait_send()
+        copy.wait_recv()
+
+    each_peer(finish)
 
 
 def exchange_blocks(blocks):
@@ -313,57 +580,8 @@
     total = dp_size * mp_size
 
     def kernel(in_ref, out_ref, send_sem, recv_sem):
-        dp_index = lax.axis_index("dp")
-        me = dp_index * mp_size + lax.axis_index("mp")
-
-        def place(offset):
-            target = (me + offset) % total
-            return target // mp_size, target % mp_size
-
-        barrier = pltpu.get_barrier_semaphore()
-
-        def greet(offset, carry):
-            row, col = place(offset)
-            pl.semaphore_signal(
-                barrier, inc=1, device_id=(row, col), device_id_type=pl.DeviceIdType.MESH
-            )
-            return carry
-
-        lax.fori_loop(1, total, greet, 0)
-        pl.semaphore_wait(barrier, total - 1)
-
-        def send(offset):
-            row, col = place(offset)
-            return pltpu.make_async_remote_copy(
-                src_ref=in_ref.at[row],
-                dst_ref=out_ref.at[me],
-                send_sem=send_sem.at[offset],
-                recv_sem=recv_sem.at[offset],
-                device_id=(row, col),
-                device_id_type=pl.DeviceIdType.MESH,
-            )
-
-        def begin(offset, carry):
-            send(offset).start()
-            return carry
-
-        lax.fori_loop(1, total, begin, 0)
-        out_ref[me] = in_ref[dp_index]
-
-        def finish(offset, carry):
-            sender = (me + total - offset) % total
-            send(offset).wait_send()
-            pltpu.make_async_remote_copy(
-                src_ref=out_ref.at[sender],
-                dst_ref=out_ref.at[sender],
-                send_sem=send_sem.at[offset],
-                recv_sem=recv_sem.at[offset],
-                device_id=place(offset),
-                device_id_type=pl.DeviceIdType.MESH,
-            ).wait_recv()
-            return carry
-
-        lax.fori_loop(1, total, finish, 0)
+        exchange_start(in_ref, out_ref, send_sem, recv_sem)
+        exchange_finish(in_ref, out_ref, send_sem, recv_sem)
 
     return pl.pallas_call(
         kernel,
@@ -483,9 +701,15 @@
         return jnp.concatenate([split, extra], axis=1)
 
     vectors = jnp.stack([ln1_gain, ln1_bias, ln2_gain, ln2_bias]).astype(jnp.float32)
-    from_all = exchange_blocks(
-        packed(jnp.tile(vectors, (1, ring.devices)), jnp.sum(loss_mask))
-    )
+    blocks_own = packed(jnp.tile(vectors, (1, ring.devices)), jnp.sum(loss_mask))
+    inside = block == 128
+    if inside:
+        wk_full, wv_full, from_all, a_pair = gather_ring(
+            [w_key, w_value], 1, (blocks_own, tokens_in)
+        )
+        a_all = a_pair.reshape(seg_len, model_dim)
+    else:
+        from_all = exchange_blocks(blocks_own)
     valid_count = jnp.sum(from_all[:, 4, 0])
     by_row = from_all.reshape(ring.devices, -1, 8, 128)[:, 0, :4, :block]
     gain_one, bias_one, gain_two, bias_two = (
@@ -521,10 +745,10 @@
     token_rows = tokens_in.astype(jnp.float32)
     teacher_rows = teacher.astype(jnp.float32)
     normed_one, inv_one = norm_stats(token_rows, EPSILON)
-    a_own = (normed_one * gain_one + bias_one).astype(jnp.bfloat16)
-    a_all = gather_rows(a_own)
-    wk_full, wv_full = gather_ring([tie(w_key, a_own), w_value])
-    keys_raw = plain_dot(a_all, wk_full).reshape(seg_len, heads_local, DK)
+    if not inside:
+        a_all = gather_rows((normed_one * gain_one + bias_one).astype(jnp.bfloat16))
+        wk_full, wv_full = gather_ring([w_key, w_value])
+    keys_raw = lax.optimization_barrier(plain_dot(a_all, wk_full)).reshape(seg_len, heads_local, DK)
     reduced_values = (
         plain_dot(a_all, wv_full).astype(jnp.bfloat16).reshape(seg_len, heads_local, DV)
     )
@@ -542,14 +766,12 @@
         jnp.bfloat16
     )
     summed = lax.psum(slots, "dp")
-    wq_full, wg_full = gather_ring([tie(w_query, slots), w_gate])
-    both_ffn = gather_all(jnp.concatenate([w_up, tie(w_down, wq_full[:8])], axis=1))
-    wu_full, wd_full = both_ffn[:, : w_up.shape[1]], both_ffn[:, w_up.shape[1] :]
-    (wo_full,) = gather_ring([tie(w_out, wq_full[:8])], 3)
+    wq_full, wg_full, wo_full = gather_ring([tie(w_query, slots), w_gate, w_out], 3)
+    wd_full = gather_all(tie(w_down, (wq_full, summed)))
     state_lookup = jnp.sum(
         summed.astype(jnp.float32) * group_onehot[:, None, None, None], axis=0
     ).astype(jnp.bfloat16)
-    queries = plain_dot(a_all, wq_full).reshape(seg_len, heads_local, DK)
+    queries = lax.optimization_barrier(plain_dot(a_all, wq_full)).reshape(seg_len, heads_local, DK)
     gate_pre = plain_dot(a_all, wg_full)
     rotated_queries = (rotate_pairs(queries, cosine, sine_tab, grow_fac) * q_scale).astype(
         jnp.bfloat16
@@ -571,7 +793,9 @@
     attn_own = scatter_rows(contract_last(gated_out, wo_full))
     hidden_res = token_rows + attn_own
     normed_two, inv_two = norm_stats(hidden_res, EPSILON)
-    c_all = gather_rows((normed_two * gain_two + bias_two).astype(jnp.bfloat16))
+    c_own = (normed_two * gain_two + bias_two).astype(jnp.bfloat16)
+    c_all = gather_rows(c_own)
+    (wu_full,) = gather_ring([tie(w_up, c_own)], 4)
     up_pre = plain_dot(c_all, wu_full)
     up_act = jax.nn.gelu(up_pre, approximate=False).astype(jnp.bfloat16)
     ffn_own = scatter_rows(contract_last(up_act, wd_full))
@@ -582,11 +806,9 @@
     grad_out = token_total / valid_count * weighted
 
     def weight_grad(feature_side, other_side, flip):
-        mine = jnp.concatenate(
-            [feature_side[:, :own_width], ring.swap(feature_side[:, own_width:])], axis=0
-        )
-        both = jnp.concatenate([other_side, ring.swap(other_side)], axis=0)
-        return RingSum(ring, contract_first(mine, both).astype(jnp.bfloat16), flip)
+        keep = contract_first(feature_side[:, :own_width], other_side).astype(jnp.bfloat16)
+        give = contract_first(feature_side[:, own_width:], other_side).astype(jnp.bfloat16)
+        return RingSum(ring, keep, ring.swap(give), flip)
 
     def in_order(rows):
         return move_blocks(rows, table, False)
@@ -596,12 +818,12 @@
 
     grad_ffn_all = gather_rows(grad_out.astype(jnp.bfloat16))
     sum_wd = weight_grad(in_order(grad_ffn_all), up_act, False)
-    grad_up_act = plain_dot(tie(grad_ffn_all, sum_wd.full[:16, :128]), wd_full)
+    grad_up_act = plain_dot(tie(grad_ffn_all, sum_wd.full), wd_full)
     _, gelu_pull = jax.vjp(lambda inner: jax.nn.gelu(inner, approximate=False), up_pre)
     grad_up = gelu_pull(grad_up_act)[0].astype(jnp.bfloat16)
     sum_wu = weight_grad(in_order(c_all), grad_up, True)
     sum_wd.run(1)
-    grad_up = tie(then(grad_up, sum_wd), sum_wu.full[:16, :128])
+    grad_up = tie(then(grad_up, sum_wd), sum_wu.full)
     grad_c_parts = contract_last(grad_up, wu_full)
     grad_c = scatter_rows(grad_c_parts)
     sum_wd.run(1)
@@ -614,7 +836,7 @@
     sum_wu.run(1)
     grad_attn_all = then(grad_attn_all, sum_wd, sum_wu)
     sum_wo = weight_grad(in_order(grad_attn_all), gated_out, False)
-    grad_attn_all = tie(grad_attn_all, sum_wo.full[:16, :128])
+    grad_attn_all = tie(grad_attn_all, sum_wo.full)
     grad_gated = plain_dot(grad_attn_all, wo_full).reshape(seg_len, heads_local, DV)
     _, silu_pull = jax.vjp(jax.nn.silu, gate_pre)
     grad_gate = silu_pull((grad_gated * grouped).reshape(seg_len, heads_local * DV))[0].astype(
@@ -630,12 +852,13 @@
         preferred_element_type=jnp.float32,
     )
     grad_slots = (group_onehot[:, None, None, None] * state_grad_own[None]).astype(jnp.bfloat16)
-    grad_summed = lax.psum(grad_slots, "dp")
+    grad_summed = ring_total(grad_slots.reshape(-1, DV)).reshape(grad_slots.shape)
+    retained_gradient = tie(retained_gradient, grad_summed)
     sum_wu.run(2)
     a_order = in_order(a_all)
-    grad_gate = tie(then(grad_gate, sum_wu), grad_slots[:, :, :8, :128])
+    grad_gate = then(grad_gate, sum_wu)
     sum_wg = weight_grad(a_order, grad_gate, True)
-    retained_gradient = tie(retained_gradient, sum_wg.full[:16, :128])
+    retained_gradient = tie(retained_gradient, sum_wg.full)
     sum_wu.run(1)
     sum_wo.run(1)
     grad_weights = jnp.einsum(
@@ -662,9 +885,6 @@
     )
     grad_queries = then(grad_queries, sum_wo)
     sum_wq = weight_grad(a_order, grad_queries, False)
-    sum_wo.run(2)
-    sum_wg.run(2)
-    grad_summed = tie(then(grad_summed, sum_wo, sum_wg), sum_wq.full[:16, :128])
     state_gradient = (
         prompt_flag
         * jnp.sum(grad_summed.astype(jnp.float32) * group_onehot[:, None, None, None], axis=0)
@@ -682,20 +902,16 @@
     )
     grad_vlow = grad_values.reshape(seg_len, heads_local * DV).astype(jnp.bfloat16)
     grad_key_value = jnp.concatenate([grad_keys, grad_vlow], axis=1)
-    sum_wg.run(1)
-    grad_key_value = then(grad_key_value, sum_wg)
     sum_wkv = weight_grad(a_order, grad_key_value, True)
-    grad_queries, grad_keys = (tie(x, sum_wkv.full[:16, :128]) for x in (grad_queries, grad_keys))
+    grad_keys = tie(grad_keys, sum_wkv.arrived)
     grad_a = scatter_rows(
         contract_last(grad_queries, wq_full)
         + contract_last(grad_gate, wg_full)
         + contract_last(grad_keys, wk_full)
         + contract_last(grad_vlow, wv_full)
     )
+    sum_wo.run(2)
     sum_wg.run(1)
-    sum_wq.run(2)
-    sum_wkv.run(1)
-    grad_a = then(grad_a, sum_wg, sum_wq, sum_wkv)
     grad_gain1_part = jnp.sum(grad_a * normed_one, axis=0)
     grad_bias1_part = jnp.sum(grad_a, axis=0)
     grad_tokens = grad_hidden + norm_back(grad_a * gain_one, normed_one, inv_one)
@@ -704,6 +920,8 @@
     totals = jnp.sum(exchange_blocks(packed(sums, squared_own)), axis=0)
     loss_value = totals[4, 0] / (valid_count * model_dim)
     key_width = w_key.shape[1]
+    sum_wg.run(2)
+    sum_wg.moving = [tie(x, totals) for x in sum_wg.moving]
     grad_wkv = sum_wkv.result()
 
     return (

time: 884 us -> 838 us (0.948)
  waiting for transfers between devices: 276 us -> 155 us
  Pallas kernels: 270 us -> 354 us
  local copies, waits for them, and re-layouts: 45 us -> 28.9 us
  other arithmetic: 93.2 us -> 104 us
    pallas_call x3 -> x4, Pallas kernels: 232 us -> 325 us  [the longest x3 281 us: gather_ring(): pl.pallas_call(kernel, out_shape=out_shape, in_specs=in_specs, out_specs=...]
    psum x1 -> x0, waiting for transfers between devices: 54.4 us -> none  [on_device(): grad_summed = lax.psum(grad_slots, 'dp')]
    all_gather x1, waiting for transfers between devices: 29.3 us -> 0.02 us  [gather_all(): return lax.all_gather(shard, 'dp', axis=0, tiled=True)]
    ppermute x8 -> x7, waiting for transfers between devices: 54.9 us -> 29.9 us  [swap_mp(): return lax.ppermute(rows, 'mp', [(0, 1), (1, 0)])]
    convert_element_type x20 -> x26, other arithmetic: 26.7 us -> 45.9 us  [the longest x14 29 us: step(): moved = (moved.astype(jnp.float32) + self.term(k)).astype(jnp.bfloat16)]
    dot_general x6 -> x12, matrix products: 23.3 us -> 36.5 us  [contract_first(): lax.dot_general(first_op, second_op, (((0,), (0,)), ((), ())), preferred_...]
    ppermute x42, waiting for transfers between devices: 137 us -> 125 us  [shift(): return lax.ppermute(rows, 'dp', pairs)]
    dot_general x7, matrix products: 49.5 us -> 40.3 us  [plain_dot(): return jnp.dot(first_op, second_op, preferred_element_type=jnp.float32)]
  transfers between devices with their start and end apart: 63 -> 57, of which waited for: 32 -> 30; matrix products, arithmetic and copies ran while one was open for 20% -> 22% of each run, Pallas kernels for 29% -> 33%
where the time goes in v3:
time: 838 us; the launch traced here: 828 us
  Pallas kernels  354 us (42%)
  waiting for transfers between devices  155 us (18%)
  matrix products  111 us (13%)
  other arithmetic  104 us (12%)
  starting transfers between devices  55 us (7%)
  local copies, waits for them, and re-layouts  28.9 us (3%)
  between operations  20.9 us (2%)
    pallas_call x3, Pallas kernels, gather_ring(): pl.pallas_call(kernel, out_shape=out_shape, in_specs=in_specs, out_specs=...  281 us
    ppermute x42, waiting for transfers between devices, shift(): return lax.ppermute(rows, 'dp', pairs)  125 us
    ppermute x42, starting transfers between devices, shift(): return lax.ppermute(rows, 'dp', pairs)  45.2 us
    pallas_call x1, Pallas kernels, ring_total(): pl.pallas_call(kernel, out_shape=jax.ShapeDtypeStruct(shape, low), in_spe...  43.7 us
    dot_general x7, matrix products, plain_dot(): return jnp.dot(first_op, second_op, preferred_element_type=jnp.float32)  40.3 us
    dot_general x12, matrix products, contract_first(): lax.dot_general(first_op, second_op, (((0,), (0,)), ((), ())), preferred_...  36.5 us
    ppermute x7, waiting for transfers between devices, swap_mp(): return lax.ppermute(rows, 'mp', [(0, 1), (1, 0)])  29.9 us
    convert_element_type x14, other arithmetic, step(): moved = (moved.astype(jnp.float32) + self.term(k)).astype(jnp.bfloat16)  29 us
  transfers between devices with their start and end apart: 57, of which 30 were waited for; matrix products, arithmetic and copies ran while one was open for 22% of the time, Pallas kernels for 33%

profile of v3, /device:TPU:0, one launch (start us, length us, event | category | flops | bytes accessed | tf_op | source)
XLA Modules:
  0.0 828.5 jit_solution(17018780933082594272)
XLA Ops:
  19.5 75.1 %shard_map.263 = (bf16[2048,1024]{1,0:T(8,128)(2,1)}, bf16[2048,2048]{1,0:T(8,128)(2,1)}, f32[32,8,128]{2,1,0:T(8,128)}, bf16[2,128,2048]{2,1,0:T(8,128)(2,1)}) custom-call(bf16[128,1024]{1,0:T(8,128)(2,1)} %refs_0_.1, bf16[128,2048]{1,0:T(8,128)(2,1)} %refs_1_.2, f32[16,8,128]{2,1,0:T(8,128)} %concatenate.73.refs_2_, bf16[128,2048]{1,0:T(8,128)(2,1)} %refs_3_.1), custom_call_target="tpu_custom_call" | custom-call | bytes 50331648 | tf_op jit(solution)/shard_map/pallas_call | solution.py:353
  94.7 6.2 convolution_convert_fusion.10
  107.1 139.1 %shard_map.264 = (bf16[2048,1024]{1,0:T(8,128)(2,1)}, bf16[2048,2048]{1,0:T(8,128)(2,1)}, bf16[2048,2048]{1,0:T(8,128)(2,1)}) custom-call(bf16[128,1024]{1,0:T(8,128)(2,1)} %refs_0_.2, bf16[128,2048]{1,0:T(8,128)(2,1)} %refs_1_.3, bf16[128,2048]{1,0:T(8,128)(2,1)} %refs_2_.1), custom_call_target="tpu_custom_call" | custom-call | bytes 83886080 | tf_op jit(solution)/shard_map/pallas_call | solution.py:353
  246.3 7.7 fusion.13
  257.1 4.4 fusion.84
  276.1 12.0 %collective-permute-done = bf16[128,2048]{1,0:T(8,128)(2,1)S(1)} collective-permute-done((bf16[128,2048]{1,0:T(8,128)(2,1)S(1)}, bf16[128,2048]{1,0:T(8,128)(2,1)S(1)}, u32[]{:S(2)}, u32[]{:S(2)}) %collective-permute-start) | collective-permute-done | bytes 524320 | tf_op jit(solution)/shard_map/ppermute | solution.py:634
  291.0 66.9 %shard_map.265 = bf16[2048,2048]{1,0:T(8,128)(2,1)} custom-call(bf16[128,2048]{1,0:T(8,128)(2,1)} %refs_0_.3), custom_call_target="tpu_custom_call" | custom-call | bytes 33554432 | tf_op jit(solution)/shard_map/pallas_call | solution.py:353
  357.9 10.8 %multiply_convert_fusion.4 = (bf16[256,2048]{1,0:T(8,128)(2,1)}, f32[256,2048]{1,0:T(8,128)}, f32[256,2048]{1,0:T(8,128)}) fusion(bf16[2048,2048]{1,0:T(8,128)(2,1)} %shard_map.265, bf16[128,2048]{1,0:T(8,128)(2,1)} %collective-permute-done.1, bf16[128,2048]{1,0:T(8,128)(2,1)} %add_convert_fusion.36), kind=kOutput, calls=%fused_computation.33 | convolution fusion | flops 2183659520 | bytes 14680064 | tf_op jit(solution)/shard_map/dot_general | solution.py:75
  368.8 6.1 fusion.86
  380.7 10.8 %collective-permute-done.2 = bf16[128,2048]{1,0:T(8,128)(2,1)} collective-permute-done((bf16[128,2048]{1,0:T(8,128)(2,1)}, bf16[128,2048]{1,0:T(8,128)(2,1)}, u32[]{:S(2)}, u32[]{:S(2)}) %collective-permute-start.2) | collective-permute-done | bytes 524320 | tf_op jit(solution)/shard_map/ppermute | solution.py:634
  403.0 6.7 collective-permute-done.3
  414.6 4.8 convolution_convert_fusion.9
  422.7 6.5 add_convert_fusion
  444.8 6.8 collective-permute-done.5
  463.3 4.8 collective-permute-done.8
  485.9 6.7 collective-permute-done.11
  510.8 3.8 collective-permute-done.12
  518.4 4.5 convolution_convert_fusion.5
  544.4 43.7 %shard_map.270 = bf16[2,8,128,512]{3,2,1,0:T(8,128)(2,1)} custom-call(bf16[2,8,128,512]{3,2,1,0:T(8,128)(2,1)} %multiply_convert_fusion.in_ref), custom_call_target="tpu_custom_call" | custom-call | tf_op jit(solution)/shard_map/pallas_call | solution.py:502
  599.8 11.8 %collective-permute-done.23 = bf16[128,2048]{1,0:T(8,128)(2,1)S(1)} collective-permute-done((bf16[128,2048]{1,0:T(8,128)(2,1)S(1)}, bf16[128,2048]{1,0:T(8,128)(2,1)S(1)}, u32[]{:S(2)}, u32[]{:S(2)}) %collective-permute-start.23) | collective-permute-done | bytes 524320 | tf_op jit(solution)/shard_map/ppermute | solution.py:109
  615.7 7.1 fusion.91
  633.7 4.5 convolution_convert_fusion.1
  645.4 9.0 %collective-permute-done.48 = bf16[128,2048]{1,0:T(8,128)(2,1)S(1)} collective-permute-done((bf16[128,2048]{1,0:T(8,128)(2,1)S(1)}, bf16[128,2048]{1,0:T(8,128)(2,1)S(1)}, u32[]{:S(2)}, u32[]{:S(2)}) %collective-permute-start.48) | collective-permute-done | bytes 524320 | tf_op jit(solution)/shard_map/ppermute | solution.py:109
  661.5 4.2 collective-permute-done.26
  672.2 4.3 collective-permute-done.49
  688.3 6.3 convolution_add_fusion.1
  714.6 14.4 %collective-permute-done.53 = bf16[128,2048]{1,0:T(8,128)(2,1)S(1)} collective-permute-done((bf16[128,2048]{1,0:T(8,128)(2,1)S(1)}, bf16[128,2048]{1,0:T(8,128)(2,1)S(1)}, u32[]{:S(2)}, u32[]{:S(2)}) %collective-permute-start.53) | collective-permute-done | bytes 524320 | tf_op jit(solution)/shard_map/ppermute | solution.py:109
  747.6 10.3 %collective-permute-done.37 = bf16[128,3072]{1,0:T(8,128)(2,1)S(1)} collective-permute-done((bf16[128,3072]{1,0:T(8,128)(2,1)S(1)}, bf16[128,3072]{1,0:T(8,128)(2,1)S(1)}, u32[]{:S(2)}, u32[]{:S(2)}) %collective-permute-start.37) | collective-permute-done | bytes 786464 | tf_op jit(solution)/shard_map/ppermute | solution.py:109
  765.1 18.9 %shard_map.271 = f32[32,8,128]{2,1,0:T(8,128)} custom-call(f32[16,8,128]{2,1,0:T(8,128)} %concatenate.84.in_ref), custom_call_target="tpu_custom_call" | custom-call | tf_op jit(solution)/shard_map/pallas_call | solution.py:586
  786.7 4.4 add_convert_fusion.5
  796.3 3.8 collective-permute-done.51
  802.9 13.2 %collective-permute-done.43 = bf16[128,3072]{1,0:T(8,128)(2,1)} collective-permute-done((bf16[128,3072]{1,0:T(8,128)(2,1)}, bf16[128,3072]{1,0:T(8,128)(2,1)}, u32[]{:S(2)}, u32[]{:S(2)}) %collective-permute-start.43) | collective-permute-done | bytes 786464 | tf_op jit(solution)/shard_map/ppermute | solution.py:109
  (429 shorter events, 267.9 us)
Async XLA Ops:
  7.2 239.1 %all-reduce.4.cloned.1.call-start = ((), (), s32[]{:S(2)}) async-start(), calls=%async_computation | async-start | bytes 4194304 | tf_op jit(solution)/shard_map/psum | solution.py:768
  107.1 261.7 %all-gather.2.cloned.1.call-start = ((), (), s32[]{:S(2)}) async-start(), calls=%async_computation.1 | async-start | bytes 8912896 | tf_op jit(solution)/shard_map/all_gather | solution.py:720
  290.4 67.6 %collective-permute-start.1 = (bf16[128,2048]{1,0:T(8,128)(2,1)}, bf16[128,2048]{1,0:T(8,128)(2,1)}, u32[]{:S(2)}, u32[]{:S(2)}) collective-permute-start(bf16[128,2048]{1,0:T(8,128)(2,1)} %add_convert_fusion.36), channel_id=1, source_target_pairs={{0,1},{1,0},{2,3},{3,2},{4,5},{5,4},{6,7},{7,6},{8,9},{9,8},{10,11... | collective-permute-start | bytes 1572872 | tf_op jit(solution)/shard_map/ppermute | solution.py:634
  461.2 20.8 %collective-permute-start.19 = (bf16[128,2048]{1,0:T(8,128)(2,1)S(1)}, bf16[128,2048]{1,0:T(8,128)(2,1)S(1)}, u32[]{:S(2)}, u32[]{:S(2)}) collective-permute-start(bf16[128,2048]{1,0:T(8,128)(2,1)S(1)} %get-tuple-element.105), channel_id=1, source_target_pairs={{0,4},{2,6},{8,0},{10,2},{16,8},{18,10},{24,16},{26,18},{28,24},{3... | collective-permute-start | bytes 1572872 | tf_op jit(solution)/shard_map/ppermute | solution.py:109
  461.3 20.7 %collective-permute-start.15 = (bf16[128,2048]{1,0:T(8,128)(2,1)S(1)}, bf16[128,2048]{1,0:T(8,128)(2,1)S(1)}, u32[]{:S(2)}, u32[]{:S(2)}) collective-permute-start(bf16[128,2048]{1,0:T(8,128)(2,1)S(1)} %get-tuple-element.106), channel_id=1, source_target_pairs={{0,8},{2,10},{8,16},{10,18},{16,24},{18,26},{24,28},{26,30},{28,20... | collective-permute-start | bytes 1572872 | tf_op jit(solution)/shard_map/ppermute | solution.py:109
  473.5 19.7 %collective-permute-start.9 = (bf16[128,2048]{1,0:T(8,128)(2,1)}, bf16[128,2048]{1,0:T(8,128)(2,1)S(1)}, u32[]{:S(2)}, u32[]{:S(2)}) collective-permute-start(bf16[128,2048]{1,0:T(8,128)(2,1)} %get-tuple-element.110), channel_id=1, source_target_pairs={{0,4},{2,6},{8,0},{10,2},{16,8},{18,10},{24,16},{26,18},{28,24},{3... | collective-permute-start | bytes 1572872 | tf_op jit(solution)/shard_map/ppermute | solution.py:109
  476.0 19.1 %collective-permute-start.7 = (bf16[128,2048]{1,0:T(8,128)(2,1)S(1)}, bf16[128,2048]{1,0:T(8,128)(2,1)S(1)}, u32[]{:S(2)}, u32[]{:S(2)}) collective-permute-start(bf16[128,2048]{1,0:T(8,128)(2,1)S(1)} %slice.819), channel_id=1, source_target_pairs={{0,1},{1,0},{2,3},{3,2},{4,5},{5,4},{6,7},{7,6},{8,9},{9,8},{10,11... | collective-permute-start | bytes 1572872 | tf_op jit(solution)/shard_map/ppermute | solution.py:634
  483.8 20.7 %collective-permute-start.20 = (bf16[128,2048]{1,0:T(8,128)(2,1)S(1)}, bf16[128,2048]{1,0:T(8,128)(2,1)S(1)}, u32[]{:S(2)}, u32[]{:S(2)}) collective-permute-start(bf16[128,2048]{1,0:T(8,128)(2,1)S(1)} %get-tuple-element.103), channel_id=1, source_target_pairs={{0,4},{2,6},{8,0},{10,2},{16,8},{18,10},{24,16},{26,18},{28,24},{3... | collective-permute-start | bytes 1572872 | tf_op jit(solution)/shard_map/ppermute | solution.py:109
  483.9 20.6 %collective-permute-start.17 = (bf16[128,2048]{1,0:T(8,128)(2,1)S(1)}, bf16[128,2048]{1,0:T(8,128)(2,1)S(1)}, u32[]{:S(2)}, u32[]{:S(2)}) collective-permute-start(bf16[128,2048]{1,0:T(8,128)(2,1)S(1)} %get-tuple-element.104), channel_id=1, source_target_pairs={{0,8},{2,10},{8,16},{10,18},{16,24},{18,26},{24,28},{26,30},{28,20... | collective-permute-start | bytes 1572872 | tf_op jit(solution)/shard_map/ppermute | solution.py:109
  495.1 20.8 %collective-permute-start.13 = (bf16[128,2048]{1,0:T(8,128)(2,1)S(1)}, bf16[128,2048]{1,0:T(8,128)(2,1)}, u32[]{:S(2)}, u32[]{:S(2)}) collective-permute-start(bf16[128,2048]{1,0:T(8,128)(2,1)S(1)} %get-tuple-element.108), channel_id=1, source_target_pairs={{0,4},{2,6},{8,0},{10,2},{16,8},{18,10},{24,16},{26,18},{28,24},{3... | collective-permute-start | bytes 1572872 | tf_op jit(solution)/shard_map/ppermute | solution.py:109
  507.2 31.1 %collective-permute-start.18 = (bf16[128,2048]{1,0:T(8,128)(2,1)}, bf16[128,2048]{1,0:T(8,128)(2,1)}, u32[]{:S(2)}, u32[]{:S(2)}) collective-permute-start(bf16[128,2048]{1,0:T(8,128)(2,1)} %get-tuple-element.102), channel_id=1, source_target_pairs={{0,8},{2,10},{8,16},{10,18},{16,24},{18,26},{24,28},{26,30},{28,20... | collective-permute-start | bytes 1572872 | tf_op jit(solution)/shard_map/ppermute | solution.py:109
  507.4 122.9 %collective-permute-start.21 = (bf16[128,2048]{1,0:T(8,128)(2,1)}, bf16[128,2048]{1,0:T(8,128)(2,1)}, u32[]{:S(2)}, u32[]{:S(2)}) collective-permute-start(bf16[128,2048]{1,0:T(8,128)(2,1)} %get-tuple-element.101), channel_id=1, source_target_pairs={{0,4},{2,6},{8,0},{10,2},{16,8},{18,10},{24,16},{26,18},{28,24},{3... | collective-permute-start | bytes 1572872 | tf_op jit(solution)/shard_map/ppermute | solution.py:109
  531.5 63.7 %collective-permute-start.22 = (bf16[1024,2048]{1,0:T(8,128)(2,1)}, bf16[1024,2048]{1,0:T(8,128)(2,1)}, u32[]{:S(2)}, u32[]{:S(2)}) collective-permute-start(bf16[1024,2048]{1,0:T(8,128)(2,1)} %convolution_convert_fusion.3), channel_id=1, source_target_pairs={{0,2},{2,0},{4,6},{6,4},{8,10},{10,8},{12,14},{14,12},{16,18},{18,... | collective-permute-start | bytes 12582920 | tf_op jit(solution)/shard_map/ppermute | solution.py:112
  591.4 46.8 %collective-permute-start.44 = (bf16[1024,2048]{1,0:T(8,128)(2,1)}, bf16[1024,2048]{1,0:T(8,128)(2,1)}, u32[]{:S(2)}, u32[]{:S(2)}) collective-permute-start(bf16[1024,2048]{1,0:T(8,128)(2,1)} %convolution_convert_fusion.2), channel_id=1, source_target_pairs={{0,2},{2,0},{4,6},{6,4},{8,10},{10,8},{12,14},{14,12},{16,18},{18,... | collective-permute-start | bytes 12582920 | tf_op jit(solution)/shard_map/ppermute | solution.py:112
  638.2 72.8 %collective-permute-start.27 = (bf16[1024,3072]{1,0:T(8,128)(2,1)}, bf16[1024,3072]{1,0:T(8,128)(2,1)}, u32[]{:S(2)}, u32[]{:S(2)}) collective-permute-start(bf16[1024,3072]{1,0:T(8,128)(2,1)} %convolution_convert_fusion.1), channel_id=1, source_target_pairs={{0,2},{2,0},{4,6},{6,4},{8,10},{10,8},{12,14},{14,12},{16,18},{18,... | collective-permute-start | bytes 18874376 | tf_op jit(solution)/shard_map/ppermute | solution.py:112
  643.4 22.3 %collective-permute-start.26 = (bf16[128,2048]{1,0:T(8,128)(2,1)}, bf16[128,2048]{1,0:T(8,128)(2,1)}, u32[]{:S(2)}, u32[]{:S(2)}) collective-permute-start(bf16[128,2048]{1,0:T(8,128)(2,1)} %get-tuple-element.98), channel_id=1, source_target_pairs={{0,4},{2,6},{8,0},{10,2},{16,8},{18,10},{24,16},{26,18},{28,24},{3... | collective-permute-start | bytes 1572872 | tf_op jit(solution)/shard_map/ppermute | solution.py:109
  658.5 18.0 %collective-permute-start.49 = (bf16[128,2048]{1,0:T(8,128)(2,1)}, bf16[128,2048]{1,0:T(8,128)(2,1)}, u32[]{:S(2)}, u32[]{:S(2)}) collective-permute-start(bf16[128,2048]{1,0:T(8,128)(2,1)} %get-tuple-element.96), channel_id=1, source_target_pairs={{0,4},{2,6},{8,0},{10,2},{16,8},{18,10},{24,16},{26,18},{28,24},{3... | collective-permute-start | bytes 1572872 | tf_op jit(solution)/shard_map/ppermute | solution.py:109
  668.9 18.3 %collective-permute-start.29 = (bf16[1024,1024]{1,0:T(8,128)(2,1)S(1)}, bf16[1024,1024]{1,0:T(8,128)(2,1)S(1)}, u32[]{:S(2)}, u32[]{:S(2)}) collective-permute-start(bf16[1024,1024]{1,0:T(8,128)(2,1)S(1)} %convolution_convert_fusion.11), channel_id=1, source_target_pairs={{0,2},{2,0},{4,6},{6,4},{8,10},{10,8},{12,14},{14,12},{16,18},{18,... | collective-permute-start | bytes 6291464 | tf_op jit(solution)/shard_map/ppermute | solution.py:112
  678.6 20.6 %collective-permute-start.46 = (bf16[128,2048]{1,0:T(8,128)(2,1)S(1)}, bf16[128,2048]{1,0:T(8,128)(2,1)S(1)}, u32[]{:S(2)}, u32[]{:S(2)}) collective-permute-start(bf16[128,2048]{1,0:T(8,128)(2,1)S(1)} %get-tuple-element.93), channel_id=1, source_target_pairs={{0,8},{2,10},{8,16},{10,18},{16,24},{18,26},{24,28},{26,30},{28,20... | collective-permute-start | bytes 1572872 | tf_op jit(solution)/shard_map/ppermute | solution.py:109
  679.8 20.2 %collective-permute-start.50 = (bf16[128,2048]{1,0:T(8,128)(2,1)S(1)}, bf16[128,2048]{1,0:T(8,128)(2,1)S(1)}, u32[]{:S(2)}, u32[]{:S(2)}) collective-permute-start(bf16[128,2048]{1,0:T(8,128)(2,1)S(1)} %get-tuple-element.94), channel_id=1, source_target_pairs={{0,4},{2,6},{8,0},{10,2},{16,8},{18,10},{24,16},{26,18},{28,24},{3... | collective-permute-start | bytes 1572872 | tf_op jit(solution)/shard_map/ppermute | solution.py:109
  682.7 31.0 %collective-permute-start.54 = (bf16[128,2048]{1,0:T(8,128)(2,1)S(1)}, bf16[128,2048]{1,0:T(8,128)(2,1)S(1)}, u32[]{:S(2)}, u32[]{:S(2)}) collective-permute-start(bf16[128,2048]{1,0:T(8,128)(2,1)S(1)} %get-tuple-element.90), channel_id=1, source_target_pairs={{0,4},{2,6},{8,0},{10,2},{16,8},{18,10},{24,16},{26,18},{28,24},{3... | collective-permute-start | bytes 1572872 | tf_op jit(solution)/shard_map/ppermute | solution.py:109
  702.7 92.4 %collective-permute-start.47 = (bf16[128,2048]{1,0:T(8,128)(2,1)}, bf16[128,2048]{1,0:T(8,128)(2,1)}, u32[]{:S(2)}, u32[]{:S(2)}) collective-permute-start(bf16[128,2048]{1,0:T(8,128)(2,1)} %get-tuple-element.91), channel_id=1, source_target_pairs={{0,8},{2,10},{8,16},{10,18},{16,24},{18,26},{24,28},{26,30},{28,20... | collective-permute-start | bytes 1572872 | tf_op jit(solution)/shard_map/ppermute | solution.py:109
  706.3 22.7 %collective-permute-start.53 = (bf16[128,2048]{1,0:T(8,128)(2,1)S(1)}, bf16[128,2048]{1,0:T(8,128)(2,1)S(1)}, u32[]{:S(2)}, u32[]{:S(2)}) collective-permute-start(bf16[128,2048]{1,0:T(8,128)(2,1)S(1)} %get-tuple-element.89), channel_id=1, source_target_pairs={{0,8},{2,10},{8,16},{10,18},{16,24},{18,26},{24,28},{26,30},{28,20... | collective-permute-start | bytes 1572872 | tf_op jit(solution)/shard_map/ppermute | solution.py:109
  710.3 22.8 %collective-permute-start.32 = (bf16[128,1024]{1,0:T(8,128)(2,1)S(1)}, bf16[128,1024]{1,0:T(8,128)(2,1)S(1)}, u32[]{:S(2)}, u32[]{:S(2)}) collective-permute-start(bf16[128,1024]{1,0:T(8,128)(2,1)S(1)} %get-tuple-element.116), channel_id=1, source_target_pairs={{0,8},{2,10},{8,16},{10,18},{16,24},{18,26},{24,28},{26,30},{28,20... | collective-permute-start | bytes 786440 | tf_op jit(solution)/shard_map/ppermute | solution.py:109
  711.0 22.1 %collective-permute-start.35 = (bf16[128,1024]{1,0:T(8,128)(2,1)S(1)}, bf16[128,1024]{1,0:T(8,128)(2,1)S(1)}, u32[]{:S(2)}, u32[]{:S(2)}) collective-permute-start(bf16[128,1024]{1,0:T(8,128)(2,1)S(1)} %get-tuple-element.117), channel_id=1, source_target_pairs={{0,4},{2,6},{8,0},{10,2},{16,8},{18,10},{24,16},{26,18},{28,24},{3... | collective-permute-start | bytes 786440 | tf_op jit(solution)/shard_map/ppermute | solution.py:109
  713.7 21.8 %collective-permute-start.40 = (bf16[128,3072]{1,0:T(8,128)(2,1)S(1)}, bf16[128,3072]{1,0:T(8,128)(2,1)S(1)}, u32[]{:S(2)}, u32[]{:S(2)}) collective-permute-start(bf16[128,3072]{1,0:T(8,128)(2,1)S(1)} %add_convert_fusion.4), channel_id=1, source_target_pairs={{0,4},{2,6},{8,0},{10,2},{16,8},{18,10},{24,16},{26,18},{28,24},{3... | collective-permute-start | bytes 2359304 | tf_op jit(solution)/shard_map/ppermute | solution.py:109
  737.6 20.2 %collective-permute-start.37 = (bf16[128,3072]{1,0:T(8,128)(2,1)S(1)}, bf16[128,3072]{1,0:T(8,128)(2,1)S(1)}, u32[]{:S(2)}, u32[]{:S(2)}) collective-permute-start(bf16[128,3072]{1,0:T(8,128)(2,1)S(1)} %get-tuple-element.87), channel_id=1, source_target_pairs={{0,8},{2,10},{8,16},{10,18},{16,24},{18,26},{24,28},{26,30},{28,20... | collective-permute-start | bytes 2359304 | tf_op jit(solution)/shard_map/ppermute | solution.py:109
  738.9 19.0 %collective-permute-start.41 = (bf16[128,3072]{1,0:T(8,128)(2,1)S(1)}, bf16[128,3072]{1,0:T(8,128)(2,1)S(1)}, u32[]{:S(2)}, u32[]{:S(2)}) collective-permute-start(bf16[128,3072]{1,0:T(8,128)(2,1)S(1)} %get-tuple-element.88), channel_id=1, source_target_pairs={{0,4},{2,6},{8,0},{10,2},{16,8},{18,10},{24,16},{26,18},{28,24},{3... | collective-permute-start | bytes 2359304 | tf_op jit(solution)/shard_map/ppermute | solution.py:109
  761.1 25.5 %collective-permute-start.38 = (bf16[128,3072]{1,0:T(8,128)(2,1)}, bf16[128,3072]{1,0:T(8,128)(2,1)}, u32[]{:S(2)}, u32[]{:S(2)}) collective-permute-start(bf16[128,3072]{1,0:T(8,128)(2,1)} %get-tuple-element.85), channel_id=1, source_target_pairs={{0,8},{2,10},{8,16},{10,18},{16,24},{18,26},{24,28},{26,30},{28,20... | collective-permute-start | bytes 2359304 | tf_op jit(solution)/shard_map/ppermute | solution.py:109
  762.2 24.5 %collective-permute-start.42 = (bf16[128,3072]{1,0:T(8,128)(2,1)}, bf16[128,3072]{1,0:T(8,128)(2,1)}, u32[]{:S(2)}, u32[]{:S(2)}) collective-permute-start(bf16[128,3072]{1,0:T(8,128)(2,1)} %get-tuple-element.86), channel_id=1, source_target_pairs={{0,4},{2,6},{8,0},{10,2},{16,8},{18,10},{24,16},{26,18},{28,24},{3... | collective-permute-start | bytes 2359304 | tf_op jit(solution)/shard_map/ppermute | solution.py:109
  791.1 25.0 %collective-permute-start.43 = (bf16[128,3072]{1,0:T(8,128)(2,1)}, bf16[128,3072]{1,0:T(8,128)(2,1)}, u32[]{:S(2)}, u32[]{:S(2)}) collective-permute-start(bf16[128,3072]{1,0:T(8,128)(2,1)} %get-tuple-element.84), channel_id=1, source_target_pairs={{0,4},{2,6},{8,0},{10,2},{16,8},{18,10},{24,16},{26,18},{28,24},{3... | collective-permute-start | bytes 2359304 | tf_op jit(solution)/shard_map/ppermute | solution.py:109
  792.0 24.1 %collective-permute-start.39 = (bf16[128,3072]{1,0:T(8,128)(2,1)}, bf16[128,3072]{1,0:T(8,128)(2,1)}, u32[]{:S(2)}, u32[]{:S(2)}) collective-permute-start(bf16[128,3072]{1,0:T(8,128)(2,1)} %get-tuple-element.83), channel_id=1, source_target_pairs={{0,8},{2,10},{8,16},{10,18},{16,24},{18,26},{24,28},{26,30},{28,20... | collective-permute-start | bytes 2359304 | tf_op jit(solution)/shard_map/ppermute | solution.py:109
  (114 other events, 2218.7 us)
Sparse Core Ops, SparseCore 0:
  107.2 110.0 all-reduce.3
  246.4 88.5 all-gather.1

commit v4 on v3

--- a/solution.py
+++ b/solution.py
@@ -644,6 +644,13 @@
     return terms[:half_rows] + arrived.astype(jnp.float32)
 
 
+def scatter_product(rows, weight):
+    half_rows = rows.shape[0] // 2
+    far = contract_last(rows[half_rows:], weight).astype(jnp.bfloat16)
+    near = contract_last(tie(rows, far)[:half_rows], weight)
+    return near + swap_mp(far).astype(jnp.float32)
+
+
 def tie(value, other):
     return lax.optimization_barrier((value, other))[0]
 
@@ -701,7 +708,8 @@
         return jnp.concatenate([split, extra], axis=1)
 
     vectors = jnp.stack([ln1_gain, ln1_bias, ln2_gain, ln2_bias]).astype(jnp.float32)
-    blocks_own = packed(jnp.tile(vectors, (1, ring.devices)), jnp.sum(loss_mask))
+    ones_own = jnp.sum(valid_mask).astype(jnp.float32)
+    blocks_own = packed(jnp.tile(vectors, (1, ring.devices)), ones_own)
     inside = block == 128
     if inside:
         wk_full, wv_full, from_all, a_pair = gather_ring(
@@ -710,7 +718,14 @@
         a_all = a_pair.reshape(seg_len, model_dim)
     else:
         from_all = exchange_blocks(blocks_own)
-    valid_count = jnp.sum(from_all[:, 4, 0])
+    ones = jnp.sum(from_all[:, 4, 0].reshape(ring.devices, -1), axis=1)
+    same_group = group_of[:, None] == group_of[None, :]
+    firsts = jnp.min(jnp.where(same_group, segment_ids[None, :], seg_count), axis=1)
+    group_ids = jnp.arange(group_count, dtype=jnp.int32)
+    sizes = jnp.sum(
+        jnp.where(group_of[:, None] == group_ids[None, :], prompt_len[None, :], 0), axis=1
+    ).astype(jnp.float32)
+    valid_count = jnp.sum(jnp.where(firsts == segment_ids, jnp.minimum(ones, sizes), ones))
     by_row = from_all.reshape(ring.devices, -1, 8, 128)[:, 0, :4, :block]
     gain_one, bias_one, gain_two, bias_two = (
         by_row[:, i].reshape(1, model_dim) for i in range(4)
@@ -772,7 +787,7 @@
         summed.astype(jnp.float32) * group_onehot[:, None, None, None], axis=0
     ).astype(jnp.bfloat16)
     queries = lax.optimization_barrier(plain_dot(a_all, wq_full)).reshape(seg_len, heads_local, DK)
-    gate_pre = plain_dot(a_all, wg_full)
+    gate_pre = lax.optimization_barrier(plain_dot(a_all, wg_full))
     rotated_queries = (rotate_pairs(queries, cosine, sine_tab, grow_fac) * q_scale).astype(
         jnp.bfloat16
     )
@@ -790,7 +805,7 @@
     grouped, inv_group = norm_stats(retained_output, GROUP_EPSILON)
     gate_act = jax.nn.silu(gate_pre).reshape(seg_len, heads_local, DV)
     gated_out = (gate_act * grouped).reshape(seg_len, heads_local * DV).astype(jnp.bfloat16)
-    attn_own = scatter_rows(contract_last(gated_out, wo_full))
+    attn_own = scatter_product(gated_out, wo_full)
     hidden_res = token_rows + attn_own
     normed_two, inv_two = norm_stats(hidden_res, EPSILON)
     c_own = (normed_two * gain_two + bias_two).astype(jnp.bfloat16)
@@ -798,7 +813,7 @@
     (wu_full,) = gather_ring([tie(w_up, c_own)], 4)
     up_pre = plain_dot(c_all, wu_full)
     up_act = jax.nn.gelu(up_pre, approximate=False).astype(jnp.bfloat16)
-    ffn_own = scatter_rows(contract_last(up_act, wd_full))
+    ffn_own = scatter_product(up_act, wd_full)
     block_out = hidden_res + ffn_own
     error_rows = block_out - teacher_rows
     weighted = loss_mask[:, None] * error_rows

time: 838 us -> 835 us (level)
    dot_general x7 -> x9, matrix products: 28.3 us -> 44.6 us  [contract_last(): lax.dot_general(first_op, second_op, (((1,), (1,)), ((), ())), preferred_...]
  transfers between devices with their start and end apart: 57 -> 57, of which waited for: 30 -> 28; matrix products, arithmetic and copies ran while one was open for 22% -> 23% of each run, Pallas kernels for 33% -> 33%
where the time goes in v4:
time: 835 us; the launch traced here: 825 us
  Pallas kernels  346 us (41%)
  waiting for transfers between devices  156 us (19%)
  matrix products  115 us (14%)
  other arithmetic  99.4 us (12%)
  starting transfers between devices  54.1 us (6%)
  local copies, waits for them, and re-layouts  32.5 us (4%)
  between operations  21.5 us (3%)
    pallas_call x3, Pallas kernels, gather_ring(): pl.pallas_call(kernel, out_shape=out_shape, in_specs=in_specs, out_specs=...  273 us
    ppermute x42, waiting for transfers between devices, shift(): return lax.ppermute(rows, 'dp', pairs)  122 us
    ppermute x42, starting transfers between devices, shift(): return lax.ppermute(rows, 'dp', pairs)  45.6 us
    dot_general x9, matrix products, contract_last(): lax.dot_general(first_op, second_op, (((1,), (1,)), ((), ())), preferred_...  44.6 us
    pallas_call x1, Pallas kernels, ring_total(): pl.pallas_call(kernel, out_shape=jax.ShapeDtypeStruct(shape, low), in_spe...  44.3 us
    dot_general x7, matrix products, plain_dot(): return jnp.dot(first_op, second_op, preferred_element_type=jnp.float32)  35.4 us
    ppermute x7, waiting for transfers between devices, swap_mp(): return lax.ppermute(rows, 'mp', [(0, 1), (1, 0)])  30.8 us
    dot_general x12, matrix products, contract_first(): lax.dot_general(first_op, second_op, (((0,), (0,)), ((), ())), preferred_...  28.9 us
  transfers between devices with their start and end apart: 57, of which 28 were waited for; matrix products, arithmetic and copies ran while one was open for 23% of the time, Pallas kernels for 33%

profile of v4, /device:TPU:0, one launch (start us, length us, event | category | flops | bytes accessed | tf_op | source)
XLA Modules:
  0.0 824.9 jit_solution(6340643223987905609)
XLA Ops:
  18.4 75.1 %shard_map.263 = (bf16[2048,1024]{1,0:T(8,128)(2,1)}, bf16[2048,2048]{1,0:T(8,128)(2,1)}, f32[32,8,128]{2,1,0:T(8,128)}, bf16[2,128,2048]{2,1,0:T(8,128)(2,1)}) custom-call(bf16[128,1024]{1,0:T(8,128)(2,1)} %refs_0_.1, bf16[128,2048]{1,0:T(8,128)(2,1)} %refs_1_.2, f32[16,8,128]{2,1,0:T(8,128)} %concatenate.73.refs_2_, bf16[128,2048]{1,0:T(8,128)(2,1)} %refs_3_.1), custom_call_target="tpu_custom_call" | custom-call | bytes 50331648 | tf_op jit(solution)/shard_map/pallas_call | solution.py:353
  93.6 6.2 convolution_convert_fusion.10
  107.2 139.1 %shard_map.264 = (bf16[2048,1024]{1,0:T(8,128)(2,1)}, bf16[2048,2048]{1,0:T(8,128)(2,1)}, bf16[2048,2048]{1,0:T(8,128)(2,1)}) custom-call(bf16[128,1024]{1,0:T(8,128)(2,1)} %refs_0_.2, bf16[128,2048]{1,0:T(8,128)(2,1)} %refs_1_.3, bf16[128,2048]{1,0:T(8,128)(2,1)} %refs_2_.1), custom_call_target="tpu_custom_call" | custom-call | bytes 83886080 | tf_op jit(solution)/shard_map/pallas_call | solution.py:353
  246.3 6.0 fusion.92
  257.8 4.8 fusion.93
  277.4 12.1 %collective-permute-done = bf16[128,2048]{1,0:T(8,128)(2,1)S(1)} collective-permute-done((bf16[128,2048]{1,0:T(8,128)(2,1)S(1)}, bf16[128,2048]{1,0:T(8,128)(2,1)S(1)}, u32[]{:S(2)}, u32[]{:S(2)}) %collective-permute-start) | collective-permute-done | bytes 524320 | tf_op jit(solution)/shard_map/ppermute | solution.py:634
  298.8 59.1 %shard_map.265 = bf16[2048,2048]{1,0:T(8,128)(2,1)} custom-call(bf16[128,2048]{1,0:T(8,128)(2,1)} %refs_0_.3), custom_call_target="tpu_custom_call" | custom-call | bytes 33554432 | tf_op jit(solution)/shard_map/pallas_call | solution.py:353
  358.0 10.8 %multiply_convert_fusion.4 = (bf16[256,2048]{1,0:T(8,128)(2,1)}, f32[256,2048]{1,0:T(8,128)}, f32[256,2048]{1,0:T(8,128)}) fusion(bf16[2048,2048]{1,0:T(8,128)(2,1)} %shard_map.265, bf16[128,2048]{1,0:T(8,128)(2,1)} %collective-permute-done.1, bf16[128,2048]{1,0:T(8,128)(2,1)} %add_convert_fusion.36), kind=kOutput, calls=%fused_computation.35 | convolution fusion | flops 2183659520 | bytes 14680064 | tf_op jit(solution)/shard_map/dot_general | solution.py:75
  368.8 7.3 convolution_convert_fusion.11
  380.4 10.1 %collective-permute-done.2 = bf16[128,2048]{1,0:T(8,128)(2,1)} collective-permute-done((bf16[128,2048]{1,0:T(8,128)(2,1)}, bf16[128,2048]{1,0:T(8,128)(2,1)}, u32[]{:S(2)}, u32[]{:S(2)}) %collective-permute-start.2) | collective-permute-done | bytes 524320 | tf_op jit(solution)/shard_map/ppermute | solution.py:634
  390.6 7.9 fusion.40
  405.4 6.7 collective-permute-done.3
  437.8 6.6 collective-permute-done.5
  456.6 4.4 collective-permute-done.8
  466.6 6.1 fusion.94
  478.4 10.7 %collective-permute-done.11 = bf16[128,2048]{1,0:T(8,128)(2,1)S(1)} collective-permute-done((bf16[128,2048]{1,0:T(8,128)(2,1)S(1)}, bf16[128,2048]{1,0:T(8,128)(2,1)S(1)}, u32[]{:S(2)}, u32[]{:S(2)}) %collective-permute-start.11) | collective-permute-done | bytes 524320 | tf_op jit(solution)/shard_map/ppermute | solution.py:109
  507.2 5.2 collective-permute-done.12
  514.9 4.4 convolution_convert_fusion.5
  540.8 44.3 %shard_map.270 = bf16[2,8,128,512]{3,2,1,0:T(8,128)(2,1)} custom-call(bf16[2,8,128,512]{3,2,1,0:T(8,128)(2,1)} %multiply_convert_fusion.in_ref), custom_call_target="tpu_custom_call" | custom-call | tf_op jit(solution)/shard_map/pallas_call | solution.py:502
  596.6 11.9 %collective-permute-done.23 = bf16[128,2048]{1,0:T(8,128)(2,1)S(1)} collective-permute-done((bf16[128,2048]{1,0:T(8,128)(2,1)S(1)}, bf16[128,2048]{1,0:T(8,128)(2,1)S(1)}, u32[]{:S(2)}, u32[]{:S(2)}) %collective-permute-start.23) | collective-permute-done | bytes 524320 | tf_op jit(solution)/shard_map/ppermute | solution.py:109
  612.5 7.1 fusion.98
  619.6 3.8 collective-permute-done.25
  630.3 4.4 convolution_convert_fusion.1
  642.1 8.8 %collective-permute-done.48 = bf16[128,2048]{1,0:T(8,128)(2,1)S(1)} collective-permute-done((bf16[128,2048]{1,0:T(8,128)(2,1)S(1)}, bf16[128,2048]{1,0:T(8,128)(2,1)S(1)}, u32[]{:S(2)}, u32[]{:S(2)}) %collective-permute-start.48) | collective-permute-done | bytes 524320 | tf_op jit(solution)/shard_map/ppermute | solution.py:109
  658.1 4.2 collective-permute-done.26
  668.8 4.3 collective-permute-done.49
  685.1 6.3 convolution_add_fusion.1
  711.4 14.1 %collective-permute-done.53 = bf16[128,2048]{1,0:T(8,128)(2,1)S(1)} collective-permute-done((bf16[128,2048]{1,0:T(8,128)(2,1)S(1)}, bf16[128,2048]{1,0:T(8,128)(2,1)S(1)}, u32[]{:S(2)}, u32[]{:S(2)}) %collective-permute-start.53) | collective-permute-done | bytes 524320 | tf_op jit(solution)/shard_map/ppermute | solution.py:109
  744.4 10.1 %collective-permute-done.37 = bf16[128,3072]{1,0:T(8,128)(2,1)S(1)} collective-permute-done((bf16[128,3072]{1,0:T(8,128)(2,1)S(1)}, bf16[128,3072]{1,0:T(8,128)(2,1)S(1)}, u32[]{:S(2)}, u32[]{:S(2)}) %collective-permute-start.37) | collective-permute-done | bytes 786464 | tf_op jit(solution)/shard_map/ppermute | solution.py:109
  761.7 18.7 %shard_map.271 = f32[32,8,128]{2,1,0:T(8,128)} custom-call(f32[16,8,128]{2,1,0:T(8,128)} %concatenate.84.in_ref), custom_call_target="tpu_custom_call" | custom-call | tf_op jit(solution)/shard_map/pallas_call | solution.py:586
  783.1 4.4 add_convert_fusion.5
  799.3 13.2 %collective-permute-done.43 = bf16[128,3072]{1,0:T(8,128)(2,1)} collective-permute-done((bf16[128,3072]{1,0:T(8,128)(2,1)}, bf16[128,3072]{1,0:T(8,128)(2,1)}, u32[]{:S(2)}, u32[]{:S(2)}) %collective-permute-start.43) | collective-permute-done | bytes 786464 | tf_op jit(solution)/shard_map/ppermute | solution.py:109
  (453 shorter events, 264.9 us)
Async XLA Ops:
  7.2 239.1 %all-reduce.4.cloned.1.call-start = ((), (), s32[]{:S(2)}) async-start(), calls=%async_computation | async-start | bytes 4194304 | tf_op jit(solution)/shard_map/psum | solution.py:783
  107.2 261.6 %all-gather.2.cloned.1.call-start = ((), (), s32[]{:S(2)}) async-start(), calls=%async_computation.1 | async-start | bytes 8912896 | tf_op jit(solution)/shard_map/all_gather | solution.py:735
  293.9 64.1 %collective-permute-start.1 = (bf16[128,2048]{1,0:T(8,128)(2,1)}, bf16[128,2048]{1,0:T(8,128)(2,1)}, u32[]{:S(2)}, u32[]{:S(2)}) collective-permute-start(bf16[128,2048]{1,0:T(8,128)(2,1)} %add_convert_fusion.36), channel_id=1, source_target_pairs={{0,1},{1,0},{2,3},{3,2},{4,5},{5,4},{6,7},{7,6},{8,9},{9,8},{10,11... | collective-permute-start | bytes 1572872 | tf_op jit(solution)/shard_map/ppermute | solution.py:634
  454.5 21.2 %collective-permute-start.19 = (bf16[128,2048]{1,0:T(8,128)(2,1)S(1)}, bf16[128,2048]{1,0:T(8,128)(2,1)S(1)}, u32[]{:S(2)}, u32[]{:S(2)}) collective-permute-start(bf16[128,2048]{1,0:T(8,128)(2,1)S(1)} %get-tuple-element.103), channel_id=1, source_target_pairs={{0,4},{2,6},{8,0},{10,2},{16,8},{18,10},{24,16},{26,18},{28,24},{3... | collective-permute-start | bytes 1572872 | tf_op jit(solution)/shard_map/ppermute | solution.py:109
  455.1 20.6 %collective-permute-start.15 = (bf16[128,2048]{1,0:T(8,128)(2,1)S(1)}, bf16[128,2048]{1,0:T(8,128)(2,1)S(1)}, u32[]{:S(2)}, u32[]{:S(2)}) collective-permute-start(bf16[128,2048]{1,0:T(8,128)(2,1)S(1)} %get-tuple-element.104), channel_id=1, source_target_pairs={{0,8},{2,10},{8,16},{10,18},{16,24},{18,26},{24,28},{26,30},{28,20... | collective-permute-start | bytes 1572872 | tf_op jit(solution)/shard_map/ppermute | solution.py:109
  466.0 23.1 %collective-permute-start.9 = (bf16[128,2048]{1,0:T(8,128)(2,1)S(1)}, bf16[128,2048]{1,0:T(8,128)(2,1)S(1)}, u32[]{:S(2)}, u32[]{:S(2)}) collective-permute-start(bf16[128,2048]{1,0:T(8,128)(2,1)S(1)} %get-tuple-element.108), channel_id=1, source_target_pairs={{0,4},{2,6},{8,0},{10,2},{16,8},{18,10},{24,16},{26,18},{28,24},{3... | collective-permute-start | bytes 1572872 | tf_op jit(solution)/shard_map/ppermute | solution.py:109
  472.8 20.6 %collective-permute-start.7 = (bf16[128,2048]{1,0:T(8,128)(2,1)S(1)}, bf16[128,2048]{1,0:T(8,128)(2,1)S(1)}, u32[]{:S(2)}, u32[]{:S(2)}) collective-permute-start(bf16[128,2048]{1,0:T(8,128)(2,1)S(1)} %slice.821), channel_id=1, source_target_pairs={{0,1},{1,0},{2,3},{3,2},{4,5},{5,4},{6,7},{7,6},{8,9},{9,8},{10,11... | collective-permute-start | bytes 1572872 | tf_op jit(solution)/shard_map/ppermute | solution.py:634
  476.3 21.2 %collective-permute-start.20 = (bf16[128,2048]{1,0:T(8,128)(2,1)S(1)}, bf16[128,2048]{1,0:T(8,128)(2,1)S(1)}, u32[]{:S(2)}, u32[]{:S(2)}) collective-permute-start(bf16[128,2048]{1,0:T(8,128)(2,1)S(1)} %get-tuple-element.101), channel_id=1, source_target_pairs={{0,4},{2,6},{8,0},{10,2},{16,8},{18,10},{24,16},{26,18},{28,24},{3... | collective-permute-start | bytes 1572872 | tf_op jit(solution)/shard_map/ppermute | solution.py:109
  477.0 23.3 %collective-permute-start.17 = (bf16[128,2048]{1,0:T(8,128)(2,1)S(1)}, bf16[128,2048]{1,0:T(8,128)(2,1)S(1)}, u32[]{:S(2)}, u32[]{:S(2)}) collective-permute-start(bf16[128,2048]{1,0:T(8,128)(2,1)S(1)} %get-tuple-element.102), channel_id=1, source_target_pairs={{0,8},{2,10},{8,16},{10,18},{16,24},{18,26},{24,28},{26,30},{28,20... | collective-permute-start | bytes 1572872 | tf_op jit(solution)/shard_map/ppermute | solution.py:109
  491.3 21.1 %collective-permute-start.13 = (bf16[128,2048]{1,0:T(8,128)(2,1)S(1)}, bf16[128,2048]{1,0:T(8,128)(2,1)}, u32[]{:S(2)}, u32[]{:S(2)}) collective-permute-start(bf16[128,2048]{1,0:T(8,128)(2,1)S(1)} %get-tuple-element.106), channel_id=1, source_target_pairs={{0,4},{2,6},{8,0},{10,2},{16,8},{18,10},{24,16},{26,18},{28,24},{3... | collective-permute-start | bytes 1572872 | tf_op jit(solution)/shard_map/ppermute | solution.py:109
  501.9 32.9 %collective-permute-start.18 = (bf16[128,2048]{1,0:T(8,128)(2,1)}, bf16[128,2048]{1,0:T(8,128)(2,1)}, u32[]{:S(2)}, u32[]{:S(2)}) collective-permute-start(bf16[128,2048]{1,0:T(8,128)(2,1)} %get-tuple-element.100), channel_id=1, source_target_pairs={{0,8},{2,10},{8,16},{10,18},{16,24},{18,26},{24,28},{26,30},{28,20... | collective-permute-start | bytes 1572872 | tf_op jit(solution)/shard_map/ppermute | solution.py:109
  502.8 124.1 %collective-permute-start.21 = (bf16[128,2048]{1,0:T(8,128)(2,1)}, bf16[128,2048]{1,0:T(8,128)(2,1)}, u32[]{:S(2)}, u32[]{:S(2)}) collective-permute-start(bf16[128,2048]{1,0:T(8,128)(2,1)} %get-tuple-element.99), channel_id=1, source_target_pairs={{0,4},{2,6},{8,0},{10,2},{16,8},{18,10},{24,16},{26,18},{28,24},{3... | collective-permute-start | bytes 1572872 | tf_op jit(solution)/shard_map/ppermute | solution.py:109
  528.0 64.2 %collective-permute-start.22 = (bf16[1024,2048]{1,0:T(8,128)(2,1)}, bf16[1024,2048]{1,0:T(8,128)(2,1)}, u32[]{:S(2)}, u32[]{:S(2)}) collective-permute-start(bf16[1024,2048]{1,0:T(8,128)(2,1)} %convolution_convert_fusion.3), channel_id=1, source_target_pairs={{0,2},{2,0},{4,6},{6,4},{8,10},{10,8},{12,14},{14,12},{16,18},{18,... | collective-permute-start | bytes 12582920 | tf_op jit(solution)/shard_map/ppermute | solution.py:112
  588.4 46.4 %collective-permute-start.44 = (bf16[1024,2048]{1,0:T(8,128)(2,1)}, bf16[1024,2048]{1,0:T(8,128)(2,1)}, u32[]{:S(2)}, u32[]{:S(2)}) collective-permute-start(bf16[1024,2048]{1,0:T(8,128)(2,1)} %convolution_convert_fusion.2), channel_id=1, source_target_pairs={{0,2},{2,0},{4,6},{6,4},{8,10},{10,8},{12,14},{14,12},{16,18},{18,... | collective-permute-start | bytes 12582920 | tf_op jit(solution)/shard_map/ppermute | solution.py:112
  634.8 73.2 %collective-permute-start.27 = (bf16[1024,3072]{1,0:T(8,128)(2,1)}, bf16[1024,3072]{1,0:T(8,128)(2,1)}, u32[]{:S(2)}, u32[]{:S(2)}) collective-permute-start(bf16[1024,3072]{1,0:T(8,128)(2,1)} %convolution_convert_fusion.1), channel_id=1, source_target_pairs={{0,2},{2,0},{4,6},{6,4},{8,10},{10,8},{12,14},{14,12},{16,18},{18,... | collective-permute-start | bytes 18874376 | tf_op jit(solution)/shard_map/ppermute | solution.py:112
  640.1 22.2 %collective-permute-start.26 = (bf16[128,2048]{1,0:T(8,128)(2,1)}, bf16[128,2048]{1,0:T(8,128)(2,1)}, u32[]{:S(2)}, u32[]{:S(2)}) collective-permute-start(bf16[128,2048]{1,0:T(8,128)(2,1)} %get-tuple-element.96), channel_id=1, source_target_pairs={{0,4},{2,6},{8,0},{10,2},{16,8},{18,10},{24,16},{26,18},{28,24},{3... | collective-permute-start | bytes 1572872 | tf_op jit(solution)/shard_map/ppermute | solution.py:109
  655.2 17.9 %collective-permute-start.49 = (bf16[128,2048]{1,0:T(8,128)(2,1)}, bf16[128,2048]{1,0:T(8,128)(2,1)}, u32[]{:S(2)}, u32[]{:S(2)}) collective-permute-start(bf16[128,2048]{1,0:T(8,128)(2,1)} %get-tuple-element.94), channel_id=1, source_target_pairs={{0,4},{2,6},{8,0},{10,2},{16,8},{18,10},{24,16},{26,18},{28,24},{3... | collective-permute-start | bytes 1572872 | tf_op jit(solution)/shard_map/ppermute | solution.py:109
  665.5 18.7 %collective-permute-start.29 = (bf16[1024,1024]{1,0:T(8,128)(2,1)S(1)}, bf16[1024,1024]{1,0:T(8,128)(2,1)S(1)}, u32[]{:S(2)}, u32[]{:S(2)}) collective-permute-start(bf16[1024,1024]{1,0:T(8,128)(2,1)S(1)} %convolution_convert_fusion.13), channel_id=1, source_target_pairs={{0,2},{2,0},{4,6},{6,4},{8,10},{10,8},{12,14},{14,12},{16,18},{18,... | collective-permute-start | bytes 6291464 | tf_op jit(solution)/shard_map/ppermute | solution.py:112
  675.1 20.7 %collective-permute-start.46 = (bf16[128,2048]{1,0:T(8,128)(2,1)S(1)}, bf16[128,2048]{1,0:T(8,128)(2,1)S(1)}, u32[]{:S(2)}, u32[]{:S(2)}) collective-permute-start(bf16[128,2048]{1,0:T(8,128)(2,1)S(1)} %get-tuple-element.91), channel_id=1, source_target_pairs={{0,8},{2,10},{8,16},{10,18},{16,24},{18,26},{24,28},{26,30},{28,20... | collective-permute-start | bytes 1572872 | tf_op jit(solution)/shard_map/ppermute | solution.py:109
  676.4 20.2 %collective-permute-start.50 = (bf16[128,2048]{1,0:T(8,128)(2,1)S(1)}, bf16[128,2048]{1,0:T(8,128)(2,1)S(1)}, u32[]{:S(2)}, u32[]{:S(2)}) collective-permute-start(bf16[128,2048]{1,0:T(8,128)(2,1)S(1)} %get-tuple-element.92), channel_id=1, source_target_pairs={{0,4},{2,6},{8,0},{10,2},{16,8},{18,10},{24,16},{26,18},{28,24},{3... | collective-permute-start | bytes 1572872 | tf_op jit(solution)/shard_map/ppermute | solution.py:109
  679.5 31.1 %collective-permute-start.54 = (bf16[128,2048]{1,0:T(8,128)(2,1)S(1)}, bf16[128,2048]{1,0:T(8,128)(2,1)S(1)}, u32[]{:S(2)}, u32[]{:S(2)}) collective-permute-start(bf16[128,2048]{1,0:T(8,128)(2,1)S(1)} %get-tuple-element.88), channel_id=1, source_target_pairs={{0,4},{2,6},{8,0},{10,2},{16,8},{18,10},{24,16},{26,18},{28,24},{3... | collective-permute-start | bytes 1572872 | tf_op jit(solution)/shard_map/ppermute | solution.py:109
  699.3 92.3 %collective-permute-start.47 = (bf16[128,2048]{1,0:T(8,128)(2,1)}, bf16[128,2048]{1,0:T(8,128)(2,1)}, u32[]{:S(2)}, u32[]{:S(2)}) collective-permute-start(bf16[128,2048]{1,0:T(8,128)(2,1)} %get-tuple-element.89), channel_id=1, source_target_pairs={{0,8},{2,10},{8,16},{10,18},{16,24},{18,26},{24,28},{26,30},{28,20... | collective-permute-start | bytes 1572872 | tf_op jit(solution)/shard_map/ppermute | solution.py:109
  702.8 22.7 %collective-permute-start.53 = (bf16[128,2048]{1,0:T(8,128)(2,1)S(1)}, bf16[128,2048]{1,0:T(8,128)(2,1)S(1)}, u32[]{:S(2)}, u32[]{:S(2)}) collective-permute-start(bf16[128,2048]{1,0:T(8,128)(2,1)S(1)} %get-tuple-element.87), channel_id=1, source_target_pairs={{0,8},{2,10},{8,16},{10,18},{16,24},{18,26},{24,28},{26,30},{28,20... | collective-permute-start | bytes 1572872 | tf_op jit(solution)/shard_map/ppermute | solution.py:109
  707.1 22.5 %collective-permute-start.32 = (bf16[128,1024]{1,0:T(8,128)(2,1)S(1)}, bf16[128,1024]{1,0:T(8,128)(2,1)S(1)}, u32[]{:S(2)}, u32[]{:S(2)}) collective-permute-start(bf16[128,1024]{1,0:T(8,128)(2,1)S(1)} %get-tuple-element.114), channel_id=1, source_target_pairs={{0,8},{2,10},{8,16},{10,18},{16,24},{18,26},{24,28},{26,30},{28,20... | collective-permute-start | bytes 786440 | tf_op jit(solution)/shard_map/ppermute | solution.py:109
  708.0 21.7 %collective-permute-start.35 = (bf16[128,1024]{1,0:T(8,128)(2,1)S(1)}, bf16[128,1024]{1,0:T(8,128)(2,1)S(1)}, u32[]{:S(2)}, u32[]{:S(2)}) collective-permute-start(bf16[128,1024]{1,0:T(8,128)(2,1)S(1)} %get-tuple-element.115), channel_id=1, source_target_pairs={{0,4},{2,6},{8,0},{10,2},{16,8},{18,10},{24,16},{26,18},{28,24},{3... | collective-permute-start | bytes 786440 | tf_op jit(solution)/shard_map/ppermute | solution.py:109
  710.6 21.4 %collective-permute-start.40 = (bf16[128,3072]{1,0:T(8,128)(2,1)S(1)}, bf16[128,3072]{1,0:T(8,128)(2,1)S(1)}, u32[]{:S(2)}, u32[]{:S(2)}) collective-permute-start(bf16[128,3072]{1,0:T(8,128)(2,1)S(1)} %add_convert_fusion.4), channel_id=1, source_target_pairs={{0,4},{2,6},{8,0},{10,2},{16,8},{18,10},{24,16},{26,18},{28,24},{3... | collective-permute-start | bytes 2359304 | tf_op jit(solution)/shard_map/ppermute | solution.py:109
  734.2 20.3 %collective-permute-start.37 = (bf16[128,3072]{1,0:T(8,128)(2,1)S(1)}, bf16[128,3072]{1,0:T(8,128)(2,1)S(1)}, u32[]{:S(2)}, u32[]{:S(2)}) collective-permute-start(bf16[128,3072]{1,0:T(8,128)(2,1)S(1)} %get-tuple-element.85), channel_id=1, source_target_pairs={{0,8},{2,10},{8,16},{10,18},{16,24},{18,26},{24,28},{26,30},{28,20... | collective-permute-start | bytes 2359304 | tf_op jit(solution)/shard_map/ppermute | solution.py:109
  735.5 19.0 %collective-permute-start.41 = (bf16[128,3072]{1,0:T(8,128)(2,1)S(1)}, bf16[128,3072]{1,0:T(8,128)(2,1)S(1)}, u32[]{:S(2)}, u32[]{:S(2)}) collective-permute-start(bf16[128,3072]{1,0:T(8,128)(2,1)S(1)} %get-tuple-element.86), channel_id=1, source_target_pairs={{0,4},{2,6},{8,0},{10,2},{16,8},{18,10},{24,16},{26,18},{28,24},{3... | collective-permute-start | bytes 2359304 | tf_op jit(solution)/shard_map/ppermute | solution.py:109
  757.8 25.3 %collective-permute-start.38 = (bf16[128,3072]{1,0:T(8,128)(2,1)}, bf16[128,3072]{1,0:T(8,128)(2,1)}, u32[]{:S(2)}, u32[]{:S(2)}) collective-permute-start(bf16[128,3072]{1,0:T(8,128)(2,1)} %get-tuple-element.83), channel_id=1, source_target_pairs={{0,8},{2,10},{8,16},{10,18},{16,24},{18,26},{24,28},{26,30},{28,20... | collective-permute-start | bytes 2359304 | tf_op jit(solution)/shard_map/ppermute | solution.py:109
  758.7 24.4 %collective-permute-start.42 = (bf16[128,3072]{1,0:T(8,128)(2,1)}, bf16[128,3072]{1,0:T(8,128)(2,1)}, u32[]{:S(2)}, u32[]{:S(2)}) collective-permute-start(bf16[128,3072]{1,0:T(8,128)(2,1)} %get-tuple-element.84), channel_id=1, source_target_pairs={{0,4},{2,6},{8,0},{10,2},{16,8},{18,10},{24,16},{26,18},{28,24},{3... | collective-permute-start | bytes 2359304 | tf_op jit(solution)/shard_map/ppermute | solution.py:109
  787.5 25.0 %collective-permute-start.43 = (bf16[128,3072]{1,0:T(8,128)(2,1)}, bf16[128,3072]{1,0:T(8,128)(2,1)}, u32[]{:S(2)}, u32[]{:S(2)}) collective-permute-start(bf16[128,3072]{1,0:T(8,128)(2,1)} %get-tuple-element.82), channel_id=1, source_target_pairs={{0,4},{2,6},{8,0},{10,2},{16,8},{18,10},{24,16},{26,18},{28,24},{3... | collective-permute-start | bytes 2359304 | tf_op jit(solution)/shard_map/ppermute | solution.py:109
  788.4 24.1 %collective-permute-start.39 = (bf16[128,3072]{1,0:T(8,128)(2,1)}, bf16[128,3072]{1,0:T(8,128)(2,1)}, u32[]{:S(2)}, u32[]{:S(2)}) collective-permute-start(bf16[128,3072]{1,0:T(8,128)(2,1)} %get-tuple-element.81), channel_id=1, source_target_pairs={{0,8},{2,10},{8,16},{10,18},{16,24},{18,26},{24,28},{26,30},{28,20... | collective-permute-start | bytes 2359304 | tf_op jit(solution)/shard_map/ppermute | solution.py:109
  (123 other events, 1663.0 us)
Sparse Core Ops, SparseCore 0:
  107.3 109.9 all-reduce.3
  246.5 80.9 all-gather.1

commit v5 on v4

--- a/solution.py
+++ b/solution.py
@@ -916,9 +916,9 @@
         .astype(jnp.bfloat16)
     )
     grad_vlow = grad_values.reshape(seg_len, heads_local * DV).astype(jnp.bfloat16)
-    grad_key_value = jnp.concatenate([grad_keys, grad_vlow], axis=1)
-    sum_wkv = weight_grad(a_order, grad_key_value, True)
-    grad_keys = tie(grad_keys, sum_wkv.arrived)
+    sum_wv = weight_grad(a_order, grad_vlow, True)
+    sum_wk = weight_grad(a_order, grad_keys, False)
+    grad_keys = tie(grad_keys, (sum_wv.arrived, sum_wk.arrived))
     grad_a = scatter_rows(
         contract_last(grad_queries, wq_full)
         + contract_last(grad_gate, wg_full)
@@ -937,7 +937,6 @@
     key_width = w_key.shape[1]
     sum_wg.run(2)
     sum_wg.moving = [tie(x, totals) for x in sum_wg.moving]
-    grad_wkv = sum_wkv.result()
 
     return (
         block_out,
@@ -946,8 +945,8 @@
         totals[0, :block],
         totals[1, :block],
         sum_wq.result(),
-        grad_wkv[:, :key_width],
-        grad_wkv[:, key_width:],
+        sum_wk.result(),
+        sum_wv.result(),
         sum_wg.result(),
         sum_wo.result(),
         totals[2, :block],

time: 835 us -> 862 us (1.032)
  waiting for transfers between devices: 156 us -> 173 us
  starting transfers between devices: 54.1 us -> 62.9 us
    ppermute x42 -> x49, waiting for transfers between devices: 122 us -> 137 us  [shift(): return lax.ppermute(rows, 'dp', pairs)]
    pallas_call x1, Pallas kernels: 18.7 us -> 9.59 us  [exchange_blocks(): pl.pallas_call(kernel, out_shape=jax.ShapeDtypeStruct((total, *blocks.sha...]
    ppermute x42 -> x49, starting transfers between devices: 45.6 us -> 54.1 us  [shift(): return lax.ppermute(rows, 'dp', pairs)]
    convert_element_type x14 -> x17, other arithmetic: 27 us -> 29 us  [step(): moved = (moved.astype(jnp.float32) + self.term(k)).astype(jnp.bfloat16)]
    dot_general x12 -> x14, matrix products: 28.9 us -> 28.3 us  [contract_first(): lax.dot_general(first_op, second_op, (((0,), (0,)), ((), ())), preferred_...]
  transfers between devices with their start and end apart: 57 -> 65, of which waited for: 28 -> 29; matrix products, arithmetic and copies ran while one was open for 23% -> 22% of each run, Pallas kernels for 33% -> 25%
where the time goes in v5:
time: 862 us; the launch traced here: 852 us
  Pallas kernels  339 us (39%)
  waiting for transfers between devices  173 us (20%)
  matrix products  121 us (14%)
  other arithmetic  105 us (12%)
  starting transfers between devices  62.9 us (7%)
  local copies, waits for them, and re-layouts  29.7 us (3%)
  between operations  21.7 us (3%)
    pallas_call x3, Pallas kernels, gather_ring(): pl.pallas_call(kernel, out_shape=out_shape, in_specs=in_specs, out_specs=...  275 us
    ppermute x49, waiting for transfers between devices, shift(): return lax.ppermute(rows, 'dp', pairs)  137 us
    ppermute x49, starting transfers between devices, shift(): return lax.ppermute(rows, 'dp', pairs)  54.1 us
    dot_general x9, matrix products, contract_last(): lax.dot_general(first_op, second_op, (((1,), (1,)), ((), ())), preferred_...  45 us
    pallas_call x1, Pallas kernels, ring_total(): pl.pallas_call(kernel, out_shape=jax.ShapeDtypeStruct(shape, low), in_spe...  44.5 us
    dot_general x7, matrix products, plain_dot(): return jnp.dot(first_op, second_op, preferred_element_type=jnp.float32)  38.6 us
    ppermute x7, waiting for transfers between devices, swap_mp(): return lax.ppermute(rows, 'mp', [(0, 1), (1, 0)])  31.9 us
    convert_element_type x17, other arithmetic, step(): moved = (moved.astype(jnp.float32) + self.term(k)).astype(jnp.bfloat16)  29 us
  transfers between devices with their start and end apart: 65, of which 29 were waited for; matrix products, arithmetic and copies ran while one was open for 22% of the time, Pallas kernels for 25%

profile of v5, /device:TPU:0, one launch (start us, length us, event | category | flops | bytes accessed | tf_op | source)
XLA Modules:
  0.0 852.0 jit_solution(13821091427678007460)
XLA Ops:
  18.4 75.1 %shard_map.263 = (bf16[2048,1024]{1,0:T(8,128)(2,1)}, bf16[2048,2048]{1,0:T(8,128)(2,1)}, f32[32,8,128]{2,1,0:T(8,128)}, bf16[2,128,2048]{2,1,0:T(8,128)(2,1)}) custom-call(bf16[128,1024]{1,0:T(8,128)(2,1)} %refs_0_.1, bf16[128,2048]{1,0:T(8,128)(2,1)} %refs_1_.2, f32[16,8,128]{2,1,0:T(8,128)} %concatenate.70.refs_2_, bf16[128,2048]{1,0:T(8,128)(2,1)} %refs_3_.1), custom_call_target="tpu_custom_call" | custom-call | bytes 50331648 | tf_op jit(solution)/shard_map/pallas_call | solution.py:353
  93.6 6.2 convolution_convert_fusion.10
  106.6 139.1 %shard_map.264 = (bf16[2048,1024]{1,0:T(8,128)(2,1)}, bf16[2048,2048]{1,0:T(8,128)(2,1)}, bf16[2048,2048]{1,0:T(8,128)(2,1)}) custom-call(bf16[128,1024]{1,0:T(8,128)(2,1)} %refs_0_.2, bf16[128,2048]{1,0:T(8,128)(2,1)} %refs_1_.3, bf16[128,2048]{1,0:T(8,128)(2,1)} %refs_2_.1), custom_call_target="tpu_custom_call" | custom-call | bytes 83886080 | tf_op jit(solution)/shard_map/pallas_call | solution.py:353
  245.7 5.7 fusion.92
  255.6 4.7 fusion.93
  275.2 12.1 %collective-permute-done = bf16[128,2048]{1,0:T(8,128)(2,1)S(1)} collective-permute-done((bf16[128,2048]{1,0:T(8,128)(2,1)S(1)}, bf16[128,2048]{1,0:T(8,128)(2,1)S(1)}, u32[]{:S(2)}, u32[]{:S(2)}) %collective-permute-start) | collective-permute-done | bytes 524320 | tf_op jit(solution)/shard_map/ppermute | solution.py:634
  296.7 60.5 %shard_map.265 = bf16[2048,2048]{1,0:T(8,128)(2,1)} custom-call(bf16[128,2048]{1,0:T(8,128)(2,1)} %refs_0_.3), custom_call_target="tpu_custom_call" | custom-call | bytes 33554432 | tf_op jit(solution)/shard_map/pallas_call | solution.py:353
  357.2 10.8 %multiply_convert_fusion.4 = (bf16[256,2048]{1,0:T(8,128)(2,1)}, f32[256,2048]{1,0:T(8,128)}, f32[256,2048]{1,0:T(8,128)}) fusion(bf16[2048,2048]{1,0:T(8,128)(2,1)} %shard_map.265, bf16[128,2048]{1,0:T(8,128)(2,1)} %collective-permute-done.1, bf16[128,2048]{1,0:T(8,128)(2,1)} %add_convert_fusion.36), kind=kOutput, calls=%fused_computation.35 | convolution fusion | flops 2183659520 | bytes 14680064 | tf_op jit(solution)/shard_map/dot_general | solution.py:75
  368.1 7.3 convolution_convert_fusion.11
  379.7 10.1 %collective-permute-done.2 = bf16[128,2048]{1,0:T(8,128)(2,1)} collective-permute-done((bf16[128,2048]{1,0:T(8,128)(2,1)}, bf16[128,2048]{1,0:T(8,128)(2,1)}, u32[]{:S(2)}, u32[]{:S(2)}) %collective-permute-start.2) | collective-permute-done | bytes 524320 | tf_op jit(solution)/shard_map/ppermute | solution.py:634
  389.8 8.1 fusion.40
  404.7 6.8 collective-permute-done.3
  437.3 6.1 collective-permute-done.5
  466.1 6.1 fusion.94
  478.0 10.6 %collective-permute-done.11 = bf16[128,2048]{1,0:T(8,128)(2,1)S(1)} collective-permute-done((bf16[128,2048]{1,0:T(8,128)(2,1)S(1)}, bf16[128,2048]{1,0:T(8,128)(2,1)S(1)}, u32[]{:S(2)}, u32[]{:S(2)}) %collective-permute-start.11) | collective-permute-done | bytes 524320 | tf_op jit(solution)/shard_map/ppermute | solution.py:109
  506.6 5.2 collective-permute-done.12
  514.3 4.5 convolution_convert_fusion.5
  518.8 6.9 fusion.95
  547.1 44.5 %shard_map.270 = bf16[2,8,128,512]{3,2,1,0:T(8,128)(2,1)} custom-call(bf16[2,8,128,512]{3,2,1,0:T(8,128)(2,1)} %multiply_convert_fusion.in_ref), custom_call_target="tpu_custom_call" | custom-call | tf_op jit(solution)/shard_map/pallas_call | solution.py:502
  610.7 4.3 convert_add_fusion.1
  621.9 7.3 fusion.98
  636.5 7.2 collective-permute-done.23
  652.2 6.5 collective-permute-done.56
  663.4 6.6 collective-permute-done.24
  684.7 7.8 collective-permute-done.57
  697.4 6.4 collective-permute-done.26
  709.9 6.3 convolution_add_fusion.1
  730.5 16.3 %collective-permute-done.51 = bf16[128,2048]{1,0:T(8,128)(2,1)S(1)} collective-permute-done((bf16[128,2048]{1,0:T(8,128)(2,1)S(1)}, bf16[128,2048]{1,0:T(8,128)(2,1)S(1)}, u32[]{:S(2)}, u32[]{:S(2)}) %collective-permute-start.51) | collective-permute-done | bytes 524320 | tf_op jit(solution)/shard_map/ppermute | solution.py:109
  755.2 17.8 %collective-permute-done.61 = bf16[128,2048]{1,0:T(8,128)(2,1)S(1)} collective-permute-done((bf16[128,2048]{1,0:T(8,128)(2,1)S(1)}, bf16[128,2048]{1,0:T(8,128)(2,1)S(1)}, u32[]{:S(2)}, u32[]{:S(2)}) %collective-permute-start.61) | collective-permute-done | bytes 524320 | tf_op jit(solution)/shard_map/ppermute | solution.py:109
  780.4 5.1 collective-permute-done.39
  791.5 9.6 %shard_map.271 = f32[32,8,128]{2,1,0:T(8,128)} custom-call(f32[16,8,128]{2,1,0:T(8,128)} %concatenate.80.in_ref), custom_call_target="tpu_custom_call" | custom-call | tf_op jit(solution)/shard_map/pallas_call | solution.py:586
  816.0 7.7 collective-permute-done.35
  (495 shorter events, 291.0 us)
Async XLA Ops:
  7.2 238.5 %all-reduce.4.cloned.1.call-start = ((), (), s32[]{:S(2)}) async-start(), calls=%async_computation | async-start | bytes 4194304 | tf_op jit(solution)/shard_map/psum | solution.py:783
  106.5 261.5 %all-gather.2.cloned.1.call-start = ((), (), s32[]{:S(2)}) async-start(), calls=%async_computation.1 | async-start | bytes 8912896 | tf_op jit(solution)/shard_map/all_gather | solution.py:735
  291.7 65.5 %collective-permute-start.1 = (bf16[128,2048]{1,0:T(8,128)(2,1)}, bf16[128,2048]{1,0:T(8,128)(2,1)}, u32[]{:S(2)}, u32[]{:S(2)}) collective-permute-start(bf16[128,2048]{1,0:T(8,128)(2,1)} %add_convert_fusion.36), channel_id=1, source_target_pairs={{0,1},{1,0},{2,3},{3,2},{4,5},{5,4},{6,7},{7,6},{8,9},{9,8},{10,11... | collective-permute-start | bytes 1572872 | tf_op jit(solution)/shard_map/ppermute | solution.py:634
  465.5 23.1 %collective-permute-start.9 = (bf16[128,2048]{1,0:T(8,128)(2,1)S(1)}, bf16[128,2048]{1,0:T(8,128)(2,1)S(1)}, u32[]{:S(2)}, u32[]{:S(2)}) collective-permute-start(bf16[128,2048]{1,0:T(8,128)(2,1)S(1)} %get-tuple-element.108), channel_id=1, source_target_pairs={{0,4},{2,6},{8,0},{10,2},{16,8},{18,10},{24,16},{26,18},{28,24},{3... | collective-permute-start | bytes 1572872 | tf_op jit(solution)/shard_map/ppermute | solution.py:109
  476.5 23.3 %collective-permute-start.17 = (bf16[128,2048]{1,0:T(8,128)(2,1)S(1)}, bf16[128,2048]{1,0:T(8,128)(2,1)S(1)}, u32[]{:S(2)}, u32[]{:S(2)}) collective-permute-start(bf16[128,2048]{1,0:T(8,128)(2,1)S(1)} %get-tuple-element.102), channel_id=1, source_target_pairs={{0,8},{2,10},{8,16},{10,18},{16,24},{18,26},{24,28},{26,30},{28,20... | collective-permute-start | bytes 1572872 | tf_op jit(solution)/shard_map/ppermute | solution.py:109
  501.4 38.5 %collective-permute-start.18 = (bf16[128,2048]{1,0:T(8,128)(2,1)}, bf16[128,2048]{1,0:T(8,128)(2,1)}, u32[]{:S(2)}, u32[]{:S(2)}) collective-permute-start(bf16[128,2048]{1,0:T(8,128)(2,1)} %get-tuple-element.100), channel_id=1, source_target_pairs={{0,8},{2,10},{8,16},{10,18},{16,24},{18,26},{24,28},{26,30},{28,20... | collective-permute-start | bytes 1572872 | tf_op jit(solution)/shard_map/ppermute | solution.py:109
  594.4 34.8 %collective-permute-start.22 = (bf16[1024,2048]{1,0:T(8,128)(2,1)}, bf16[1024,2048]{1,0:T(8,128)(2,1)}, u32[]{:S(2)}, u32[]{:S(2)}) collective-permute-start(bf16[1024,2048]{1,0:T(8,128)(2,1)} %convolution_convert_fusion.3), channel_id=1, source_target_pairs={{0,2},{2,0},{4,6},{6,4},{8,10},{10,8},{12,14},{14,12},{16,18},{18,... | collective-permute-start | bytes 12582920 | tf_op jit(solution)/shard_map/ppermute | solution.py:112
  600.0 31.4 %collective-permute-start.27 = (bf16[1024,2048]{1,0:T(8,128)(2,1)}, bf16[1024,2048]{1,0:T(8,128)(2,1)}, u32[]{:S(2)}, u32[]{:S(2)}) collective-permute-start(bf16[1024,2048]{1,0:T(8,128)(2,1)} %convolution_convert_fusion.2), channel_id=1, source_target_pairs={{0,2},{2,0},{4,6},{6,4},{8,10},{10,8},{12,14},{14,12},{16,18},{18,... | collective-permute-start | bytes 12582920 | tf_op jit(solution)/shard_map/ppermute | solution.py:112
  604.5 29.1 %collective-permute-start.52 = (bf16[1024,2048]{1,0:T(8,128)(2,1)S(1)}, bf16[1024,2048]{1,0:T(8,128)(2,1)S(1)}, u32[]{:S(2)}, u32[]{:S(2)}) collective-permute-start(bf16[1024,2048]{1,0:T(8,128)(2,1)S(1)} %convolution_convert_fusion), channel_id=1, source_target_pairs={{0,2},{2,0},{4,6},{6,4},{8,10},{10,8},{12,14},{14,12},{16,18},{18,... | collective-permute-start | bytes 12582920 | tf_op jit(solution)/shard_map/ppermute | solution.py:112
  635.2 23.5 %collective-permute-start.56 = (bf16[128,2048]{1,0:T(8,128)(2,1)S(1)}, bf16[128,2048]{1,0:T(8,128)(2,1)S(1)}, u32[]{:S(2)}, u32[]{:S(2)}) collective-permute-start(bf16[128,2048]{1,0:T(8,128)(2,1)S(1)} %add_convert_fusion.5), channel_id=1, source_target_pairs={{0,4},{2,6},{8,0},{10,2},{16,8},{18,10},{24,16},{26,18},{28,24},{3... | collective-permute-start | bytes 1572872 | tf_op jit(solution)/shard_map/ppermute | solution.py:109
  646.5 23.4 %collective-permute-start.24 = (bf16[128,2048]{1,0:T(8,128)(2,1)S(1)}, bf16[128,2048]{1,0:T(8,128)(2,1)S(1)}, u32[]{:S(2)}, u32[]{:S(2)}) collective-permute-start(bf16[128,2048]{1,0:T(8,128)(2,1)S(1)} %get-tuple-element.97), channel_id=1, source_target_pairs={{0,4},{2,6},{8,0},{10,2},{16,8},{18,10},{24,16},{26,18},{28,24},{3... | collective-permute-start | bytes 1572872 | tf_op jit(solution)/shard_map/ppermute | solution.py:109
  650.1 29.4 %collective-permute-start.45 = (bf16[128,2048]{1,0:T(8,128)(2,1)}, bf16[128,2048]{1,0:T(8,128)(2,1)}, u32[]{:S(2)}, u32[]{:S(2)}) collective-permute-start(bf16[128,2048]{1,0:T(8,128)(2,1)} %get-tuple-element.93), channel_id=1, source_target_pairs={{0,8},{2,10},{8,16},{10,18},{16,24},{18,26},{24,28},{26,30},{28,20... | collective-permute-start | bytes 1572872 | tf_op jit(solution)/shard_map/ppermute | solution.py:109
  651.4 29.8 %collective-permute-start.49 = (bf16[128,2048]{1,0:T(8,128)(2,1)}, bf16[128,2048]{1,0:T(8,128)(2,1)}, u32[]{:S(2)}, u32[]{:S(2)}) collective-permute-start(bf16[128,2048]{1,0:T(8,128)(2,1)} %get-tuple-element.94), channel_id=1, source_target_pairs={{0,4},{2,6},{8,0},{10,2},{16,8},{18,10},{24,16},{26,18},{28,24},{3... | collective-permute-start | bytes 1572872 | tf_op jit(solution)/shard_map/ppermute | solution.py:109
  661.3 22.2 %collective-permute-start.53 = (bf16[128,2048]{1,0:T(8,128)(2,1)}, bf16[128,2048]{1,0:T(8,128)(2,1)}, u32[]{:S(2)}, u32[]{:S(2)}) collective-permute-start(bf16[128,2048]{1,0:T(8,128)(2,1)} %get-tuple-element.87), channel_id=1, source_target_pairs={{0,8},{2,10},{8,16},{10,18},{16,24},{18,26},{24,28},{26,30},{28,20... | collective-permute-start | bytes 1572872 | tf_op jit(solution)/shard_map/ppermute | solution.py:109
  662.6 29.9 %collective-permute-start.57 = (bf16[128,2048]{1,0:T(8,128)(2,1)}, bf16[128,2048]{1,0:T(8,128)(2,1)}, u32[]{:S(2)}, u32[]{:S(2)}) collective-permute-start(bf16[128,2048]{1,0:T(8,128)(2,1)} %get-tuple-element.88), channel_id=1, source_target_pairs={{0,4},{2,6},{8,0},{10,2},{16,8},{18,10},{24,16},{26,18},{28,24},{3... | collective-permute-start | bytes 1572872 | tf_op jit(solution)/shard_map/ppermute | solution.py:109
  672.7 31.1 %collective-permute-start.26 = (bf16[128,2048]{1,0:T(8,128)(2,1)}, bf16[128,2048]{1,0:T(8,128)(2,1)}, u32[]{:S(2)}, u32[]{:S(2)}) collective-permute-start(bf16[128,2048]{1,0:T(8,128)(2,1)} %get-tuple-element.96), channel_id=1, source_target_pairs={{0,4},{2,6},{8,0},{10,2},{16,8},{18,10},{24,16},{26,18},{28,24},{3... | collective-permute-start | bytes 1572872 | tf_op jit(solution)/shard_map/ppermute | solution.py:109
  681.3 70.0 %collective-permute-start.28 = (bf16[1024,1024]{1,0:T(8,128)(2,1)S(1)}, bf16[1024,1024]{1,0:T(8,128)(2,1)S(1)}, u32[]{:S(2)}, u32[]{:S(2)}) collective-permute-start(bf16[1024,1024]{1,0:T(8,128)(2,1)S(1)} %convolution_convert_fusion.16), channel_id=1, source_target_pairs={{0,2},{2,0},{4,6},{6,4},{8,10},{10,8},{12,14},{14,12},{16,18},{18,... | collective-permute-start | bytes 6291464 | tf_op jit(solution)/shard_map/ppermute | solution.py:112
  683.5 34.3 %collective-permute-start.46 = (bf16[128,2048]{1,0:T(8,128)(2,1)S(1)}, bf16[128,2048]{1,0:T(8,128)(2,1)S(1)}, u32[]{:S(2)}, u32[]{:S(2)}) collective-permute-start(bf16[128,2048]{1,0:T(8,128)(2,1)S(1)} %get-tuple-element.91), channel_id=1, source_target_pairs={{0,8},{2,10},{8,16},{10,18},{16,24},{18,26},{24,28},{26,30},{28,20... | collective-permute-start | bytes 1572872 | tf_op jit(solution)/shard_map/ppermute | solution.py:109
  692.5 26.3 %collective-permute-start.50 = (bf16[128,2048]{1,0:T(8,128)(2,1)S(1)}, bf16[128,2048]{1,0:T(8,128)(2,1)}, u32[]{:S(2)}, u32[]{:S(2)}) collective-permute-start(bf16[128,2048]{1,0:T(8,128)(2,1)S(1)} %get-tuple-element.92), channel_id=1, source_target_pairs={{0,4},{2,6},{8,0},{10,2},{16,8},{18,10},{24,16},{26,18},{28,24},{3... | collective-permute-start | bytes 1572872 | tf_op jit(solution)/shard_map/ppermute | solution.py:109
  696.3 24.4 %collective-permute-start.54 = (bf16[128,2048]{1,0:T(8,128)(2,1)}, bf16[128,2048]{1,0:T(8,128)(2,1)S(1)}, u32[]{:S(2)}, u32[]{:S(2)}) collective-permute-start(bf16[128,2048]{1,0:T(8,128)(2,1)} %get-tuple-element.85), channel_id=1, source_target_pairs={{0,8},{2,10},{8,16},{10,18},{16,24},{18,26},{24,28},{26,30},{28,20... | collective-permute-start | bytes 1572872 | tf_op jit(solution)/shard_map/ppermute | solution.py:109
  703.7 22.5 %collective-permute-start.58 = (bf16[128,2048]{1,0:T(8,128)(2,1)S(1)}, bf16[128,2048]{1,0:T(8,128)(2,1)}, u32[]{:S(2)}, u32[]{:S(2)}) collective-permute-start(bf16[128,2048]{1,0:T(8,128)(2,1)S(1)} %get-tuple-element.86), channel_id=1, source_target_pairs={{0,4},{2,6},{8,0},{10,2},{16,8},{18,10},{24,16},{26,18},{28,24},{3... | collective-permute-start | bytes 1572872 | tf_op jit(solution)/shard_map/ppermute | solution.py:109
  717.8 36.3 %collective-permute-start.62 = (bf16[128,2048]{1,0:T(8,128)(2,1)S(1)}, bf16[128,2048]{1,0:T(8,128)(2,1)S(1)}, u32[]{:S(2)}, u32[]{:S(2)}) collective-permute-start(bf16[128,2048]{1,0:T(8,128)(2,1)S(1)} %get-tuple-element.82), channel_id=1, source_target_pairs={{0,4},{2,6},{8,0},{10,2},{16,8},{18,10},{24,16},{26,18},{28,24},{3... | collective-permute-start | bytes 1572872 | tf_op jit(solution)/shard_map/ppermute | solution.py:109
  718.9 59.5 %collective-permute-start.30 = (bf16[1024,1024]{1,0:T(8,128)(2,1)S(1)}, bf16[1024,1024]{1,0:T(8,128)(2,1)S(1)}, u32[]{:S(2)}, u32[]{:S(2)}) collective-permute-start(bf16[1024,1024]{1,0:T(8,128)(2,1)S(1)} %convolution_convert_fusion.14), channel_id=1, source_target_pairs={{0,2},{2,0},{4,6},{6,4},{8,10},{10,8},{12,14},{14,12},{16,18},{18,... | collective-permute-start | bytes 6291464 | tf_op jit(solution)/shard_map/ppermute | solution.py:112
  720.8 26.1 %collective-permute-start.51 = (bf16[128,2048]{1,0:T(8,128)(2,1)S(1)}, bf16[128,2048]{1,0:T(8,128)(2,1)S(1)}, u32[]{:S(2)}, u32[]{:S(2)}) collective-permute-start(bf16[128,2048]{1,0:T(8,128)(2,1)S(1)} %get-tuple-element.90), channel_id=1, source_target_pairs={{0,4},{2,6},{8,0},{10,2},{16,8},{18,10},{24,16},{26,18},{28,24},{3... | collective-permute-start | bytes 1572872 | tf_op jit(solution)/shard_map/ppermute | solution.py:109
  746.8 57.6 %collective-permute-start.55 = (bf16[128,2048]{1,0:T(8,128)(2,1)}, bf16[128,2048]{1,0:T(8,128)(2,1)S(1)}, u32[]{:S(2)}, u32[]{:S(2)}) collective-permute-start(bf16[128,2048]{1,0:T(8,128)(2,1)} %get-tuple-element.83), channel_id=1, source_target_pairs={{0,8},{2,10},{8,16},{10,18},{16,24},{18,26},{24,28},{26,30},{28,20... | collective-permute-start | bytes 1572872 | tf_op jit(solution)/shard_map/ppermute | solution.py:109
  748.1 24.9 %collective-permute-start.61 = (bf16[128,2048]{1,0:T(8,128)(2,1)S(1)}, bf16[128,2048]{1,0:T(8,128)(2,1)S(1)}, u32[]{:S(2)}, u32[]{:S(2)}) collective-permute-start(bf16[128,2048]{1,0:T(8,128)(2,1)S(1)} %get-tuple-element.81), channel_id=1, source_target_pairs={{0,8},{2,10},{8,16},{10,18},{16,24},{18,26},{24,28},{26,30},{28,20... | collective-permute-start | bytes 1572872 | tf_op jit(solution)/shard_map/ppermute | solution.py:109
  752.8 25.7 %collective-permute-start.29 = (bf16[128,2048]{1,0:T(8,128)(2,1)S(1)}, bf16[128,2048]{1,0:T(8,128)(2,1)S(1)}, u32[]{:S(2)}, u32[]{:S(2)}) collective-permute-start(bf16[128,2048]{1,0:T(8,128)(2,1)S(1)} %slice.912), channel_id=1, source_target_pairs={{0,1},{1,0},{2,3},{3,2},{4,5},{5,4},{6,7},{7,6},{8,9},{9,8},{10,11... | collective-permute-start | bytes 1572872 | tf_op jit(solution)/shard_map/ppermute | solution.py:634
  779.1 26.1 %collective-permute-start.31 = (bf16[128,1024]{1,0:T(8,128)(2,1)S(1)}, bf16[128,1024]{1,0:T(8,128)(2,1)}, u32[]{:S(2)}, u32[]{:S(2)}) collective-permute-start(bf16[128,1024]{1,0:T(8,128)(2,1)S(1)} %add_convert_fusion.50), channel_id=1, source_target_pairs={{0,8},{2,10},{8,16},{10,18},{16,24},{18,26},{24,28},{26,30},{28,20... | collective-permute-start | bytes 786440 | tf_op jit(solution)/shard_map/ppermute | solution.py:109
  786.6 22.3 %collective-permute-start.40 = (bf16[128,1024]{1,0:T(8,128)(2,1)}, bf16[128,1024]{1,0:T(8,128)(2,1)}, u32[]{:S(2)}, u32[]{:S(2)}) collective-permute-start(bf16[128,1024]{1,0:T(8,128)(2,1)} %get-tuple-element.114), channel_id=1, source_target_pairs={{0,8},{2,10},{8,16},{10,18},{16,24},{18,26},{24,28},{26,30},{28,20... | collective-permute-start | bytes 786440 | tf_op jit(solution)/shard_map/ppermute | solution.py:109
  803.1 23.0 %collective-permute-start.59 = (bf16[128,2048]{1,0:T(8,128)(2,1)}, bf16[128,2048]{1,0:T(8,128)(2,1)S(1)}, u32[]{:S(2)}, u32[]{:S(2)}) collective-permute-start(bf16[128,2048]{1,0:T(8,128)(2,1)} %get-tuple-element.63), channel_id=1, source_target_pairs={{0,4},{2,6},{8,0},{10,2},{16,8},{18,10},{24,16},{26,18},{28,24},{3... | collective-permute-start | bytes 1572872 | tf_op jit(solution)/shard_map/ppermute | solution.py:109
  810.5 25.8 %collective-permute-start.44 = (bf16[128,1024]{1,0:T(8,128)(2,1)S(1)}, bf16[128,1024]{1,0:T(8,128)(2,1)S(1)}, u32[]{:S(2)}, u32[]{:S(2)}) collective-permute-start(bf16[128,1024]{1,0:T(8,128)(2,1)S(1)} %get-tuple-element.113), channel_id=1, source_target_pairs={{0,4},{2,6},{8,0},{10,2},{16,8},{18,10},{24,16},{26,18},{28,24},{3... | collective-permute-start | bytes 786440 | tf_op jit(solution)/shard_map/ppermute | solution.py:109
  811.7 24.6 %collective-permute-start.41 = (bf16[128,1024]{1,0:T(8,128)(2,1)S(1)}, bf16[128,1024]{1,0:T(8,128)(2,1)S(1)}, u32[]{:S(2)}, u32[]{:S(2)}) collective-permute-start(bf16[128,1024]{1,0:T(8,128)(2,1)S(1)} %get-tuple-element.112), channel_id=1, source_target_pairs={{0,8},{2,10},{8,16},{10,18},{16,24},{18,26},{24,28},{26,30},{28,20... | collective-permute-start | bytes 786440 | tf_op jit(solution)/shard_map/ppermute | solution.py:109
  (142 other events, 2077.0 us)
Sparse Core Ops, SparseCore 0:
  106.6 110.0 all-reduce.3
  245.8 82.4 all-gather.1
